TPU v7x, 32 devices: a whole 2x2x4 slice. The times are simulated.
32 devices in a mesh: frames: 2 (over y), az: 8 (over z, x), rg: 2 (over core).
Axes of the slice: x: 2, y: 2, z: 4, core: 2. Of those that a mesh axis runs over, the one named last changes fastest.
Arguments:
- raw: bfloat16 [2, 512, 8, 2048], P(None, ('frames', 'az'), None, 'rg'), parts along dimension 1, may hold values from -6 to 6
- stolt_weights: bfloat16 [4, 16, 256, 128], P(None, 'rg'), may hold values from -0.375 to 0.375
- band_start: int32 [4, 16], replicated, may hold values from 0 to 14, as said below
Outputs:
- image: bfloat16 [2, 512, 8, 2048], P(None, ('frames', 'az'), None, 'rg'), parts along dimension 1
There are 2 independent parts, one for each index of `frames`. A program takes and returns all parts, laid end to end along the dimension named above; an argument that names none is the same for every part. Nothing has to cross between parts.
Inputs may be any that keep to these rules, and one draw needn't show every extreme that they name: band_start[g, j] is (j) - 1 or (j), clipped to the range; for every block j from 1 to 14 some slab has (j) - 1 and some slab has (j).
All inputs are finite; a program needn't handle non-finite values.
Results may differ from a plain program's by a relative error of at most 0.001.
Values may be sent and summed in bfloat16 or wider, within the bound.
No kernel may reach another device: no remote copies, remote signals or barrier semaphores. Data moves between devices by JAX's collectives and lax.ppermute only.
A program may use at most 64 MiB of HBM per device.

v0:
```python
import math

import jax
import jax.numpy as jnp
from jax import lax
from jax.sharding import PartitionSpec as P

LINES_DEV = 256
SLABS = 4


def with_halo(cells, sides, width):
    for axis, dim in sides:
        count = lax.axis_size(axis)
        ends = count - 1
        head = lax.slice_in_dim(cells, 0, width, axis=dim)
        tail = lax.slice_in_dim(cells, cells.shape[dim] - width, cells.shape[dim], axis=dim)
        cells = jnp.concatenate(
            [
                lax.ppermute(tail, axis, [(i, (i + 1) % count) for i in range(ends)]),
                cells,
                lax.ppermute(head, axis, [((i + 1) % count, i) for i in range(ends)]),
            ],
            axis=dim,
        )
    return cells


def dft_table(length, direction, factor):
    counter = jnp.arange(length, dtype=jnp.int32)
    product = counter[:, None] * counter[None, :] % length
    angles = product.astype(jnp.float32) * (2.0 * math.pi / length)
    cosine = jnp.cos(angles) * factor
    sines = jnp.sin(angles) * (factor * direction)
    return jnp.stack([jnp.stack([cosine, -sines], 1), jnp.stack([sines, cosine], 1)], 0)


def rotate(real_part, imag_part, phase_index, line_total, direction):
    angles = phase_index.astype(jnp.float32) * (2.0 * math.pi / line_total)
    cosine = jnp.cos(angles)
    sines = jnp.sin(angles) * direction
    return (real_part * cosine - imag_part * sines, imag_part * cosine + real_part * sines)


def stolt(slab_source, weights, starts, slab_rows):
    pieces = []
    for slab_index in range(weights.shape[0]):
        slab_data = slab_source[:, slab_index * slab_rows : (slab_index + 1) * slab_rows, :]

        def window_at(start_bin):
            return lax.dynamic_slice_in_dim(slab_data, start_bin, 256, 2)

        windows = jax.vmap(window_at)(starts[slab_index])
        remixed = jnp.einsum(
            "jcmb,jbo->cmjo",
            windows,
            weights[slab_index].astype(jnp.float32),
            precision=lax.Precision.HIGHEST,
        )
        pieces.append(remixed.reshape(2, slab_rows, -1))
    return jnp.concatenate(pieces, 1)


def body(raw, stolt_weights, band_start):
    groups = lax.axis_size("az")
    az_index = lax.axis_index("az")
    rg_index = lax.axis_index("rg")
    part_lines = raw.shape[1]
    bin_count = raw.shape[3]
    line_total = LINES_DEV * groups
    short_forward = dft_table(groups, -1.0, 1.0 / math.sqrt(groups))
    spread = jnp.einsum(
        "dkcp,cmpr->dmkr", short_forward, raw.astype(jnp.float32), precision=lax.Precision.HIGHEST
    )
    line_index = az_index * part_lines + jnp.arange(part_lines, dtype=jnp.int32)
    freq_index = jnp.arange(groups, dtype=jnp.int32)
    phase_index = line_index[:, None] * freq_index[None, :] % line_total
    real_part, imag_part = rotate(spread[0], spread[1], phase_index[:, :, None], line_total, -1.0)
    twisted = jnp.stack([real_part, imag_part])
    long_forward = dft_table(LINES_DEV, -1.0, 1.0 / math.sqrt(LINES_DEV))
    spectrum = jnp.einsum(
        "dkcm,cmjr->dkjr",
        long_forward,
        lax.all_to_all(twisted, "az", split_axis=2, concat_axis=1, tiled=True),
        precision=lax.Precision.HIGHEST,
    )
    spectrum_rows = spectrum[:, :, 0, :]
    slab_rows = LINES_DEV // SLABS
    block_count = bin_count // 128
    padded = with_halo(spectrum_rows, (("rg", 2),), 128)
    local_band = lax.dynamic_slice_in_dim(band_start, rg_index * block_count, block_count, 1)
    starts = (local_band - rg_index * block_count) * 128 + 128
    remapped = stolt(padded, stolt_weights, starts, slab_rows)
    long_inverse = dft_table(LINES_DEV, 1.0, 1.0 / math.sqrt(LINES_DEV))
    lines_back = jnp.einsum(
        "dmck,ckr->dmr", long_inverse, remapped, precision=lax.Precision.HIGHEST
    )
    all_lines = jnp.arange(LINES_DEV, dtype=jnp.int32)
    back_index = all_lines * az_index % line_total
    real_part, imag_part = rotate(
        lines_back[0], lines_back[1], back_index[:, None], line_total, 1.0
    )
    unrolled = jnp.stack([real_part, imag_part])[:, :, None, :]
    short_inverse = dft_table(groups, 1.0, 1.0 / math.sqrt(groups))
    focused = jnp.einsum(
        "dpck,cmkr->dmpr",
        short_inverse,
        lax.all_to_all(unrolled, "az", split_axis=1, concat_axis=2, tiled=True),
        precision=lax.Precision.HIGHEST,
    )
    return focused.astype(jnp.bfloat16)


def solution(mesh):
    placed = (P(None, ("frames", "az"), None, "rg"), P(None, "rg", None, None), P())
    return jax.shard_map(
        body,
        mesh=mesh,
        in_specs=placed,
        out_specs=P(None, ("frames", "az"), None, "rg"),
        check_vma=False,
    )
```

profile of v0, /device:TPU:0, one launch (start us, length us, event | category | flops | bytes accessed | tf_op | source)
XLA Modules:
  0.0 164.7 jit_solution(4455382401302081138)
XLA Ops:
  0.0 0.1 cosine_multiply_fusion.1
  0.1 0.1 broadcast_multiply_fusion.3
  0.1 0.1 fusion.88
  0.2 0.2 fusion.79
  0.4 2.3 %convolution_bitcast_fusion.1 = f32[2,32,8,1024]{3,2,1,0:T(8,128)S(1)} fusion(bf16[2,32,8,1024]{3,2,1,0:T(8,128)(2,1)} %param.3, f32[1,8,2,8]{3,1,2,0:T(8,128)S(1)} %get-tuple-element.21, f32[1,8,2,8]{3,1,2,0:T(8,128)S(1)} %get-tuple-element.22), kind=kOutput, calls=%fused_computation.29 | convolution fusion | flops 100663552 | bytes 3146752 | tf_op jit(solution)/shard_map/dkcp,cmpr->dmkr/dot_general | solution.py:72
  2.6 0.3 multiply_subtract_fusion.1
  2.9 0.2 pad_maximum_fusion.1
  3.2 2.6 %copy.49 = f32[2,32,8,1024]{3,1,0,2:T(8,128)} copy(f32[2,32,8,1024]{3,2,1,0:T(8,128)S(1)} %pad_maximum_fusion.1) | data formatting | bytes 4194304 | tf_op jit(solution)/shard_map/stack | solution.py:79
  5.7 7.3 %all-to-all-start = ((f32[2,32,8,1024]{3,1,0,2:T(8,128)}), f32[2,32,8,1024]{3,1,0,2:T(8,128)S(1)}, u32[]{:S(2)}, u32[]{:S(2)}) async-start(f32[2,32,8,1024]{3,1,0,2:T(8,128)} %copy.49), calls=%async_computation | async-start | bytes 4194304 | tf_op jit(solution)/shard_map/all_to_all | solution.py:84
  13.0 0.1 fusion.104
  13.0 1.0 fusion.64
  14.0 1.1 cosine_multiply_fusion
  15.1 1.0 broadcast_multiply_fusion.1
  16.1 1.2 fusion.46
  17.2 44.0 %all-to-all-done = f32[2,32,8,1024]{3,1,0,2:T(8,128)S(1)} async-done(((f32[2,32,8,1024]{3,1,0,2:T(8,128)}), f32[2,32,8,1024]{3,1,0,2:T(8,128)S(1)}, u32[]{:S(2)}, u32[]{:S(2)}) %all-to-all-start) | async-done | bytes 2097184 | tf_op jit(solution)/shard_map/all_to_all | solution.py:84
  61.2 0.1 copy.50
  61.4 0.0 copy-start.5
  61.4 3.6 %convolution_bitcast_fusion = f32[2,256,1024]{2,1,0:T(8,128)S(1)} fusion(f32[2,256,1024,1]{2,1,0,3:T(8,128)S(1)} %bitcast.139, f32[1,256,2,256]{3,1,2,0:T(8,128)S(1)} %get-tuple-element.16, f32[1,256,2,256]{3,1,2,0:T(8,128)S(1)} %get-tuple-element.17), kind=kOutput, calls=%fused_computation.28 | convolution fusion | flops 3221487616 | bytes 5242880 | tf_op jit(solution)/shard_map/dkcm,cmjr->dkjr/dot_general | solution.py:81
  65.0 1.3 collective-permute-start
  66.3 1.3 collective-permute-start.1
  67.6 0.0 copy-done.5
  67.6 0.1 multiply_add_fusion.2
  67.7 0.0 collective-permute-done
  67.8 2.0 %collective-permute-done.1 = f32[2,256,128]{2,1,0:T(8,128)S(1)} collective-permute-done((f32[2,256,128]{2,1,0:T(8,128)S(1)}, f32[2,256,128]{2,1,0:T(8,128)S(1)}, u32[]{:S(2)}, u32[]{:S(2)}) %collective-permute-start.1) | collective-permute-done | bytes 262176 | tf_op jit(solution)/shard_map/ppermute | solution.py:22
  69.8 0.2 pad_maximum_fusion
  70.0 1.3 fusion.110
  71.3 0.7 copy.57
  71.9 2.8 %gather_fusion.2 = f32[8,2,64,256]{2,1,3,0:T(2,128)S(1)} fusion(f32[2,64,1280]{1,0,2:T(2,128)S(1)} %copy.57, s32[8]{0:T(128)S(1)} %get-tuple-element.25), kind=kCustom, calls=%fused_computation.2 | custom fusion | bytes 2097248 | tf_op jit(solution)/shard_map/vmap()/gather | solution.py:51
  74.7 2.9 %fusion.30 = f32[8,2,8,8,128]{4,3,2,1,0:T(8,128)S(1)} fusion(f32[8,2,64,256]{2,1,3,0:T(2,128)S(1)} %gather_fusion.2, bf16[4,8,256,128]{3,2,1,0:T(8,128)(2,1)} %param.4), kind=kOutput, calls=%fused_computation.33 | convolution fusion | flops 402653184 | bytes 2097152 | tf_op jit(solution)/shard_map/jcmb,jbo->cmjo/dot_general | solution.py:54
  77.6 0.9 copy.116
  78.5 1.6 copy.54
  80.1 2.8 %gather_fusion.1 = f32[8,2,64,256]{2,1,3,0:T(2,128)S(1)} fusion(f32[2,64,1280]{1,0,2:T(2,128)S(1)} %copy.54, s32[8]{0:T(128)S(1)} %get-tuple-element.26), kind=kCustom, calls=%fused_computation.1 | custom fusion | bytes 2097248 | tf_op jit(solution)/shard_map/vmap()/gather | solution.py:51
  82.9 2.9 %fusion.27 = f32[8,2,8,8,128]{4,3,2,1,0:T(8,128)S(1)} fusion(f32[8,2,64,256]{2,1,3,0:T(2,128)S(1)} %gather_fusion.1, bf16[4,8,256,128]{3,2,1,0:T(8,128)(2,1)} %param.4), kind=kOutput, calls=%fused_computation.32 | convolution fusion | flops 402653184 | bytes 2097152 | tf_op jit(solution)/shard_map/jcmb,jbo->cmjo/dot_general | solution.py:54
  85.8 0.9 copy.117
  86.6 1.6 copy.51
  88.2 2.8 %gather_fusion = f32[8,2,64,256]{2,1,3,0:T(2,128)S(1)} fusion(f32[2,64,1280]{1,0,2:T(2,128)S(1)} %copy.51, s32[8]{0:T(128)S(1)} %get-tuple-element.23), kind=kCustom, calls=%fused_computation | custom fusion | bytes 2097248 | tf_op jit(solution)/shard_map/vmap()/gather | solution.py:51
  91.0 2.9 %fusion.24 = f32[8,2,8,8,128]{4,3,2,1,0:T(8,128)S(1)} fusion(f32[8,2,64,256]{2,1,3,0:T(2,128)S(1)} %gather_fusion, bf16[4,8,256,128]{3,2,1,0:T(8,128)(2,1)} %param.4), kind=kOutput, calls=%fused_computation.31 | convolution fusion | flops 402653184 | bytes 2097152 | tf_op jit(solution)/shard_map/jcmb,jbo->cmjo/dot_general | solution.py:54
  93.9 0.9 copy.118
  94.7 1.6 copy.60
  96.3 2.8 %gather_fusion.3 = f32[8,2,64,256]{2,1,3,0:T(2,128)S(1)} fusion(f32[2,64,1280]{1,0,2:T(2,128)S(1)} %copy.60, s32[8]{0:T(128)S(1)} %get-tuple-element.24), kind=kCustom, calls=%fused_computation.3 | custom fusion | bytes 2097248 | tf_op jit(solution)/shard_map/vmap()/gather | solution.py:51
  99.1 0.0 copy-start
  99.1 0.0 copy-start.1
  99.1 0.0 copy-start.2
  99.1 0.0 copy-start.3
  99.2 0.0 copy-start.4
  99.2 3.0 %fusion.33 = f32[8,2,8,8,128]{4,3,2,1,0:T(8,128)S(1)} fusion(f32[8,2,64,256]{2,1,3,0:T(2,128)S(1)} %gather_fusion.3, bf16[4,8,256,128]{3,2,1,0:T(8,128)(2,1)} %param.4), kind=kOutput, calls=%fused_computation.34 | convolution fusion | flops 402653184 | bytes 2097152 | tf_op jit(solution)/shard_map/jcmb,jbo->cmjo/dot_general | solution.py:54
  102.3 0.0 copy-done
  102.3 0.0 copy-done.1
  102.3 0.0 copy-done.2
  102.3 0.0 copy-done.3
  102.3 0.0 copy-done.4
  102.3 3.6 %fusion.18 = f32[2,256,1024]{2,1,0:T(8,128)S(1)} fusion(f32[2,64,1024]{2,1,0:T(8,128)S(1)} %bitcast.143, f32[2,64,1024]{2,1,0:T(8,128)S(1)} %bitcast.140, f32[2,64,1024]{2,1,0:T(8,128)S(1)} %bitcast.141, f32[2,64,1024]{2,1,0:T(8,128)S(1)} %bitcast.142, f32[1,256,2,256]{3,1,2,0:T(8,128)S(1)} %copy-done.4, f32[1,256,2,256]{3,1,2,0:T(8,128)S(1)} %copy-done.3), kind=kOutput, calls=%fused_computation.27 | convolution fusion | flops 3223060480 | bytes 5242880 | tf_op jit(solution)/shard_map/dmck,ckr->dmr/dot_general | solution.py:95
  105.9 0.3 multiply_subtract_fusion
  106.2 0.2 maximum_bitcast_fusion.2
  106.5 1.6 copy.63
  108.1 52.6 %all_to_all.33 = f32[2,256,1,1024]{3,0,2,1:T(2,128)S(1)} all-to-all(f32[2,256,1,1024]{3,0,2,1:T(2,128)S(1)} %copy.63), channel_id=1, replica_groups=mesh['frames'=2,'az'=8,'rg'=2] {'az'}, dimensions={1} | all-to-all | bytes 4194304 | tf_op jit(solution)/shard_map/all_to_all | solution.py:108
  160.6 3.0 %fusion.21 = bf16[2,32,8,1024]{3,2,0,1:T(8,128)(2,1)S(1)} fusion(f32[2,8,32,1,1024]{4,0,2,1,3:T(2,128)S(1)} %bitcast.138, f32[1,8,2,8]{3,1,2,0:T(8,128)S(1)} %get-tuple-element.20, f32[1,8,2,8]{3,1,2,0:T(8,128)S(1)} %get-tuple-element.19), kind=kOutput, calls=%fused_computation.30 | convolution fusion | flops 101187840 | bytes 3146752 | tf_op jit(solution)/shard_map/dpck,cmkr->dmpr/dot_general | solution.py:105
  163.6 1.1 copy.66
  (5 shorter events, 0.1 us)
Async XLA Ops:
  5.7 55.5 %all-to-all-start = ((f32[2,32,8,1024]{3,1,0,2:T(8,128)}), f32[2,32,8,1024]{3,1,0,2:T(8,128)S(1)}, u32[]{:S(2)}, u32[]{:S(2)}) async-start(f32[2,32,8,1024]{3,1,0,2:T(8,128)} %copy.49), calls=%async_computation | async-start | bytes 4194304 | tf_op jit(solution)/shard_map/all_to_all | solution.py:84
  61.4 6.3 %copy-start.5 = (s32[4,16]{1,0:T(4,128)S(1)}, s32[4,16]{1,0:T(4,128)}, u32[]{:S(2)}) copy-start(s32[4,16]{1,0:T(4,128)} %param.5) | copy-start | bytes 772
  65.0 2.7 %collective-permute-start = (f32[2,256,128]{2,1,0:T(8,128)S(1)}, f32[2,256,128]{2,1,0:T(8,128)S(1)}, u32[]{:S(2)}, u32[]{:S(2)}) collective-permute-start(f32[2,256,128]{2,1,0:T(8,128)S(1)} %get-tuple-element.13), channel_id=1, source_target_pairs={{0,1},{2,3},{4,5},{6,7},{8,9},{10,11},{12,13},{14,15},{16,17},{18,... | collective-permute-start | bytes 786440 | tf_op jit(solution)/shard_map/ppermute | solution.py:20
  66.3 3.4 %collective-permute-start.1 = (f32[2,256,128]{2,1,0:T(8,128)S(1)}, f32[2,256,128]{2,1,0:T(8,128)S(1)}, u32[]{:S(2)}, u32[]{:S(2)}) collective-permute-start(f32[2,256,128]{2,1,0:T(8,128)S(1)} %get-tuple-element.14), channel_id=1, source_target_pairs={{1,0},{3,2},{5,4},{7,6},{9,8},{11,10},{13,12},{15,14},{17,16},{19,... | collective-permute-start | bytes 786440 | tf_op jit(solution)/shard_map/ppermute | solution.py:22
  99.1 3.1 %copy-start = (f32[8,2,8,8,128]{4,3,0,2,1:T(8,128)S(1)}, f32[8,2,8,8,128]{4,3,0,2,1:T(8,128)}, u32[]{:S(2)}) copy-start(f32[8,2,8,8,128]{4,3,0,2,1:T(8,128)} %copy.116) | copy-start | bytes 1572868
  99.1 3.1 %copy-start.1 = (f32[8,2,8,8,128]{4,3,0,2,1:T(8,128)S(1)}, f32[8,2,8,8,128]{4,3,0,2,1:T(8,128)}, u32[]{:S(2)}) copy-start(f32[8,2,8,8,128]{4,3,0,2,1:T(8,128)} %copy.117) | copy-start | bytes 1572868
  99.1 3.1 %copy-start.2 = (f32[8,2,8,8,128]{4,3,0,2,1:T(8,128)S(1)}, f32[8,2,8,8,128]{4,3,0,2,1:T(8,128)}, u32[]{:S(2)}) copy-start(f32[8,2,8,8,128]{4,3,0,2,1:T(8,128)} %copy.118) | copy-start | bytes 1572868
  99.1 3.1 %copy-start.3 = (f32[1,256,2,256]{3,1,2,0:T(8,128)S(1)}, f32[1,256,2,256]{3,1,2,0:T(8,128)}, u32[]{:S(2)}) copy-start(f32[1,256,2,256]{3,1,2,0:T(8,128)} %get-tuple-element.15) | copy-start | bytes 1572868
  99.2 3.1 %copy-start.4 = (f32[1,256,2,256]{3,1,2,0:T(8,128)S(1)}, f32[1,256,2,256]{3,1,2,0:T(8,128)}, u32[]{:S(2)}) copy-start(f32[1,256,2,256]{3,1,2,0:T(8,128)} %get-tuple-element.18) | copy-start | bytes 1572868
where the time goes:
time: 165 us
  blocking collectives  52.6 us (32%)
  waiting for transfers between devices  46 us (28%)
  local copies, waits for them, and re-layouts  25.9 us (16%)
  matrix products  24.1 us (15%)
  starting transfers between devices  9.85 us (6%)
  other arithmetic  5.92 us (4%)
    all_to_all x1, blocking collectives, body(): lax.all_to_all(unrolled, 'az', split_axis=1, concat_axis=2, tiled=True)  52.6 us
    all_to_all x1, waiting for transfers between devices, body(): lax.all_to_all(twisted, 'az', split_axis=2, concat_axis=1, tiled=True)  44 us
    dot_general x4, matrix products, stolt(): jnp.einsum('jcmb,jbo->cmjo', windows, weights[slab_index].astype(jnp.floa...  11.7 us
    gather x4, local copies, waits for them, and re-layouts, window_at(): return lax.dynamic_slice_in_dim(slab_data, start_bin, 256, 2)  11.2 us
    all_to_all x1, starting transfers between devices, body(): lax.all_to_all(twisted, 'az', split_axis=2, concat_axis=1, tiled=True)  7.25 us
    slice x5, local copies, waits for them, and re-layouts, stolt(): slab_source[:, slab_index * slab_rows:(slab_index + 1) * slab_rows, :]  6.67 us
    dot_general x1, matrix products, body(): jnp.einsum('dkcm,cmjr->dkjr', long_forward, lax.all_to_all(twisted, 'az',...  3.58 us
    dot_general x1, matrix products, body(): jnp.einsum('dmck,ckr->dmr', long_inverse, remapped, precision=lax.Precisi...  3.58 us
  transfers between devices with their start and end apart: 3, of which 2 were waited for; matrix products, arithmetic and copies ran while one was open for 3% of the time, Pallas kernels for 0%

commit v1 on v0

--- a/solution.py
+++ b/solution.py
@@ -1,12 +1,21 @@
+import functools
 import math
 
 import jax
 import jax.numpy as jnp
+import numpy as np
 from jax import lax
+from jax.experimental import pallas as pl
+from jax.experimental.pallas import tpu as pltpu
 from jax.sharding import PartitionSpec as P
 
 LINES_DEV = 256
 SLABS = 4
+TILE = 128
+BF16 = jnp.bfloat16
+F32 = jnp.float32
+CODE_STEPS = 256.0
+FULL = 32767.0
 
 
 def with_halo(cells, sides, width):
@@ -61,7 +70,7 @@
     return jnp.concatenate(pieces, 1)
 
 
-def body(raw, stolt_weights, band_start):
+def generic_body(raw, stolt_weights, band_start):
     groups = lax.axis_size("az")
     az_index = lax.axis_index("az")
     rg_index = lax.axis_index("rg")
@@ -111,6 +120,289 @@
     return focused.astype(jnp.bfloat16)
 
 
+NDEV = 8
+MLOC = LINES_DEV // NDEV
+ROWS = 2 * MLOC
+HALF = 16
+VMEM_LIMIT = 48 * 1024 * 1024
+
+
+def split2(x):
+    hi = x.astype(BF16)
+    lo = (x - hi.astype(F32)).astype(BF16)
+    return hi, lo
+
+
+def mm(a, b):
+    return jnp.dot(a, b, preferred_element_type=F32)
+
+
+def short_forward_table():
+    k1, co, mo = np.meshgrid(np.arange(8), np.arange(2), np.arange(HALF), indexing="ij")
+    ci, mi, p = np.meshgrid(np.arange(2), np.arange(HALF), np.arange(8), indexing="ij")
+    k1, co, mo = (v.reshape(-1, 1) for v in (k1, co, mo))
+    ci, mi, p = (v.reshape(1, -1) for v in (ci, mi, p))
+    turn = (k1 * p + 2 * (co - ci)) % 8
+    unit = np.array([1, math.sqrt(0.5), 0, -math.sqrt(0.5), -1, -math.sqrt(0.5), 0, math.sqrt(0.5)])
+    table = np.where(mo == mi, unit[turn], 0.0).astype(np.float32)
+    hi = table.astype(jnp.bfloat16)
+    lo = (table - hi.astype(np.float32)).astype(jnp.bfloat16)
+    return np.stack([hi, lo])
+
+
+def cos_pair(turn, total, factor):
+    value = jnp.cos(turn.astype(F32) * (2.0 * math.pi / total)) * factor
+    hi = lax.reduce_precision(value, 8, 7)
+    return jnp.stack([hi.astype(BF16), (value - hi).astype(BF16)])
+
+
+def long_turn(row, col, me):
+    k2 = row // 128 * 64 + row % 64
+    co = row // 64 % 2
+    ci = col // LINES_DEV
+    line = ((col // MLOC % NDEV) ^ me) * MLOC + col % MLOC
+    total = NDEV * LINES_DEV
+    return (line * (NDEV * k2 + me) + (co - ci + 4) * (total // 4)) % total
+
+
+def long_tables(me):
+    total = NDEV * LINES_DEV
+    shape = (2 * LINES_DEV, 2 * LINES_DEV)
+    a = lax.broadcasted_iota(jnp.int32, shape, 0)
+    b = lax.broadcasted_iota(jnp.int32, shape, 1)
+    forward = cos_pair(long_turn(a, b, me), total, 1.0 / 32.0)
+    inverse = cos_pair(long_turn(b, a, me), total, 1.0 / 64.0)
+    return forward, inverse
+
+
+def short_inverse_table(me):
+    a = lax.broadcasted_iota(jnp.int32, (256, 256), 0)
+    b = lax.broadcasted_iota(jnp.int32, (256, 256), 1)
+    co, mo, p = a // 128, a // 8 % HALF, a % 8
+    k1, ci, mi = (b // 32) ^ me, b // HALF % 2, b % HALF
+    turn = (k1 * p + 2 * (ci - co) + 8) % 8
+    value = jnp.cos(turn.astype(F32) * (2.0 * math.pi / 8))
+    value = jnp.where(mo == mi, value, 0.0)
+    hi = lax.reduce_precision(value, 8, 7)
+    return jnp.stack([hi.astype(BF16), (value - hi).astype(BF16)])
+
+
+def store_coded(out_ref, pieces, tiles):
+    peak = None
+    for _, value in pieces:
+        top = jnp.max(jnp.abs(value), axis=0, keepdims=True)
+        peak = top if peak is None else jnp.maximum(peak, top)
+    code = jnp.ceil(jnp.log2(jnp.maximum(peak, 1e-30) * (1.0 / FULL)) * CODE_STEPS + 0.01)
+    inverse = jnp.exp2(code * (-1.0 / CODE_STEPS))
+    for row, value in pieces:
+        coded = jnp.round(value * inverse).astype(jnp.int32).astype(jnp.int16)
+        for tile in range(tiles):
+            at = tile * ROWS + row
+            out_ref[at : at + value.shape[0], :] = coded[:, tile * TILE : (tile + 1) * TILE]
+    which = lax.broadcasted_iota(jnp.int32, (16, TILE), 0)
+    scales = jnp.zeros((16, TILE), F32)
+    for tile in range(tiles):
+        scales = jnp.where(which == tile, code[:, tile * TILE : (tile + 1) * TILE], scales)
+    out_ref[tiles * ROWS : tiles * ROWS + 16, :] = scales.astype(jnp.int32).astype(jnp.int16)
+
+
+def load_scales(ref, tiles):
+    code = ref[tiles * ROWS : tiles * ROWS + 16, :].astype(jnp.int32).astype(F32)
+    return jnp.exp2(code * (1.0 / CODE_STEPS))
+
+
+def load_coded(ref, scale_row, at):
+    return ref[pl.ds(at, ROWS), :].astype(jnp.int32).astype(F32) * scale_row
+
+
+def spread_kernel(me_ref, x_ref, table_ref, *out_refs):
+    me = me_ref[0]
+    hi, lo = [
+        jnp.concatenate(
+            [table_ref[part, pl.ds(pl.multiple_of((me ^ i) * 32, 32), 32), :] for i in range(NDEV)], 0
+        )
+        for part in range(2)
+    ]
+    halves = []
+    for h in range(2):
+        at = h * 128
+        x = jnp.concatenate([x_ref[at : at + 128, :], x_ref[256 + at : 256 + at + 128, :]], 0)
+        halves.append(mm(hi, x) + mm(lo, x))
+    tiles = x_ref.shape[1] // TILE
+    for i in range(NDEV):
+        pieces = []
+        for c in range(2):
+            for h in range(2):
+                at = i * 32 + c * HALF
+                pieces.append((c * MLOC + h * HALF, halves[h][at : at + HALF, :]))
+        store_coded(out_refs[i], pieces, tiles)
+
+
+def gather_columns(refs, scales, at_rows, rows_of):
+    columns = []
+    for at, row in zip(at_rows, rows_of):
+        parts = [load_coded(ref, scale[row : row + 1, :], at) for ref, scale in zip(refs, scales)]
+        columns.append(
+            jnp.concatenate([v[:MLOC] for v in parts] + [v[MLOC:] for v in parts], 0)
+        )
+    return split2(jnp.concatenate(columns, 1) if len(columns) > 1 else columns[0])
+
+
+def long_product(table_ref, hi, lo):
+    return mm(table_ref[0], hi) + mm(table_ref[0], lo) + mm(table_ref[1], hi)
+
+
+def edge_kernel(side_ref, table_ref, *refs):
+    in_refs, out_ref = refs[:NDEV], refs[NDEV]
+    tiles = (in_refs[0].shape[0] - 16) // ROWS
+    edge = side_ref[0]
+    parts = []
+    which = lax.broadcasted_iota(jnp.int32, (16, TILE), 0)
+    for ref in in_refs:
+        scales = load_scales(ref, tiles)
+        scale = jnp.sum(jnp.where(which == edge, scales, 0.0), axis=0, keepdims=True)
+        parts.append(load_coded(ref, scale, pl.multiple_of(edge * ROWS, ROWS)))
+    x = jnp.concatenate([v[:MLOC] for v in parts] + [v[MLOC:] for v in parts], 0)
+    hi, lo = split2(x)
+    out_ref[0], out_ref[1] = split2(long_product(table_ref, hi, lo))
+
+
+def forward_kernel(table_ref, *refs):
+    in_refs, out_ref = refs[:NDEV], refs[NDEV]
+    tiles = (in_refs[0].shape[0] - 16) // ROWS
+    scales = [load_scales(ref, tiles) for ref in in_refs]
+    for tile in range(0, tiles, 2):
+        pair = (tile, tile + 1)
+        hi, lo = gather_columns(in_refs, scales, [t * ROWS for t in pair], pair)
+        result = long_product(table_ref, hi, lo)
+        for at, t in enumerate(pair):
+            out_ref[t, 0], out_ref[t, 1] = split2(result[:, at * TILE : (at + 1) * TILE])
+
+
+def remap_kernel(starts_ref, spectrum_ref, weights_ref, table_ref, *refs):
+    out_refs, hi_ref, lo_ref = refs[:NDEV], refs[NDEV], refs[NDEV + 1]
+    tiles = weights_ref.shape[1]
+    for j in range(tiles):
+        for g in range(SLABS):
+            first = starts_ref[g, j]
+            second = lax.rem(first + 1, tiles + 1)
+            rows = slice(g * 128, (g + 1) * 128)
+            window = jnp.concatenate(
+                [
+                    jnp.concatenate([spectrum_ref[first, part, rows, :], spectrum_ref[second, part, rows, :]], 1)
+                    for part in range(2)
+                ],
+                0,
+            )
+            both = mm(window, weights_ref[g, j])
+            hi, lo = split2(both[:128] + both[128:])
+            hi_ref[rows, j * TILE : (j + 1) * TILE] = hi
+            lo_ref[rows, j * TILE : (j + 1) * TILE] = lo
+    lines = long_product(table_ref, hi_ref[...], lo_ref[...])
+    for i in range(NDEV):
+        pieces = []
+        for c in range(2):
+            at = c * LINES_DEV + i * MLOC
+            pieces.append((c * MLOC, lines[at : at + MLOC, :]))
+        store_coded(out_refs[i], pieces, tiles)
+
+
+def image_kernel(table_ref, *refs):
+    in_refs, out_ref = refs[:NDEV], refs[NDEV]
+    tiles = (in_refs[0].shape[0] - 16) // ROWS
+    scales = [load_scales(ref, tiles) for ref in in_refs]
+    for tile in range(0, tiles, 2):
+        values = [
+            jnp.concatenate(
+                [load_coded(ref, scale[t : t + 1, :], t * ROWS) for t in (tile, tile + 1)], 1
+            )
+            for ref, scale in zip(in_refs, scales)
+        ]
+        for h in range(2):
+            x = jnp.concatenate(
+                [v[c * MLOC + h * HALF : c * MLOC + (h + 1) * HALF] for v in values for c in range(2)], 0
+            )
+            hi, lo = split2(x)
+            result = (mm(table_ref[0], hi) + mm(table_ref[0], lo) + mm(table_ref[1], hi)).astype(BF16)
+            for c in range(2):
+                at = c * 256 + h * 128
+                out_ref[at : at + 128, tile * TILE : (tile + 2) * TILE] = result[c * 128 : (c + 1) * 128]
+
+
+def vmem_call(kernel, name, out_shape, smem=0, vmem=0, scratch=()):
+    return pl.pallas_call(
+        kernel,
+        name=name,
+        out_shape=out_shape,
+        in_specs=[pl.BlockSpec(memory_space=pltpu.SMEM)] * smem
+        + [pl.BlockSpec(memory_space=pltpu.VMEM)] * vmem,
+        out_specs=jax.tree.map(lambda _: pl.BlockSpec(memory_space=pltpu.VMEM), out_shape),
+        scratch_shapes=scratch,
+        compiler_params=pltpu.CompilerParams(vmem_limit_bytes=VMEM_LIMIT),
+    )
+
+
+def exchange(messages):
+    out = list(messages)
+    for i in (6, 7, 4, 5, 3, 2, 1):
+        out[i] = lax.ppermute(messages[i], "az", [(d, d ^ i) for d in range(NDEV)])
+    return out
+
+
+def fast_body(raw, stolt_weights, band_start):
+    me = lax.axis_index("az").astype(jnp.int32)
+    rg = lax.axis_index("rg").astype(jnp.int32)
+    bins = raw.shape[3]
+    tiles = bins // TILE
+    message = [jax.ShapeDtypeStruct((tiles * ROWS + 16, TILE), jnp.int16)] * NDEV
+    forward_table, inverse_table = long_tables(me)
+    image_table = short_inverse_table(me)
+
+    sent = vmem_call(spread_kernel, "spread", message, smem=1, vmem=2)(
+        me[None], raw.reshape(2 * MLOC * NDEV, bins), jnp.asarray(short_forward_table())
+    )
+    got = exchange(sent)
+
+    edge = vmem_call(
+        edge_kernel, "edge", jax.ShapeDtypeStruct((2, 512, TILE), BF16), smem=1, vmem=1 + NDEV
+    )(((1 - rg) * (tiles - 1))[None], forward_table, *got)
+    halo = lax.ppermute(edge, "rg", [(0, 1), (1, 0)])
+    spectrum = vmem_call(
+        forward_kernel,
+        "forward",
+        jax.ShapeDtypeStruct((tiles + 1, 2, 512, TILE), BF16),
+        vmem=1 + NDEV,
+    )(forward_table, *got)
+    spectrum = lax.dynamic_update_slice_in_dim(spectrum, halo[None], tiles, 0)
+
+    local = lax.dynamic_slice_in_dim(band_start, rg * tiles, tiles, 1) - rg * tiles
+    slots = (local + (tiles + 1)) % (tiles + 1)
+    back = vmem_call(
+        remap_kernel,
+        "remap",
+        message,
+        smem=1,
+        vmem=3,
+        scratch=[pltpu.VMEM((512, bins), BF16), pltpu.VMEM((512, bins), BF16)],
+    )(slots, spectrum, stolt_weights, inverse_table)
+    lines = exchange(back)
+
+    image = vmem_call(
+        image_kernel, "image", jax.ShapeDtypeStruct((2 * MLOC * NDEV, bins), BF16), vmem=1 + NDEV
+    )(image_table, *lines)
+    return image.reshape(2, MLOC, NDEV, bins)
+
+
+def body(raw, stolt_weights, band_start):
+    fast = (
+        lax.axis_size("az") == NDEV
+        and lax.axis_size("rg") == 2
+        and raw.shape[1:3] == (MLOC, NDEV)
+        and raw.shape[3] % (2 * TILE) == 0
+    )
+    return (fast_body if fast else generic_body)(raw, stolt_weights, band_start)
+
+
 def solution(mesh):
     placed = (P(None, ("frames", "az"), None, "rg"), P(None, "rg", None, None), P())
     return jax.shard_map(

time: 165 us -> 75.2 us (0.46)
  blocking collectives: 52.6 us -> 0 us
  waiting for transfers between devices: 46 us -> 20.6 us
  matrix products: 24.1 us -> 0 us
  local copies, waits for them, and re-layouts: 25.9 us -> 3.64 us
  starting transfers between devices: 9.85 us -> 24.6 us
  Pallas kernels: 0 us -> 10.9 us
  other arithmetic: 5.92 us -> 14.5 us
    all_to_all x1 -> x0, blocking collectives: 52.6 us -> none  [body(): lax.all_to_all(unrolled, 'az', split_axis=1, concat_axis=2, tiled=True)]
    all_to_all x1 -> x0, waiting for transfers between devices: 44 us -> none  [body(): lax.all_to_all(twisted, 'az', split_axis=2, concat_axis=1, tiled=True)]
    dot_general x8 -> x0, matrix products: 24.1 us -> none  [the longest x4 11.7 us: stolt(): jnp.einsum('jcmb,jbo->cmjo', windows, weights[slab_index].astype(jnp.floa...]
    ppermute x2 -> x15, starting transfers between devices: 2.6 us -> 24.6 us  [the longest x14 24.6 us: exchange(): out[i] = lax.ppermute(messages[i], 'az', [(d, d ^ i) for d in range(NDEV)])]
    ppermute x2 -> x15, waiting for transfers between devices: 2.02 us -> 20.6 us  [the longest x14 20.6 us: exchange(): out[i] = lax.ppermute(messages[i], 'az', [(d, d ^ i) for d in range(NDEV)])]
    convert_element_type x0 -> x2, other arithmetic: none -> 11.9 us  [the longest x1 10.3 us: cos_pair(): return jnp.stack([hi.astype(BF16), (value - hi).astype(BF16)])]
    gather x4 -> x0, local copies, waits for them, and re-layouts: 11.2 us -> none  [window_at(): return lax.dynamic_slice_in_dim(slab_data, start_bin, 256, 2)]
    pallas_call x0 -> x5, Pallas kernels: none -> 10.9 us  [the longest x1 5.06 us: fast_body(): vmem_call(remap_kernel, 'remap', message, smem=1, vmem=3, scratch=[pltpu....]
  transfers between devices with their start and end apart: 3 -> 15, of which waited for: 2 -> 5; matrix products, arithmetic and copies ran while one was open for 3% -> 20% of each run, Pallas kernels for 0% -> 3%
where the time goes in v1:
time: 75.2 us; the launch traced here: 74.5 us
  starting transfers between devices  24.6 us (33%)
  waiting for transfers between devices  20.6 us (27%)
  other arithmetic  14.5 us (19%)
  Pallas kernels  10.9 us (14%)
  local copies, waits for them, and re-layouts  3.64 us (5%)
    ppermute x14, starting transfers between devices, exchange(): out[i] = lax.ppermute(messages[i], 'az', [(d, d ^ i) for d in range(NDEV)])  24.6 us
    ppermute x14, waiting for transfers between devices, exchange(): out[i] = lax.ppermute(messages[i], 'az', [(d, d ^ i) for d in range(NDEV)])  20.6 us
    convert_element_type x1, other arithmetic, cos_pair(): return jnp.stack([hi.astype(BF16), (value - hi).astype(BF16)])  10.3 us
    pallas_call x1, Pallas kernels, fast_body(): vmem_call(remap_kernel, 'remap', message, smem=1, vmem=3, scratch=[pltpu....  5.06 us
    unnamed x10, local copies, waits for them, and re-layouts  3.6 us
    another operation x2, other arithmetic, cos_pair(): return jnp.stack([hi.astype(BF16), (value - hi).astype(BF16)])  2.44 us
    pallas_call x1, Pallas kernels, fast_body(): vmem_call(image_kernel, 'image', jax.ShapeDtypeStruct((2 * MLOC * NDEV, b...  2.06 us
    pallas_call x1, Pallas kernels, fast_body(): vmem_call(forward_kernel, 'forward', jax.ShapeDtypeStruct((tiles + 1, 2,...  1.93 us
  transfers between devices with their start and end apart: 15, of which 5 were waited for; matrix products, arithmetic and copies ran while one was open for 20% of the time, Pallas kernels for 3%

profile of v1, /device:TPU:0, one launch (start us, length us, event | category | flops | bytes accessed | tf_op | source)
XLA Modules:
  0.0 74.5 jit_solution(3974245911630479732)
XLA Ops:
  0.0 0.0 copy-start.2
  0.0 1.2 %copy-done.2 = bf16[2,32,8,1024]{3,2,1,0:T(8,128)(2,1)S(1)} copy-done((bf16[2,32,8,1024]{3,2,1,0:T(8,128)(2,1)S(1)}, bf16[2,32,8,1024]{3,2,1,0:T(8,128)(2,1)}, u32[]{:S(2)}) %copy-start.2) | copy-done | bytes 1048600
  1.2 0.0 copy-start.3
  1.2 0.9 %copy-done.3 = bf16[2,256,256]{2,1,0:T(8,128)(2,1)S(1)} copy-done((bf16[2,256,256]{2,1,0:T(8,128)(2,1)S(1)}, bf16[2,256,256]{2,1,0:T(8,128)(2,1)}, u32[]{:S(2)}) %copy-start.3) | copy-done | bytes 262168
  2.2 1.2 %spread.1 = (s16[528,128]{1,0:T(8,128)(2,1)S(1)}, s16[528,128]{1,0:T(8,128)(2,1)S(1)}, s16[528,128]{1,0:T(8,128)(2,1)S(1)}, s16[528,128]{1,0:T(8,128)(2,1)S(1)},...) custom-call(s32[1]{0:T(128)} %bitcast.me_ref, ...), custom_call_target="tpu_custom_call" | custom-call | tf_op jit(solution)/shard_map/spread/pallas_call | solution.py:361
  3.4 3.0 %collective-permute-start = (s16[528,128]{1,0:T(8,128)(2,1)S(1)}, s16[528,128]{1,0:T(8,128)(2,1)S(1)}, u32[]{:S(2)}, u32[]{:S(2)}) collective-permute-start(s16[528,128]{1,0:T(8,128)(2,1)S(1)} %get-tuple-element.22), channel_id=1, source_target_pairs={{0,2},{2,0},{4,6},{6,4},{8,10},{10,8},{12,14},{14,12},{1,3},{3,1},... | collective-permute-start | bytes 405512 | tf_op jit(solution)/shard_map/ppermute | solution.py:348
  6.4 1.6 %collective-permute-start.1 = (s16[528,128]{1,0:T(8,128)(2,1)S(1)}, s16[528,128]{1,0:T(8,128)(2,1)S(1)}, u32[]{:S(2)}, u32[]{:S(2)}) collective-permute-start(s16[528,128]{1,0:T(8,128)(2,1)S(1)} %get-tuple-element.23), channel_id=1, source_target_pairs={{0,4},{2,6},{4,0},{6,2},{8,12},{10,14},{12,8},{14,10},{1,5},{3,7},... | collective-permute-start | bytes 405512 | tf_op jit(solution)/shard_map/ppermute | solution.py:348
  8.0 0.0 collective-permute-start.2
  8.0 3.0 %collective-permute-start.3 = (s16[528,128]{1,0:T(8,128)(2,1)S(1)}, s16[528,128]{1,0:T(8,128)(2,1)S(1)}, u32[]{:S(2)}, u32[]{:S(2)}) collective-permute-start(s16[528,128]{1,0:T(8,128)(2,1)S(1)} %get-tuple-element.25), channel_id=1, source_target_pairs={{0,8},{2,10},{4,12},{6,14},{8,0},{10,2},{12,4},{14,6},{1,9},{3,11}... | collective-permute-start | bytes 405512 | tf_op jit(solution)/shard_map/ppermute | solution.py:348
  11.0 1.3 %collective-permute-start.4 = (s16[528,128]{1,0:T(8,128)(2,1)S(1)}, s16[528,128]{1,0:T(8,128)(2,1)S(1)}, u32[]{:S(2)}, u32[]{:S(2)}) collective-permute-start(s16[528,128]{1,0:T(8,128)(2,1)S(1)} %get-tuple-element.26), channel_id=1, source_target_pairs={{0,10},{2,8},{4,14},{6,12},{8,2},{10,0},{12,6},{14,4},{1,11},{3,9}... | collective-permute-start | bytes 405512 | tf_op jit(solution)/shard_map/ppermute | solution.py:348
  12.4 10.3 %reduce-precision_convert_fusion = (bf16[1,512,512]{2,1,0:T(8,128)(2,1)S(1)}, bf16[1,512,512]{2,1,0:T(8,128)(2,1)}, bf16[1,512,512]{2,1,0:T(8,128)(2,1)}, bf16[1,512,512]{2,1,0:T(8,128)(2,1)}) fusion(s32[512]{0:T(512)S(1)} %get-tuple-element.65, s32[512]{0:T(512)S(1)} %get-tuple-element.75, pred[512]{0:T(512)(128)(4,1)S(1)} %get-tuple-element.70, ...), kind=kLoop, calls=%fused_computation.27 | loop fusion | flops 30408704 | bytes 2124804 | tf_op jit(solution)/shard_map/convert_element_type | solution.py:156
  22.7 0.0 copy-start.4
  22.7 0.0 collective-permute-done.refs_1_
  22.7 3.7 %collective-permute-start.5 = (s16[528,128]{1,0:T(8,128)(2,1)S(1)}, s16[528,128]{1,0:T(8,128)(2,1)S(1)}, u32[]{:S(2)}, u32[]{:S(2)}) collective-permute-start(s16[528,128]{1,0:T(8,128)(2,1)S(1)} %get-tuple-element.27), channel_id=1, source_target_pairs={{0,12},{2,14},{4,8},{6,10},{8,4},{10,6},{12,0},{14,2},{1,13},{3,15... | collective-permute-start | bytes 405512 | tf_op jit(solution)/shard_map/ppermute | solution.py:348
  26.4 0.0 collective-permute-done.1.refs_2_
  26.4 0.1 collective-permute-start.6
  26.5 1.3 %pad_maximum_fusion.table_ref = bf16[2,512,512]{2,1,0:T(8,128)(2,1)S(1)} fusion(bf16[1,512,512]{2,1,0:T(8,128)(2,1)} %get-tuple-element.40, bf16[1,512,512]{2,1,0:T(8,128)(2,1)} %get-tuple-element.39), kind=kLoop, calls=%fused_computation.62 | loop fusion | flops 524288 | bytes 2097152 | tf_op jit(solution)/shard_map/stack | solution.py:156
  27.8 0.0 collective-permute-done.2.refs_3_
  27.8 0.0 collective-permute-done.3.refs_4_
  27.8 0.0 collective-permute-done.4.refs_5_
  27.8 2.6 %collective-permute-done.5.refs_6_ = s16[528,128]{1,0:T(8,128)(2,1)S(1)} collective-permute-done((s16[528,128]{1,0:T(8,128)(2,1)S(1)}, s16[528,128]{1,0:T(8,128)(2,1)S(1)}, u32[]{:S(2)}, u32[]{:S(2)}) %collective-permute-start.5) | collective-permute-done | bytes 135200 | tf_op jit(solution)/shard_map/ppermute | solution.py:348
  30.4 3.8 %collective-permute-done.6.refs_7_ = s16[528,128]{1,0:T(8,128)(2,1)S(1)} collective-permute-done((s16[528,128]{1,0:T(8,128)(2,1)S(1)}, s16[528,128]{1,0:T(8,128)(2,1)S(1)}, u32[]{:S(2)}, u32[]{:S(2)}) %collective-permute-start.6) | collective-permute-done | bytes 135200 | tf_op jit(solution)/shard_map/ppermute | solution.py:348
  34.2 0.6 edge.1
  34.8 0.1 collective-permute-start.7
  34.9 0.0 copy-done.4
  34.9 0.1 add_select_fusion.9.starts_ref
  35.0 1.1 %pad_maximum_fusion.1.table_ref = bf16[2,512,512]{2,1,0:T(8,128)(2,1)S(1)} fusion(bf16[1,512,512]{2,1,0:T(8,128)(2,1)} %get-tuple-element.38, bf16[1,512,512]{2,1,0:T(8,128)(2,1)S(1)} %get-tuple-element.37), kind=kLoop, calls=%fused_computation.63 | loop fusion | flops 524288 | bytes 2097152 | tf_op jit(solution)/shard_map/stack | solution.py:156
  36.2 0.0 copy-start.1
  36.2 1.9 %forward.1 = bf16[9,2,512,128]{3,2,1,0:T(8,128)(2,1)S(1)} custom-call(bf16[2,512,512]{2,1,0:T(8,128)(2,1)S(1)} %pad_maximum_fusion.table_ref, s16[528,128]{1,0:T(8,128)(2,1)S(1)} %get-tuple-element.21.refs_0_, s16[528,128]{1,0:T(8,128)(2,1)S(1)} %collective-permute-done.refs_1_, s16[528,128]{1,0:T(8,128)(2,1)S(1)} %collective-permute-done.1.refs_2_, ...), custom_call_target="tpu_custom_call" | custom-call | tf_op jit(solution)/shard_map/forward/pallas_call | solution.py:370
  38.1 0.0 collective-permute-done.7
  38.2 0.0 copy-start
  38.2 1.4 %copy-done = bf16[9,2,512,128]{3,2,1,0:T(8,128)(2,1)} copy-done((bf16[9,2,512,128]{3,2,1,0:T(8,128)(2,1)}, bf16[9,2,512,128]{3,2,1,0:T(8,128)(2,1)S(1)}, u32[]{:S(2)}) %copy-start) | copy-done | bytes 2359320
  39.6 0.0 copy-done.1
  39.6 5.1 %remap.1 = (s16[528,128]{1,0:T(8,128)(2,1)S(1)}, s16[528,128]{1,0:T(8,128)(2,1)S(1)}, s16[528,128]{1,0:T(8,128)(2,1)S(1)}, s16[528,128]{1,0:T(8,128)(2,1)S(1)}, ...) custom-call(s32[4,8]{1,0:T(4,128)S(1)} %add_select_fusion.9.starts_r, ...), custom_call_target="tpu_custom_call" | custom-call | tf_op jit(solution)/shard_map/remap/pallas_call | solution.py:380
  44.7 3.7 %collective-permute-start.10 = (s16[528,128]{1,0:T(8,128)(2,1)S(1)}, s16[528,128]{1,0:T(8,128)(2,1)S(1)}, u32[]{:S(2)}, u32[]{:S(2)}) collective-permute-start(s16[528,128]{1,0:T(8,128)(2,1)S(1)} %get-tuple-element.32), channel_id=1, source_target_pairs={{0,6},{2,4},{4,2},{6,0},{8,14},{10,12},{12,10},{14,8},{1,7},{3,5},... | collective-permute-start | bytes 405512 | tf_op jit(solution)/shard_map/ppermute | solution.py:348
  48.4 0.2 collective-permute-start.11
  48.6 2.8 %collective-permute-start.12 = (s16[528,128]{1,0:T(8,128)(2,1)S(1)}, s16[528,128]{1,0:T(8,128)(2,1)S(1)}, u32[]{:S(2)}, u32[]{:S(2)}) collective-permute-start(s16[528,128]{1,0:T(8,128)(2,1)S(1)} %get-tuple-element.34), channel_id=1, source_target_pairs={{0,10},{2,8},{4,14},{6,12},{8,2},{10,0},{12,6},{14,4},{1,11},{3,9}... | collective-permute-start | bytes 405512 | tf_op jit(solution)/shard_map/ppermute | solution.py:348
  51.4 2.5 %collective-permute-start.13 = (s16[528,128]{1,0:T(8,128)(2,1)S(1)}, s16[528,128]{1,0:T(8,128)(2,1)S(1)}, u32[]{:S(2)}, u32[]{:S(2)}) collective-permute-start(s16[528,128]{1,0:T(8,128)(2,1)S(1)} %get-tuple-element.35), channel_id=1, source_target_pairs={{0,12},{2,14},{4,8},{6,10},{8,4},{10,6},{12,0},{14,2},{1,13},{3,15... | collective-permute-start | bytes 405512 | tf_op jit(solution)/shard_map/ppermute | solution.py:348
  53.9 2.3 %collective-permute-start.14 = (s16[528,128]{1,0:T(8,128)(2,1)S(1)}, s16[528,128]{1,0:T(8,128)(2,1)S(1)}, u32[]{:S(2)}, u32[]{:S(2)}) collective-permute-start(s16[528,128]{1,0:T(8,128)(2,1)S(1)} %get-tuple-element.36), channel_id=1, source_target_pairs={{0,14},{2,12},{4,10},{6,8},{8,6},{10,4},{12,2},{14,0},{1,15},{3,13... | collective-permute-start | bytes 405512 | tf_op jit(solution)/shard_map/ppermute | solution.py:348
  56.1 0.0 collective-permute-done.10.refs_3_
  56.1 0.5 collective-permute-start.8
  56.7 10.7 %collective-permute-done.11.refs_4_ = s16[528,128]{1,0:T(8,128)(2,1)S(1)} collective-permute-done((s16[528,128]{1,0:T(8,128)(2,1)S(1)}, s16[528,128]{1,0:T(8,128)(2,1)S(1)}, u32[]{:S(2)}, u32[]{:S(2)}) %collective-permute-start.11) | collective-permute-done | bytes 135200 | tf_op jit(solution)/shard_map/ppermute | solution.py:348
  67.4 0.0 collective-permute-start.9
  67.4 1.6 %reduce-precision_convert_fusion.2 = (bf16[1,256,256]{2,1,0:T(8,128)(2,1)S(1)}, bf16[1,256,256]{2,1,0:T(8,128)(2,1)S(1)}) fusion(s32[256]{0:T(256)S(1)} %get-tuple-element.49, s32[256]{0:T(256)S(1)} %get-tuple-element.57, pred[256]{0:T(512)(128)(4,1)S(1)} %get-tuple-element.45, s32[256]{0:T(256)S(1)} %get-tuple-element.51, s32[256]{0:T(256)S(1)} %get-tuple-element.58, ...), kind=kLoop, calls=%fused_computation.78 | loop fusion | flops 3473408 | bytes 275972 | tf_op jit(solution)/shard_map/convert_element_type | solution.py:187
  69.1 1.2 %collective-permute-done.12.refs_5_ = s16[528,128]{1,0:T(8,128)(2,1)S(1)} collective-permute-done((s16[528,128]{1,0:T(8,128)(2,1)S(1)}, s16[528,128]{1,0:T(8,128)(2,1)S(1)}, u32[]{:S(2)}, u32[]{:S(2)}) %collective-permute-start.12) | collective-permute-done | bytes 135200 | tf_op jit(solution)/shard_map/ppermute | solution.py:348
  70.3 0.0 collective-permute-done.13.refs_6_
  70.3 0.0 collective-permute-done.14.refs_7_
  70.3 0.0 collective-permute-done.8.refs_1_
  70.3 2.1 %collective-permute-done.9.refs_2_ = s16[528,128]{1,0:T(8,128)(2,1)S(1)} collective-permute-done((s16[528,128]{1,0:T(8,128)(2,1)S(1)}, s16[528,128]{1,0:T(8,128)(2,1)S(1)}, u32[]{:S(2)}, u32[]{:S(2)}) %collective-permute-start.9) | collective-permute-done | bytes 135200 | tf_op jit(solution)/shard_map/ppermute | solution.py:348
  72.4 2.1 %image.1 = bf16[512,1024]{1,0:T(8,128)(2,1)} custom-call(bf16[2,256,256]{2,1,0:T(8,128)(2,1)S(1)} %pad_maximum_fusion.2.table_ref, s16[528,128]{1,0:T(8,128)(2,1)S(1)} %get-tuple-element.29.refs_0_, s16[528,128]{1,0:T(8,128)(2,1)S(1)} %collective-permute-done.8.refs_1_, s16[528,128]{1,0:T(8,128)(2,1)S(1)} %collective-permute-done.9.refs_2_, ...), custom_call_target="tpu_custom_call" | custom-call | tf_op jit(solution)/shard_map/image/pallas_call | solution.py:390
  (20 shorter events, 0.2 us)
Async XLA Ops:
  0.0 1.2 %copy-start.2 = (bf16[2,32,8,1024]{3,2,1,0:T(8,128)(2,1)S(1)}, bf16[2,32,8,1024]{3,2,1,0:T(8,128)(2,1)}, u32[]{:S(2)}) copy-start(bf16[2,32,8,1024]{3,2,1,0:T(8,128)(2,1)} %param.4) | copy-start | bytes 3145732
  1.2 0.9 %copy-start.3 = (bf16[2,256,256]{2,1,0:T(8,128)(2,1)S(1)}, bf16[2,256,256]{2,1,0:T(8,128)(2,1)}, u32[]{:S(2)}) copy-start(bf16[2,256,256]{2,1,0:T(8,128)(2,1)} %constant.294.clone.table_ref) | copy-start | bytes 786436
  3.4 19.3 %collective-permute-start = (s16[528,128]{1,0:T(8,128)(2,1)S(1)}, s16[528,128]{1,0:T(8,128)(2,1)S(1)}, u32[]{:S(2)}, u32[]{:S(2)}) collective-permute-start(s16[528,128]{1,0:T(8,128)(2,1)S(1)} %get-tuple-element.22), channel_id=1, source_target_pairs={{0,2},{2,0},{4,6},{6,4},{8,10},{10,8},{12,14},{14,12},{1,3},{3,1},... | collective-permute-start | bytes 405512 | tf_op jit(solution)/shard_map/ppermute | solution.py:348
  6.4 20.0 %collective-permute-start.1 = (s16[528,128]{1,0:T(8,128)(2,1)S(1)}, s16[528,128]{1,0:T(8,128)(2,1)S(1)}, u32[]{:S(2)}, u32[]{:S(2)}) collective-permute-start(s16[528,128]{1,0:T(8,128)(2,1)S(1)} %get-tuple-element.23), channel_id=1, source_target_pairs={{0,4},{2,6},{4,0},{6,2},{8,12},{10,14},{12,8},{14,10},{1,5},{3,7},... | collective-permute-start | bytes 405512 | tf_op jit(solution)/shard_map/ppermute | solution.py:348
  8.0 19.8 %collective-permute-start.2 = (s16[528,128]{1,0:T(8,128)(2,1)S(1)}, s16[528,128]{1,0:T(8,128)(2,1)S(1)}, u32[]{:S(2)}, u32[]{:S(2)}) collective-permute-start(s16[528,128]{1,0:T(8,128)(2,1)S(1)} %get-tuple-element.24), channel_id=1, source_target_pairs={{0,6},{2,4},{4,2},{6,0},{8,14},{10,12},{12,10},{14,8},{1,7},{3,5},... | collective-permute-start | bytes 405512 | tf_op jit(solution)/shard_map/ppermute | solution.py:348
  8.0 19.8 %collective-permute-start.3 = (s16[528,128]{1,0:T(8,128)(2,1)S(1)}, s16[528,128]{1,0:T(8,128)(2,1)S(1)}, u32[]{:S(2)}, u32[]{:S(2)}) collective-permute-start(s16[528,128]{1,0:T(8,128)(2,1)S(1)} %get-tuple-element.25), channel_id=1, source_target_pairs={{0,8},{2,10},{4,12},{6,14},{8,0},{10,2},{12,4},{14,6},{1,9},{3,11}... | collective-permute-start | bytes 405512 | tf_op jit(solution)/shard_map/ppermute | solution.py:348
  11.0 16.8 %collective-permute-start.4 = (s16[528,128]{1,0:T(8,128)(2,1)S(1)}, s16[528,128]{1,0:T(8,128)(2,1)S(1)}, u32[]{:S(2)}, u32[]{:S(2)}) collective-permute-start(s16[528,128]{1,0:T(8,128)(2,1)S(1)} %get-tuple-element.26), channel_id=1, source_target_pairs={{0,10},{2,8},{4,14},{6,12},{8,2},{10,0},{12,6},{14,4},{1,11},{3,9}... | collective-permute-start | bytes 405512 | tf_op jit(solution)/shard_map/ppermute | solution.py:348
  22.7 12.2 %copy-start.4 = (s32[4,16]{1,0:T(4,128)S(1)}, s32[4,16]{1,0:T(4,128)}, u32[]{:S(2)}) copy-start(s32[4,16]{1,0:T(4,128)} %param.6) | copy-start | bytes 772
  22.7 7.7 %collective-permute-start.5 = (s16[528,128]{1,0:T(8,128)(2,1)S(1)}, s16[528,128]{1,0:T(8,128)(2,1)S(1)}, u32[]{:S(2)}, u32[]{:S(2)}) collective-permute-start(s16[528,128]{1,0:T(8,128)(2,1)S(1)} %get-tuple-element.27), channel_id=1, source_target_pairs={{0,12},{2,14},{4,8},{6,10},{8,4},{10,6},{12,0},{14,2},{1,13},{3,15... | collective-permute-start | bytes 405512 | tf_op jit(solution)/shard_map/ppermute | solution.py:348
  26.4 7.8 %collective-permute-start.6 = (s16[528,128]{1,0:T(8,128)(2,1)S(1)}, s16[528,128]{1,0:T(8,128)(2,1)S(1)}, u32[]{:S(2)}, u32[]{:S(2)}) collective-permute-start(s16[528,128]{1,0:T(8,128)(2,1)S(1)} %get-tuple-element.28), channel_id=1, source_target_pairs={{0,14},{2,12},{4,10},{6,8},{8,6},{10,4},{12,2},{14,0},{1,15},{3,13... | collective-permute-start | bytes 405512 | tf_op jit(solution)/shard_map/ppermute | solution.py:348
  34.8 3.3 %collective-permute-start.7 = (bf16[2,512,128]{2,1,0:T(8,128)(2,1)S(1)}, bf16[2,512,128]{2,1,0:T(8,128)(2,1)S(1)}, u32[]{:S(2)}, u32[]{:S(2)}) collective-permute-start(bf16[2,512,128]{2,1,0:T(8,128)(2,1)S(1)} %edge.1), channel_id=1, source_target_pairs={{0,1},{1,0},{2,3},{3,2},{4,5},{5,4},{6,7},{7,6},{8,9},{9,8},{10,11... | collective-permute-start | bytes 786440 | tf_op jit(solution)/shard_map/ppermute | solution.py:369
  36.2 3.4 %copy-start.1 = (bf16[4,8,256,128]{3,2,1,0:T(8,128)(2,1)S(1)}, bf16[4,8,256,128]{3,2,1,0:T(8,128)(2,1)}, u32[]{:S(2)}) copy-start(bf16[4,8,256,128]{3,2,1,0:T(8,128)(2,1)} %weights_ref.1) | copy-start | bytes 6291460
  38.2 1.4 %copy-start = (bf16[9,2,512,128]{3,2,1,0:T(8,128)(2,1)}, bf16[9,2,512,128]{3,2,1,0:T(8,128)(2,1)S(1)}, u32[]{:S(2)}) copy-start(bf16[9,2,512,128]{3,2,1,0:T(8,128)(2,1)S(1)} %bitcast_dynamic-update-slice_fusion.spectrum_ref) | copy-start | bytes 7077892
  44.7 11.5 %collective-permute-start.10 = (s16[528,128]{1,0:T(8,128)(2,1)S(1)}, s16[528,128]{1,0:T(8,128)(2,1)S(1)}, u32[]{:S(2)}, u32[]{:S(2)}) collective-permute-start(s16[528,128]{1,0:T(8,128)(2,1)S(1)} %get-tuple-element.32), channel_id=1, source_target_pairs={{0,6},{2,4},{4,2},{6,0},{8,14},{10,12},{12,10},{14,8},{1,7},{3,5},... | collective-permute-start | bytes 405512 | tf_op jit(solution)/shard_map/ppermute | solution.py:348
  48.4 19.0 %collective-permute-start.11 = (s16[528,128]{1,0:T(8,128)(2,1)S(1)}, s16[528,128]{1,0:T(8,128)(2,1)S(1)}, u32[]{:S(2)}, u32[]{:S(2)}) collective-permute-start(s16[528,128]{1,0:T(8,128)(2,1)S(1)} %get-tuple-element.33), channel_id=1, source_target_pairs={{0,8},{2,10},{4,12},{6,14},{8,0},{10,2},{12,4},{14,6},{1,9},{3,11}... | collective-permute-start | bytes 405512 | tf_op jit(solution)/shard_map/ppermute | solution.py:348
  48.6 21.7 %collective-permute-start.12 = (s16[528,128]{1,0:T(8,128)(2,1)S(1)}, s16[528,128]{1,0:T(8,128)(2,1)S(1)}, u32[]{:S(2)}, u32[]{:S(2)}) collective-permute-start(s16[528,128]{1,0:T(8,128)(2,1)S(1)} %get-tuple-element.34), channel_id=1, source_target_pairs={{0,10},{2,8},{4,14},{6,12},{8,2},{10,0},{12,6},{14,4},{1,11},{3,9}... | collective-permute-start | bytes 405512 | tf_op jit(solution)/shard_map/ppermute | solution.py:348
  51.4 18.9 %collective-permute-start.13 = (s16[528,128]{1,0:T(8,128)(2,1)S(1)}, s16[528,128]{1,0:T(8,128)(2,1)S(1)}, u32[]{:S(2)}, u32[]{:S(2)}) collective-permute-start(s16[528,128]{1,0:T(8,128)(2,1)S(1)} %get-tuple-element.35), channel_id=1, source_target_pairs={{0,12},{2,14},{4,8},{6,10},{8,4},{10,6},{12,0},{14,2},{1,13},{3,15... | collective-permute-start | bytes 405512 | tf_op jit(solution)/shard_map/ppermute | solution.py:348
  53.9 16.4 %collective-permute-start.14 = (s16[528,128]{1,0:T(8,128)(2,1)S(1)}, s16[528,128]{1,0:T(8,128)(2,1)S(1)}, u32[]{:S(2)}, u32[]{:S(2)}) collective-permute-start(s16[528,128]{1,0:T(8,128)(2,1)S(1)} %get-tuple-element.36), channel_id=1, source_target_pairs={{0,14},{2,12},{4,10},{6,8},{8,6},{10,4},{12,2},{14,0},{1,15},{3,13... | collective-permute-start | bytes 405512 | tf_op jit(solution)/shard_map/ppermute | solution.py:348
  56.1 14.1 %collective-permute-start.8 = (s16[528,128]{1,0:T(8,128)(2,1)S(1)}, s16[528,128]{1,0:T(8,128)(2,1)S(1)}, u32[]{:S(2)}, u32[]{:S(2)}) collective-permute-start(s16[528,128]{1,0:T(8,128)(2,1)S(1)} %get-tuple-element.30), channel_id=1, source_target_pairs={{0,2},{2,0},{4,6},{6,4},{8,10},{10,8},{12,14},{14,12},{1,3},{3,1},... | collective-permute-start | bytes 405512 | tf_op jit(solution)/shard_map/ppermute | solution.py:348
  67.4 5.0 %collective-permute-start.9 = (s16[528,128]{1,0:T(8,128)(2,1)S(1)}, s16[528,128]{1,0:T(8,128)(2,1)S(1)}, u32[]{:S(2)}, u32[]{:S(2)}) collective-permute-start(s16[528,128]{1,0:T(8,128)(2,1)S(1)} %get-tuple-element.31), channel_id=1, source_target_pairs={{0,4},{2,6},{4,0},{6,2},{8,12},{10,14},{12,8},{14,10},{1,5},{3,7},... | collective-permute-start | bytes 405512 | tf_op jit(solution)/shard_map/ppermute | solution.py:348

commit v2 on v0

--- a/solution.py
+++ b/solution.py
@@ -1,12 +1,21 @@
+import functools
 import math
 
 import jax
 import jax.numpy as jnp
+import numpy as np
 from jax import lax
+from jax.experimental import pallas as pl
+from jax.experimental.pallas import tpu as pltpu
 from jax.sharding import PartitionSpec as P
 
 LINES_DEV = 256
 SLABS = 4
+TILE = 128
+BF16 = jnp.bfloat16
+F32 = jnp.float32
+CODE_STEPS = 256.0
+FULL = 32767.0
 
 
 def with_halo(cells, sides, width):
@@ -61,7 +70,7 @@
     return jnp.concatenate(pieces, 1)
 
 
-def body(raw, stolt_weights, band_start):
+def generic_body(raw, stolt_weights, band_start):
     groups = lax.axis_size("az")
     az_index = lax.axis_index("az")
     rg_index = lax.axis_index("rg")
@@ -111,6 +120,345 @@
     return focused.astype(jnp.bfloat16)
 
 
+NDEV = 8
+MLOC = LINES_DEV // NDEV
+ROWS = 2 * MLOC
+HALF = 16
+TAIL = 8
+TILES = 8
+LINES = 2 * LINES_DEV
+SIDE = LINES_DEV // 2
+ORDER = (1, 2, 4, 5, 6, 7, 3, 0)
+PLACE = tuple(ORDER.index(i) for i in range(NDEV))
+VMEM_LIMIT = 20 * 1024 * 1024
+
+
+def split2(x):
+    hi = x.astype(BF16)
+    lo = (x - hi.astype(F32)).astype(BF16)
+    return hi, lo
+
+
+def mm(a, b):
+    return jnp.dot(a, b, preferred_element_type=F32)
+
+
+def product3(table, pair):
+    return mm(table[0], pair[0]) + mm(table[0], pair[1]) + mm(table[1], pair[0])
+
+
+def table_pair(table):
+    hi = table.astype(jnp.bfloat16)
+    return np.stack([hi, (table - hi.astype(np.float32)).astype(jnp.bfloat16)])
+
+
+def short_table(upper):
+    k1, co, mo = np.meshgrid(np.arange(8), np.arange(2), np.arange(HALF), indexing="ij")
+    ci, mi, p = np.meshgrid(np.arange(2), np.arange(HALF), np.arange(8), indexing="ij")
+    k1, co, mo = (v.reshape(-1, 1) for v in (k1, co, mo))
+    ci, mi, p = (v.reshape(1, -1) for v in (ci, mi, p))
+    turn = (k1 * (2 * p + upper) + 4 * (co - ci)) % 16
+    unit = np.cos(2 * np.pi * np.arange(16) / 16)
+    unit[[4, 12]] = 0.0
+    return np.where(mo == mi, unit[turn], 0.0).astype(np.float32)
+
+
+def long_base():
+    k2 = np.arange(LINES_DEV).reshape(-1, 2).T.reshape(1, -1)
+    angle = 2 * np.pi * (np.arange(SIDE).reshape(-1, 1) * k2 % LINES_DEV) / LINES_DEV
+    return np.stack([np.cos(angle), np.sin(angle)]).astype(np.float32)
+
+
+def rows_at(index, size):
+    return pl.ds(pl.multiple_of(index * size, size), size)
+
+
+def tiles_of(ref):
+    return (ref.shape[-2] - TAIL) // ROWS
+
+
+def store_coded(out_ref, pieces):
+    tiles = tiles_of(out_ref)
+    peak = None
+    for _, value in pieces:
+        top = jnp.max(jnp.abs(value), axis=0, keepdims=True)
+        peak = top if peak is None else jnp.maximum(peak, top)
+    code = jnp.ceil(jnp.log2(jnp.maximum(peak, 1e-30) * (1.0 / FULL)) * CODE_STEPS + 0.01)
+    inverse = jnp.exp2(code * (-1.0 / CODE_STEPS))
+    for row, value in pieces:
+        coded = jnp.round(value * inverse).astype(jnp.int32).astype(jnp.int16)
+        for tile in range(tiles):
+            at = tile * ROWS + row
+            out_ref[at : at + value.shape[0], :] = coded[:, tile * TILE : (tile + 1) * TILE]
+    which = lax.broadcasted_iota(jnp.int32, (TAIL, TILE), 0)
+    scales = jnp.zeros((TAIL, TILE), F32)
+    for tile in range(tiles):
+        scales = jnp.where(which == tile, code[:, tile * TILE : (tile + 1) * TILE], scales)
+    out_ref[tiles * ROWS : tiles * ROWS + TAIL, :] = scales.astype(jnp.int32).astype(jnp.int16)
+
+
+def load_scales(ref):
+    at = tiles_of(ref) * ROWS
+    code = ref[at : at + TAIL, :].astype(jnp.int32).astype(F32)
+    return jnp.exp2(code * (1.0 / CODE_STEPS))
+
+
+def load_columns(ref, scales, tiles):
+    parts = []
+    for t in tiles:
+        value = ref[t * ROWS : (t + 1) * ROWS, :].astype(jnp.int32).astype(F32)
+        parts.append(value * scales[t : t + 1, :])
+    return jnp.concatenate(parts, 1)
+
+
+def tile_pairs(tiles):
+    return [(t, t + 1) for t in range(0, tiles, 2)]
+
+
+def in_order(refs):
+    return [refs[at] for at in PLACE]
+
+
+def sign_of(me):
+    return (1 - 2 * (me // 4)).astype(F32)
+
+
+def spread_kernel(me_ref, x_ref, table_ref, *out_refs):
+    me = me_ref[0]
+    hi, lo = [
+        jnp.concatenate([table_ref[me // 4, part, rows_at(me ^ i, 32), :] for i in range(NDEV)], 0)
+        for part in range(2)
+    ]
+    halves = []
+    for h in range(2):
+        at = h * 128
+        x = jnp.concatenate([x_ref[at : at + 128, :], x_ref[256 + at : 256 + at + 128, :]], 0)
+        halves.append(mm(hi, x) + mm(lo, x))
+    for n, out_ref in enumerate(out_refs):
+        pieces = []
+        for c in range(2):
+            for h in range(2):
+                at = n * 32 + c * HALF
+                pieces.append((c * MLOC + h * HALF, halves[h][at : at + HALF, :]))
+        store_coded(out_ref, pieces)
+
+
+def tables_kernel(me_ref, base_ref, short_ref, forward_ref, inverse_ref, image_ref):
+    me = me_ref[0]
+    step = 2.0 * math.pi / (NDEV * LINES_DEV)
+    blocks = []
+    for i in range(4):
+        slot = (me & 3) ^ i
+        line = lax.broadcasted_iota(jnp.int32, (MLOC, TILE), 0) + slot * MLOC
+        angle = (line * me).astype(F32) * step
+        turn_cos, turn_sin = jnp.cos(angle) * (1.0 / 64.0), jnp.sin(angle) * (1.0 / 64.0)
+        cosine, sine = [base_ref[n, rows_at(slot, MLOC), :] for n in range(2)]
+        turn_cos = jnp.concatenate([turn_cos, turn_cos], 1)
+        turn_sin = jnp.concatenate([turn_sin, turn_sin], 1)
+        blocks.append((cosine * turn_cos - sine * turn_sin, sine * turn_cos + cosine * turn_sin))
+    whole = [jnp.concatenate([b[n] for b in blocks], 0) for n in range(2)]
+    for parity in range(2):
+        co, si = [w[:, parity * SIDE : (parity + 1) * SIDE] for w in whole]
+        inverse = jnp.concatenate([jnp.concatenate([co, -si], 1), jnp.concatenate([si, co], 1)], 0)
+        ct, st = co.T * 2.0, si.T * 2.0
+        forward = jnp.concatenate([jnp.concatenate([ct, st], 1), jnp.concatenate([-st, ct], 1)], 0)
+        for ref, value in ((inverse_ref, inverse), (forward_ref, forward)):
+            ref[0, parity], ref[1, parity] = split2(value)
+    for part in range(2):
+        rows = [short_ref[me // 4, part, rows_at(me ^ i, 32), :] for i in range(NDEV)]
+        image_ref[part] = jnp.concatenate(rows, 0).astype(F32).T.astype(BF16)
+
+
+def forward_kernel(me_ref, rg_ref, table_ref, *refs):
+    in_refs, (out_ref, edge_ref) = in_order(refs[:NDEV]), refs[NDEV:]
+    sign = sign_of(me_ref[0])
+    scales = [load_scales(ref) for ref in in_refs]
+    for tiles in tile_pairs(TILES):
+        values = [load_columns(ref, scale, tiles) for ref, scale in zip(in_refs, scales)]
+        sums = [values[i] + values[i + 4] for i in range(4)]
+        gaps = [(values[i] - values[i + 4]) * sign for i in range(4)]
+        for parity, lines in enumerate((sums, gaps)):
+            lines = jnp.concatenate([v[:MLOC] for v in lines] + [v[MLOC:] for v in lines], 0)
+            result = product3((table_ref[0, parity], table_ref[1, parity]), split2(lines))
+            for at, t in enumerate(tiles):
+                for part, half in enumerate(split2(result[:, at * TILE : (at + 1) * TILE])):
+                    out_ref[t, part, parity * 256 : (parity + 1) * 256, :] = half
+    edge_ref[...] = out_ref[(1 - rg_ref[0]) * (TILES - 1)]
+
+
+def remap_block(starts_ref, weights_ref, rg, j, tile_at):
+    for g in range(SLABS):
+        at = starts_ref[g, rg * TILES + j] - rg * TILES
+        window = []
+        for part in range(2):
+            for parity in range(2):
+                for c in range(2):
+                    row = parity * 256 + c * 128 + g * 32
+                    rows = slice(row, row + 32)
+                    window.append(jnp.concatenate([tile_at(at + n, part, rows) for n in range(2)], 1))
+        both = mm(jnp.concatenate(window, 0), weights_ref[g, j])
+        yield g, split2(both[:128] + both[128:])
+
+
+def focus_rows(g):
+    return [(parity, c * 128 + g * 32) for parity in range(2) for c in range(2)]
+
+
+def inner_kernel(rg_ref, starts_ref, spectrum_ref, weights_ref, focus_ref):
+    rg = rg_ref[0]
+    for n in range(TILES - 1):
+        j = n + rg
+        for g, pair in remap_block(
+            starts_ref, weights_ref, rg, j, lambda t, part, rows: spectrum_ref[t, part, rows, :]
+        ):
+            for part, half in enumerate(pair):
+                for at, (parity, row) in enumerate(focus_rows(g)):
+                    focus_ref[part, parity, n, row : row + 32, :] = half[at * 32 : (at + 1) * 32]
+
+
+def outer_kernel(me_ref, rg_ref, starts_ref, spectrum_ref, halo_ref, weights_ref, table_ref, focus_ref, *refs):
+    out_refs, window_ref = refs[:NDEV], refs[NDEV]
+    me, rg = me_ref[0], rg_ref[0]
+    first = 6 - 7 * rg
+    window_ref[2 - 2 * rg] = halo_ref[...]
+    for n in range(2):
+        window_ref[rg + n] = spectrum_ref[(1 - rg) * 6 + n]
+    face = [[[None] * 8 for _ in range(2)] for _ in range(2)]
+    for g, pair in remap_block(
+        starts_ref,
+        weights_ref,
+        rg,
+        (1 - rg) * (TILES - 1),
+        lambda t, part, rows: window_ref[t - first, part, rows, :],
+    ):
+        for part, half in enumerate(pair):
+            for at, (parity, row) in enumerate(focus_rows(g)):
+                face[part][parity][row // 32] = half[at * 32 : (at + 1) * 32]
+    results = []
+    for parity in range(2):
+        pair = []
+        for part in range(2):
+            block = jnp.concatenate(face[part][parity], 0)
+            inner = [focus_ref[part, parity, n] for n in range(TILES - 1)]
+            pair.append(
+                jnp.concatenate(
+                    [jnp.where(rg == 1, block, inner[0])]
+                    + [jnp.where(rg == 1, inner[n - 1], inner[n]) for n in range(1, TILES - 1)]
+                    + [jnp.where(rg == 1, inner[-1], block)],
+                    1,
+                )
+            )
+        results.append(product3((table_ref[0, parity], table_ref[1, parity]), pair))
+    even, odd = results[0], results[1] * sign_of(me)
+    for i, out_ref in enumerate(out_refs):
+        lines = even + odd if i < 4 else even - odd
+        pieces = []
+        for c in range(2):
+            at = c * SIDE + (i % 4) * MLOC
+            pieces.append((c * MLOC, lines[at : at + MLOC, :]))
+        store_coded(out_ref, pieces)
+
+
+def image_kernel(table_ref, *refs):
+    in_refs, out_ref = in_order(refs[:NDEV]), refs[NDEV]
+    scales = [load_scales(ref) for ref in in_refs]
+    for tiles in tile_pairs(TILES):
+        values = [load_columns(ref, scale, tiles) for ref, scale in zip(in_refs, scales)]
+        for h in range(2):
+            x = jnp.concatenate(
+                [v[c * MLOC + h * HALF : c * MLOC + (h + 1) * HALF] for v in values for c in range(2)], 0
+            )
+            result = product3(table_ref, split2(x)).astype(BF16)
+            for c in range(2):
+                at = c * 256 + h * 128
+                columns = slice(tiles[0] * TILE, (tiles[0] + 2) * TILE)
+                out_ref[at : at + 128, columns] = result[c * 128 : (c + 1) * 128]
+
+
+def vmem_call(kernel, name, out_shape, smem=0, vmem=0, scratch=()):
+    return pl.pallas_call(
+        kernel,
+        name=name,
+        out_shape=out_shape,
+        in_specs=[pl.BlockSpec(memory_space=pltpu.SMEM)] * smem
+        + [pl.BlockSpec(memory_space=pltpu.VMEM)] * vmem,
+        out_specs=jax.tree.map(lambda _: pl.BlockSpec(memory_space=pltpu.VMEM), out_shape),
+        scratch_shapes=scratch,
+        compiler_params=pltpu.CompilerParams(vmem_limit_bytes=VMEM_LIMIT),
+    )
+
+
+def after(value, *others):
+    return lax.optimization_barrier((value, *others))[0]
+
+
+def exchange(messages):
+    return [
+        lax.ppermute(messages[i], "az", [(d, d ^ i) for d in range(NDEV)]) if i else messages[0]
+        for i in ORDER
+    ]
+
+
+def fast_body(raw, stolt_weights, band_start):
+    me = lax.axis_index("az").astype(jnp.int32)[None]
+    rg = lax.axis_index("rg").astype(jnp.int32)[None]
+    bins = raw.shape[3]
+    message = jax.ShapeDtypeStruct((TILES * ROWS + TAIL, TILE), jnp.int16)
+    short = jnp.asarray(np.stack([table_pair(short_table(upper)) for upper in range(2)]))
+    long_shape = jax.ShapeDtypeStruct((2, 2, LINES_DEV, LINES_DEV), BF16)
+
+    sent = vmem_call(spread_kernel, "spread", [message] * NDEV, smem=1, vmem=2)(
+        me, raw.reshape(LINES, bins), short
+    )
+    got = exchange(sent)
+    forward_table, inverse_table, image_table = vmem_call(
+        tables_kernel,
+        "tables",
+        [long_shape, long_shape, jax.ShapeDtypeStruct((2, 256, 256), BF16)],
+        smem=1,
+        vmem=2,
+    )(after(me, *sent), jnp.asarray(long_base()), short)
+
+    spectrum, edge = vmem_call(
+        forward_kernel,
+        "forward",
+        [jax.ShapeDtypeStruct((TILES, 2, LINES, TILE), BF16), jax.ShapeDtypeStruct((2, LINES, TILE), BF16)],
+        smem=2,
+        vmem=1 + NDEV,
+    )(me, rg, forward_table, *got)
+    halo = lax.ppermute(edge, "rg", [(0, 1), (1, 0)])
+    focus = vmem_call(
+        inner_kernel,
+        "inner",
+        jax.ShapeDtypeStruct((2, 2, TILES - 1, LINES_DEV, TILE), BF16),
+        smem=2,
+        vmem=2,
+    )(rg, band_start, spectrum, stolt_weights)
+    back = vmem_call(
+        outer_kernel,
+        "outer",
+        [message] * NDEV,
+        smem=3,
+        vmem=5,
+        scratch=[pltpu.VMEM((3, 2, LINES, TILE), BF16)],
+    )(me, rg, band_start, spectrum, halo, stolt_weights, inverse_table, focus)
+    lines = exchange(back)
+    image = vmem_call(image_kernel, "image", jax.ShapeDtypeStruct((LINES, bins), BF16), vmem=1 + NDEV)(
+        image_table, *lines
+    )
+    return image.reshape(2, MLOC, NDEV, bins)
+
+
+def body(raw, stolt_weights, band_start):
+    fast = (
+        lax.axis_size("az") == NDEV
+        and lax.axis_size("rg") == 2
+        and raw.shape[1:3] == (MLOC, NDEV)
+        and raw.shape[3] == TILES * TILE
+    )
+    return (fast_body if fast else generic_body)(raw, stolt_weights, band_start)
+
+
 def solution(mesh):
     placed = (P(None, ("frames", "az"), None, "rg"), P(None, "rg", None, None), P())
     return jax.shard_map(

time: 165 us -> 70.4 us (0.43)
  the two profiles are of different devices: /device:TPU:0 before, /device:TPU:16 now
where the time goes in v2:
time: 70.4 us; the launch traced here: 70.2 us
  waiting for transfers between devices  38.4 us (55%)
  starting transfers between devices  17.6 us (25%)
  Pallas kernels  9.69 us (14%)
  local copies, waits for them, and re-layouts  4.41 us (6%)
    ppermute x14, waiting for transfers between devices, exchange(): lax.ppermute(messages[i], 'az', [(d, d ^ i) for d in range(NDEV)])  38.4 us
    ppermute x14, starting transfers between devices, exchange(): lax.ppermute(messages[i], 'az', [(d, d ^ i) for d in range(NDEV)])  17.5 us
    unnamed x12, local copies, waits for them, and re-layouts  4.41 us
    pallas_call x1, Pallas kernels, fast_body(): vmem_call(outer_kernel, 'outer', [message] * NDEV, smem=3, vmem=5, scratc...  2.35 us
    pallas_call x1, Pallas kernels, fast_body(): vmem_call(image_kernel, 'image', jax.ShapeDtypeStruct((LINES, bins), BF16...  2.07 us
    pallas_call x1, Pallas kernels, fast_body(): vmem_call(spread_kernel, 'spread', [message] * NDEV, smem=1, vmem=2)  1.86 us
    pallas_call x1, Pallas kernels, fast_body(): vmem_call(inner_kernel, 'inner', jax.ShapeDtypeStruct((2, 2, TILES - 1, L...  1.68 us
  transfers between devices with their start and end apart: 15, of which 10 were waited for; matrix products, arithmetic and copies ran while one was open for 0% of the time, Pallas kernels for 3%

profile of v2, /device:TPU:16, one launch (start us, length us, event | category | flops | bytes accessed | tf_op | source)
XLA Modules:
  0.0 70.2 jit_solution(5995533544719841993)
XLA Ops:
  0.0 0.0 copy-start
  0.0 0.0 copy-start.1
  0.0 1.2 %copy-done.1 = bf16[2,2,256,256]{3,2,1,0:T(8,128)(2,1)S(1)} copy-done((bf16[2,2,256,256]{3,2,1,0:T(8,128)(2,1)S(1)}, bf16[2,2,256,256]{3,2,1,0:T(8,128)(2,1)}, u32[]{:S(2)}) %copy-start.1) | copy-done | bytes 524312
  1.2 0.0 copy-start.3
  1.2 1.2 %copy-done.3 = bf16[2,32,8,1024]{3,2,1,0:T(8,128)(2,1)S(1)} copy-done((bf16[2,32,8,1024]{3,2,1,0:T(8,128)(2,1)S(1)}, bf16[2,32,8,1024]{3,2,1,0:T(8,128)(2,1)}, u32[]{:S(2)}) %copy-start.3) | copy-done | bytes 1048600
  2.4 1.9 %spread.1 = (s16[520,128]{1,0:T(8,128)(2,1)S(1)}, s16[520,128]{1,0:T(8,128)(2,1)S(1)}, s16[520,128]{1,0:T(8,128)(2,1)S(1)}, s16[520,128]{1,0:T(8,128)(2,1)}, s16...) custom-call(s32[1]{0:T(128)} %bitcast.me_ref, ...), custom_call_target="tpu_custom_call" | custom-call | tf_op jit(solution)/shard_map/spread/pallas_call | solution.py:410
  4.3 1.5 %collective-permute-start = (s16[520,128]{1,0:T(8,128)(2,1)S(1)}, s16[520,128]{1,0:T(8,128)(2,1)S(1)}, u32[]{:S(2)}, u32[]{:S(2)}) collective-permute-start(s16[520,128]{1,0:T(8,128)(2,1)S(1)} %get-tuple-element.28), channel_id=1, source_target_pairs={{0,2},{2,0},{4,6},{6,4},{8,10},{10,8},{12,14},{14,12},{1,3},{3,1},... | collective-permute-start | bytes 399368 | tf_op jit(solution)/shard_map/ppermute | solution.py:397
  5.8 1.6 %collective-permute-start.1 = (s16[520,128]{1,0:T(8,128)(2,1)S(1)}, s16[520,128]{1,0:T(8,128)(2,1)S(1)}, u32[]{:S(2)}, u32[]{:S(2)}) collective-permute-start(s16[520,128]{1,0:T(8,128)(2,1)S(1)} %get-tuple-element.29), channel_id=1, source_target_pairs={{0,4},{2,6},{4,0},{6,2},{8,12},{10,14},{12,8},{14,10},{1,5},{3,7},... | collective-permute-start | bytes 399368 | tf_op jit(solution)/shard_map/ppermute | solution.py:397
  7.3 0.4 collective-permute-start.6
  7.8 0.0 collective-permute-start.2
  7.8 3.8 %collective-permute-start.3 = (s16[520,128]{1,0:T(8,128)(2,1)}, s16[520,128]{1,0:T(8,128)(2,1)S(1)}, u32[]{:S(2)}, u32[]{:S(2)}) collective-permute-start(s16[520,128]{1,0:T(8,128)(2,1)} %get-tuple-element.32), channel_id=1, source_target_pairs={{0,10},{2,8},{4,14},{6,12},{8,2},{10,0},{12,6},{14,4},{1,11},{3,9}... | collective-permute-start | bytes 399368 | tf_op jit(solution)/shard_map/ppermute | solution.py:397
  11.6 0.0 collective-permute-done.refs_0_
  11.6 0.5 collective-permute-start.4
  12.1 2.2 %collective-permute-done.1.refs_1_ = s16[520,128]{1,0:T(8,128)(2,1)S(1)} collective-permute-done((s16[520,128]{1,0:T(8,128)(2,1)S(1)}, s16[520,128]{1,0:T(8,128)(2,1)S(1)}, u32[]{:S(2)}, u32[]{:S(2)}) %collective-permute-start.1) | collective-permute-done | bytes 133152 | tf_op jit(solution)/shard_map/ppermute | solution.py:397
  14.3 0.0 collective-permute-start.5
  14.3 0.0 copy-start.2
  14.3 1.0 %copy-done.2 = bf16[2,2,256,256]{3,2,1,0:T(8,128)(2,1)S(1)} copy-done((bf16[2,2,256,256]{3,2,1,0:T(8,128)(2,1)S(1)}, bf16[2,2,256,256]{3,2,1,0:T(8,128)(2,1)}, u32[]{:S(2)}) %copy-start.2) | copy-done | bytes 524312
  15.4 0.0 copy-start.4
  15.4 0.9 %copy-done.4 = f32[2,128,256]{2,1,0:T(8,128)S(1)} copy-done((f32[2,128,256]{2,1,0:T(8,128)S(1)}, f32[2,128,256]{2,1,0:T(8,128)}, u32[]{:S(2)}) %copy-start.4) | copy-done | bytes 262168
  16.3 0.0 copy-start.5
  16.3 0.5 tables.1
  16.8 0.0 collective-permute-done.6.refs_6_
  16.8 1.1 %collective-permute-done.2.refs_2_ = s16[520,128]{1,0:T(8,128)(2,1)S(1)} collective-permute-done((s16[520,128]{1,0:T(8,128)(2,1)}, s16[520,128]{1,0:T(8,128)(2,1)S(1)}, u32[]{:S(2)}, u32[]{:S(2)}) %collective-permute-start.2) | collective-permute-done | bytes 133152 | tf_op jit(solution)/shard_map/ppermute | solution.py:397
  17.9 8.6 %collective-permute-done.3.refs_3_ = s16[520,128]{1,0:T(8,128)(2,1)S(1)} collective-permute-done((s16[520,128]{1,0:T(8,128)(2,1)}, s16[520,128]{1,0:T(8,128)(2,1)S(1)}, u32[]{:S(2)}, u32[]{:S(2)}) %collective-permute-start.3) | collective-permute-done | bytes 133152 | tf_op jit(solution)/shard_map/ppermute | solution.py:397
  26.5 5.5 %collective-permute-done.4.refs_4_ = s16[520,128]{1,0:T(8,128)(2,1)S(1)} collective-permute-done((s16[520,128]{1,0:T(8,128)(2,1)S(1)}, s16[520,128]{1,0:T(8,128)(2,1)S(1)}, u32[]{:S(2)}, u32[]{:S(2)}) %collective-permute-start.4) | collective-permute-done | bytes 133152 | tf_op jit(solution)/shard_map/ppermute | solution.py:397
  32.0 2.3 %collective-permute-done.5.refs_5_ = s16[520,128]{1,0:T(8,128)(2,1)S(1)} collective-permute-done((s16[520,128]{1,0:T(8,128)(2,1)S(1)}, s16[520,128]{1,0:T(8,128)(2,1)S(1)}, u32[]{:S(2)}, u32[]{:S(2)}) %collective-permute-start.5) | collective-permute-done | bytes 133152 | tf_op jit(solution)/shard_map/ppermute | solution.py:397
  34.3 1.2 %forward.1 = (bf16[8,2,512,128]{3,2,1,0:T(8,128)(2,1)S(1)}, bf16[2,512,128]{2,1,0:T(8,128)(2,1)S(1)}) custom-call(s32[1]{0:T(128)} %bitcast.me_ref, s32[1]{0:T(128)} %bitcast.2.rg_ref, bf16[2,2,256,256]{3,2,1,0:T(8,128)(2,1)S(1)} %get-tuple-element.37.table_ref, s16[520,128]{1,0:T(8,128)(2,1)S(1)} %collective-permute-done.refs_0_, ...), custom_call_target="tpu_custom_call" | custom-call | tf_op jit(solution)/shard_map/forward/pallas_call | solution.py:422
  35.6 0.1 collective-permute-start.7
  35.6 0.0 copy-done
  35.7 0.0 copy-done.5
  35.7 1.7 %inner.1.focus_ref = bf16[2,2,7,256,128]{4,3,2,1,0:T(8,128)(2,1)S(1)} custom-call(s32[1]{0:T(128)} %bitcast.2.rg_ref, s32[4,16]{1,0:T(4,128)S(1)} %copy-done.5, bf16[8,2,512,128]{3,2,1,0:T(8,128)(2,1)S(1)} %get-tuple-element.38.spectrum_ref, bf16[4,8,256,128]{3,2,1,0:T(8,128)(2,1)S(1)} %copy-done), custom_call_target="tpu_custom_call" | custom-call | tf_op jit(solution)/shard_map/inner/pallas_call | solution.py:430
  37.4 0.0 collective-permute-done.7.halo_ref
  37.4 2.4 %outer.1 = (s16[520,128]{1,0:T(8,128)(2,1)S(1)}, s16[520,128]{1,0:T(8,128)(2,1)S(1)}, s16[520,128]{1,0:T(8,128)(2,1)S(1)}, s16[520,128]{1,0:T(8,128)(2,1)S(1)}, ...) custom-call(s32[1]{0:T(128)} %bitcast.me_ref, ...), custom_call_target="tpu_custom_call" | custom-call | tf_op jit(solution)/shard_map/outer/pallas_call | solution.py:437
  39.7 0.6 collective-permute-start.8
  40.4 0.0 collective-permute-start.9
  40.4 1.1 %collective-permute-start.10 = (s16[520,128]{1,0:T(8,128)(2,1)S(1)}, s16[520,128]{1,0:T(8,128)(2,1)S(1)}, u32[]{:S(2)}, u32[]{:S(2)}) collective-permute-start(s16[520,128]{1,0:T(8,128)(2,1)S(1)} %get-tuple-element.43), channel_id=1, source_target_pairs={{0,8},{2,10},{4,12},{6,14},{8,0},{10,2},{12,4},{14,6},{1,9},{3,11}... | collective-permute-start | bytes 399368 | tf_op jit(solution)/shard_map/ppermute | solution.py:397
  41.5 2.7 %collective-permute-start.11 = (s16[520,128]{1,0:T(8,128)(2,1)S(1)}, s16[520,128]{1,0:T(8,128)(2,1)S(1)}, u32[]{:S(2)}, u32[]{:S(2)}) collective-permute-start(s16[520,128]{1,0:T(8,128)(2,1)S(1)} %get-tuple-element.44), channel_id=1, source_target_pairs={{0,10},{2,8},{4,14},{6,12},{8,2},{10,0},{12,6},{14,4},{1,11},{3,9}... | collective-permute-start | bytes 399368 | tf_op jit(solution)/shard_map/ppermute | solution.py:397
  44.2 0.6 collective-permute-start.12
  44.8 1.0 %collective-permute-done.8.refs_0_ = s16[520,128]{1,0:T(8,128)(2,1)S(1)} collective-permute-done((s16[520,128]{1,0:T(8,128)(2,1)S(1)}, s16[520,128]{1,0:T(8,128)(2,1)S(1)}, u32[]{:S(2)}, u32[]{:S(2)}) %collective-permute-start.8) | collective-permute-done | bytes 133152 | tf_op jit(solution)/shard_map/ppermute | solution.py:397
  45.7 0.5 collective-permute-start.13
  46.2 0.5 collective-permute-done.9.refs_1_
  46.8 4.2 %collective-permute-start.14 = (s16[520,128]{1,0:T(8,128)(2,1)S(1)}, s16[520,128]{1,0:T(8,128)(2,1)S(1)}, u32[]{:S(2)}, u32[]{:S(2)}) collective-permute-start(s16[520,128]{1,0:T(8,128)(2,1)S(1)} %get-tuple-element.47), channel_id=1, source_target_pairs={{0,6},{2,4},{4,2},{6,0},{8,14},{10,12},{12,10},{14,8},{1,7},{3,5},... | collective-permute-start | bytes 399368 | tf_op jit(solution)/shard_map/ppermute | solution.py:397
  50.9 0.0 collective-permute-done.10.refs_2_
  50.9 8.1 %collective-permute-done.11.refs_3_ = s16[520,128]{1,0:T(8,128)(2,1)S(1)} collective-permute-done((s16[520,128]{1,0:T(8,128)(2,1)S(1)}, s16[520,128]{1,0:T(8,128)(2,1)S(1)}, u32[]{:S(2)}, u32[]{:S(2)}) %collective-permute-start.11) | collective-permute-done | bytes 133152 | tf_op jit(solution)/shard_map/ppermute | solution.py:397
  59.1 5.8 %collective-permute-done.12.refs_4_ = s16[520,128]{1,0:T(8,128)(2,1)S(1)} collective-permute-done((s16[520,128]{1,0:T(8,128)(2,1)S(1)}, s16[520,128]{1,0:T(8,128)(2,1)S(1)}, u32[]{:S(2)}, u32[]{:S(2)}) %collective-permute-start.12) | collective-permute-done | bytes 133152 | tf_op jit(solution)/shard_map/ppermute | solution.py:397
  64.9 3.2 %collective-permute-done.13.refs_5_ = s16[520,128]{1,0:T(8,128)(2,1)S(1)} collective-permute-done((s16[520,128]{1,0:T(8,128)(2,1)S(1)}, s16[520,128]{1,0:T(8,128)(2,1)S(1)}, u32[]{:S(2)}, u32[]{:S(2)}) %collective-permute-start.13) | collective-permute-done | bytes 133152 | tf_op jit(solution)/shard_map/ppermute | solution.py:397
  68.1 0.0 collective-permute-done.14.refs_6_
  68.1 2.1 %image.1 = bf16[512,1024]{1,0:T(8,128)(2,1)} custom-call(bf16[2,256,256]{2,1,0:T(8,128)(2,1)S(1)} %get-tuple-element.36.table_ref, s16[520,128]{1,0:T(8,128)(2,1)S(1)} %collective-permute-done.8.refs_0_, s16[520,128]{1,0:T(8,128)(2,1)S(1)} %collective-permute-done.9.refs_1_, s16[520,128]{1,0:T(8,128)(2,1)S(1)} %collective-permute-done.10.refs_2_, ...), custom_call_target="tpu_custom_call" | custom-call | tf_op jit(solution)/shard_map/image/pallas_call | solution.py:446
Async XLA Ops:
  0.0 35.7 %copy-start = (bf16[4,8,256,128]{3,2,1,0:T(8,128)(2,1)S(1)}, bf16[4,8,256,128]{3,2,1,0:T(8,128)(2,1)}, u32[]{:S(2)}) copy-start(bf16[4,8,256,128]{3,2,1,0:T(8,128)(2,1)} %weights_ref.3) | copy-start | bytes 6291460
  0.0 1.2 %copy-start.1 = (bf16[2,2,256,256]{3,2,1,0:T(8,128)(2,1)S(1)}, bf16[2,2,256,256]{3,2,1,0:T(8,128)(2,1)}, u32[]{:S(2)}) copy-start(bf16[2,2,256,256]{3,2,1,0:T(8,128)(2,1)} %constant.12.clone.table_ref.short_ref) | copy-start | bytes 1572868
  1.2 1.2 %copy-start.3 = (bf16[2,32,8,1024]{3,2,1,0:T(8,128)(2,1)S(1)}, bf16[2,32,8,1024]{3,2,1,0:T(8,128)(2,1)}, u32[]{:S(2)}) copy-start(bf16[2,32,8,1024]{3,2,1,0:T(8,128)(2,1)} %param.5) | copy-start | bytes 3145732
  4.3 7.3 %collective-permute-start = (s16[520,128]{1,0:T(8,128)(2,1)S(1)}, s16[520,128]{1,0:T(8,128)(2,1)S(1)}, u32[]{:S(2)}, u32[]{:S(2)}) collective-permute-start(s16[520,128]{1,0:T(8,128)(2,1)S(1)} %get-tuple-element.28), channel_id=1, source_target_pairs={{0,2},{2,0},{4,6},{6,4},{8,10},{10,8},{12,14},{14,12},{1,3},{3,1},... | collective-permute-start | bytes 399368 | tf_op jit(solution)/shard_map/ppermute | solution.py:397
  5.8 8.5 %collective-permute-start.1 = (s16[520,128]{1,0:T(8,128)(2,1)S(1)}, s16[520,128]{1,0:T(8,128)(2,1)S(1)}, u32[]{:S(2)}, u32[]{:S(2)}) collective-permute-start(s16[520,128]{1,0:T(8,128)(2,1)S(1)} %get-tuple-element.29), channel_id=1, source_target_pairs={{0,4},{2,6},{4,0},{6,2},{8,12},{10,14},{12,8},{14,10},{1,5},{3,7},... | collective-permute-start | bytes 399368 | tf_op jit(solution)/shard_map/ppermute | solution.py:397
  7.3 9.5 %collective-permute-start.6 = (s16[520,128]{1,0:T(8,128)(2,1)}, s16[520,128]{1,0:T(8,128)(2,1)S(1)}, u32[]{:S(2)}, u32[]{:S(2)}) collective-permute-start(s16[520,128]{1,0:T(8,128)(2,1)} %get-tuple-element.30), channel_id=1, source_target_pairs={{0,6},{2,4},{4,2},{6,0},{8,14},{10,12},{12,10},{14,8},{1,7},{3,5},... | collective-permute-start | bytes 399368 | tf_op jit(solution)/shard_map/ppermute | solution.py:397
  7.8 10.2 %collective-permute-start.2 = (s16[520,128]{1,0:T(8,128)(2,1)}, s16[520,128]{1,0:T(8,128)(2,1)S(1)}, u32[]{:S(2)}, u32[]{:S(2)}) collective-permute-start(s16[520,128]{1,0:T(8,128)(2,1)} %get-tuple-element.31), channel_id=1, source_target_pairs={{0,8},{2,10},{4,12},{6,14},{8,0},{10,2},{12,4},{14,6},{1,9},{3,11}... | collective-permute-start | bytes 399368 | tf_op jit(solution)/shard_map/ppermute | solution.py:397
  7.8 18.7 %collective-permute-start.3 = (s16[520,128]{1,0:T(8,128)(2,1)}, s16[520,128]{1,0:T(8,128)(2,1)S(1)}, u32[]{:S(2)}, u32[]{:S(2)}) collective-permute-start(s16[520,128]{1,0:T(8,128)(2,1)} %get-tuple-element.32), channel_id=1, source_target_pairs={{0,10},{2,8},{4,14},{6,12},{8,2},{10,0},{12,6},{14,4},{1,11},{3,9}... | collective-permute-start | bytes 399368 | tf_op jit(solution)/shard_map/ppermute | solution.py:397
  11.6 20.4 %collective-permute-start.4 = (s16[520,128]{1,0:T(8,128)(2,1)S(1)}, s16[520,128]{1,0:T(8,128)(2,1)S(1)}, u32[]{:S(2)}, u32[]{:S(2)}) collective-permute-start(s16[520,128]{1,0:T(8,128)(2,1)S(1)} %get-tuple-element.33), channel_id=1, source_target_pairs={{0,12},{2,14},{4,8},{6,10},{8,4},{10,6},{12,0},{14,2},{1,13},{3,15... | collective-permute-start | bytes 399368 | tf_op jit(solution)/shard_map/ppermute | solution.py:397
  14.3 20.0 %collective-permute-start.5 = (s16[520,128]{1,0:T(8,128)(2,1)S(1)}, s16[520,128]{1,0:T(8,128)(2,1)S(1)}, u32[]{:S(2)}, u32[]{:S(2)}) collective-permute-start(s16[520,128]{1,0:T(8,128)(2,1)S(1)} %get-tuple-element.34), channel_id=1, source_target_pairs={{0,14},{2,12},{4,10},{6,8},{8,6},{10,4},{12,2},{14,0},{1,15},{3,13... | collective-permute-start | bytes 399368 | tf_op jit(solution)/shard_map/ppermute | solution.py:397
  14.3 1.0 %copy-start.2 = (bf16[2,2,256,256]{3,2,1,0:T(8,128)(2,1)S(1)}, bf16[2,2,256,256]{3,2,1,0:T(8,128)(2,1)}, u32[]{:S(2)}) copy-start(bf16[2,2,256,256]{3,2,1,0:T(8,128)(2,1)} %constant.12.clone.table_ref.short_ref) | copy-start | bytes 1572868
  15.4 0.9 %copy-start.4 = (f32[2,128,256]{2,1,0:T(8,128)S(1)}, f32[2,128,256]{2,1,0:T(8,128)}, u32[]{:S(2)}) copy-start(f32[2,128,256]{2,1,0:T(8,128)} %constant.13.clone.base_ref) | copy-start | bytes 786436
  16.3 19.4 %copy-start.5 = (s32[4,16]{1,0:T(4,128)S(1)}, s32[4,16]{1,0:T(4,128)}, u32[]{:S(2)}) copy-start(s32[4,16]{1,0:T(4,128)} %starts_ref.3) | copy-start | bytes 772
  35.6 1.8 %collective-permute-start.7 = (bf16[2,512,128]{2,1,0:T(8,128)(2,1)S(1)}, bf16[2,512,128]{2,1,0:T(8,128)(2,1)S(1)}, u32[]{:S(2)}, u32[]{:S(2)}) collective-permute-start(bf16[2,512,128]{2,1,0:T(8,128)(2,1)S(1)} %get-tuple-element.39), channel_id=1, source_target_pairs={{0,1},{1,0},{2,3},{3,2},{4,5},{5,4},{6,7},{7,6},{8,9},{9,8},{10,11... | collective-permute-start | bytes 786440 | tf_op jit(solution)/shard_map/ppermute | solution.py:429
  39.7 6.0 %collective-permute-start.8 = (s16[520,128]{1,0:T(8,128)(2,1)S(1)}, s16[520,128]{1,0:T(8,128)(2,1)S(1)}, u32[]{:S(2)}, u32[]{:S(2)}) collective-permute-start(s16[520,128]{1,0:T(8,128)(2,1)S(1)} %get-tuple-element.41), channel_id=1, source_target_pairs={{0,2},{2,0},{4,6},{6,4},{8,10},{10,8},{12,14},{14,12},{1,3},{3,1},... | collective-permute-start | bytes 399368 | tf_op jit(solution)/shard_map/ppermute | solution.py:397
  40.4 6.4 %collective-permute-start.9 = (s16[520,128]{1,0:T(8,128)(2,1)S(1)}, s16[520,128]{1,0:T(8,128)(2,1)S(1)}, u32[]{:S(2)}, u32[]{:S(2)}) collective-permute-start(s16[520,128]{1,0:T(8,128)(2,1)S(1)} %get-tuple-element.42), channel_id=1, source_target_pairs={{0,4},{2,6},{4,0},{6,2},{8,12},{10,14},{12,8},{14,10},{1,5},{3,7},... | collective-permute-start | bytes 399368 | tf_op jit(solution)/shard_map/ppermute | solution.py:397
  40.4 10.6 %collective-permute-start.10 = (s16[520,128]{1,0:T(8,128)(2,1)S(1)}, s16[520,128]{1,0:T(8,128)(2,1)S(1)}, u32[]{:S(2)}, u32[]{:S(2)}) collective-permute-start(s16[520,128]{1,0:T(8,128)(2,1)S(1)} %get-tuple-element.43), channel_id=1, source_target_pairs={{0,8},{2,10},{4,12},{6,14},{8,0},{10,2},{12,4},{14,6},{1,9},{3,11}... | collective-permute-start | bytes 399368 | tf_op jit(solution)/shard_map/ppermute | solution.py:397
  41.5 17.6 %collective-permute-start.11 = (s16[520,128]{1,0:T(8,128)(2,1)S(1)}, s16[520,128]{1,0:T(8,128)(2,1)S(1)}, u32[]{:S(2)}, u32[]{:S(2)}) collective-permute-start(s16[520,128]{1,0:T(8,128)(2,1)S(1)} %get-tuple-element.44), channel_id=1, source_target_pairs={{0,10},{2,8},{4,14},{6,12},{8,2},{10,0},{12,6},{14,4},{1,11},{3,9}... | collective-permute-start | bytes 399368 | tf_op jit(solution)/shard_map/ppermute | solution.py:397
  44.2 20.7 %collective-permute-start.12 = (s16[520,128]{1,0:T(8,128)(2,1)S(1)}, s16[520,128]{1,0:T(8,128)(2,1)S(1)}, u32[]{:S(2)}, u32[]{:S(2)}) collective-permute-start(s16[520,128]{1,0:T(8,128)(2,1)S(1)} %get-tuple-element.45), channel_id=1, source_target_pairs={{0,12},{2,14},{4,8},{6,10},{8,4},{10,6},{12,0},{14,2},{1,13},{3,15... | collective-permute-start | bytes 399368 | tf_op jit(solution)/shard_map/ppermute | solution.py:397
  45.7 22.4 %collective-permute-start.13 = (s16[520,128]{1,0:T(8,128)(2,1)S(1)}, s16[520,128]{1,0:T(8,128)(2,1)S(1)}, u32[]{:S(2)}, u32[]{:S(2)}) collective-permute-start(s16[520,128]{1,0:T(8,128)(2,1)S(1)} %get-tuple-element.46), channel_id=1, source_target_pairs={{0,14},{2,12},{4,10},{6,8},{8,6},{10,4},{12,2},{14,0},{1,15},{3,13... | collective-permute-start | bytes 399368 | tf_op jit(solution)/shard_map/ppermute | solution.py:397
  46.8 21.3 %collective-permute-start.14 = (s16[520,128]{1,0:T(8,128)(2,1)S(1)}, s16[520,128]{1,0:T(8,128)(2,1)S(1)}, u32[]{:S(2)}, u32[]{:S(2)}) collective-permute-start(s16[520,128]{1,0:T(8,128)(2,1)S(1)} %get-tuple-element.47), channel_id=1, source_target_pairs={{0,6},{2,4},{4,2},{6,0},{8,14},{10,12},{12,10},{14,8},{1,7},{3,5},... | collective-permute-start | bytes 399368 | tf_op jit(solution)/shard_map/ppermute | solution.py:397

commit v3 on v2

--- a/solution.py
+++ b/solution.py
@@ -128,7 +128,7 @@
 TILES = 8
 LINES = 2 * LINES_DEV
 SIDE = LINES_DEV // 2
-ORDER = (1, 2, 4, 5, 6, 7, 3, 0)
+ORDER = (6, 1, 4, 5, 2, 3, 7, 0)
 PLACE = tuple(ORDER.index(i) for i in range(NDEV))
 VMEM_LIMIT = 20 * 1024 * 1024
 

time: 70.4 us -> 67.2 us (0.955)
  the two profiles are of different devices: /device:TPU:16 before, /device:TPU:0 now
where the time goes in v3:
time: 67.2 us; the launch traced here: 67 us
  starting transfers between devices  34.3 us (51%)
  waiting for transfers between devices  18.6 us (28%)
  Pallas kernels  9.69 us (14%)
  local copies, waits for them, and re-layouts  4.41 us (7%)
    ppermute x14, starting transfers between devices, exchange(): lax.ppermute(messages[i], 'az', [(d, d ^ i) for d in range(NDEV)])  34.2 us
    ppermute x14, waiting for transfers between devices, exchange(): lax.ppermute(messages[i], 'az', [(d, d ^ i) for d in range(NDEV)])  18.6 us
    unnamed x12, local copies, waits for them, and re-layouts  4.41 us
    pallas_call x1, Pallas kernels, fast_body(): vmem_call(outer_kernel, 'outer', [message] * NDEV, smem=3, vmem=5, scratc...  2.35 us
    pallas_call x1, Pallas kernels, fast_body(): vmem_call(image_kernel, 'image', jax.ShapeDtypeStruct((LINES, bins), BF16...  2.07 us
    pallas_call x1, Pallas kernels, fast_body(): vmem_call(spread_kernel, 'spread', [message] * NDEV, smem=1, vmem=2)  1.86 us
    pallas_call x1, Pallas kernels, fast_body(): vmem_call(inner_kernel, 'inner', jax.ShapeDtypeStruct((2, 2, TILES - 1, L...  1.68 us
  transfers between devices with their start and end apart: 15, of which 4 were waited for; matrix products, arithmetic and copies ran while one was open for 0% of the time, Pallas kernels for 3%

profile of v3, /device:TPU:0, one launch (start us, length us, event | category | flops | bytes accessed | tf_op | source)
XLA Modules:
  0.0 67.0 jit_solution(14640690185674972603)
XLA Ops:
  0.0 0.0 copy-start
  0.0 0.0 copy-start.1
  0.0 1.2 %copy-done.1 = bf16[2,2,256,256]{3,2,1,0:T(8,128)(2,1)S(1)} copy-done((bf16[2,2,256,256]{3,2,1,0:T(8,128)(2,1)S(1)}, bf16[2,2,256,256]{3,2,1,0:T(8,128)(2,1)}, u32[]{:S(2)}) %copy-start.1) | copy-done | bytes 524312
  1.2 0.0 copy-start.3
  1.2 1.2 %copy-done.3 = bf16[2,32,8,1024]{3,2,1,0:T(8,128)(2,1)S(1)} copy-done((bf16[2,32,8,1024]{3,2,1,0:T(8,128)(2,1)S(1)}, bf16[2,32,8,1024]{3,2,1,0:T(8,128)(2,1)}, u32[]{:S(2)}) %copy-start.3) | copy-done | bytes 1048600
  2.4 1.9 %spread.1 = (s16[520,128]{1,0:T(8,128)(2,1)S(1)}, s16[520,128]{1,0:T(8,128)(2,1)S(1)}, s16[520,128]{1,0:T(8,128)(2,1)S(1)}, s16[520,128]{1,0:T(8,128)(2,1)}, s16...) custom-call(s32[1]{0:T(128)} %bitcast.me_ref, ...), custom_call_target="tpu_custom_call" | custom-call | tf_op jit(solution)/shard_map/spread/pallas_call | solution.py:410
  4.3 2.9 %collective-permute-start.1 = (s16[520,128]{1,0:T(8,128)(2,1)S(1)}, s16[520,128]{1,0:T(8,128)(2,1)S(1)}, u32[]{:S(2)}, u32[]{:S(2)}) collective-permute-start(s16[520,128]{1,0:T(8,128)(2,1)S(1)} %get-tuple-element.28), channel_id=1, source_target_pairs={{0,2},{2,0},{4,6},{6,4},{8,10},{10,8},{12,14},{14,12},{1,3},{3,1},... | collective-permute-start | bytes 399368 | tf_op jit(solution)/shard_map/ppermute | solution.py:397
  7.2 1.6 %collective-permute-start.4 = (s16[520,128]{1,0:T(8,128)(2,1)S(1)}, s16[520,128]{1,0:T(8,128)(2,1)S(1)}, u32[]{:S(2)}, u32[]{:S(2)}) collective-permute-start(s16[520,128]{1,0:T(8,128)(2,1)S(1)} %get-tuple-element.29), channel_id=1, source_target_pairs={{0,4},{2,6},{4,0},{6,2},{8,12},{10,14},{12,8},{14,10},{1,5},{3,7},... | collective-permute-start | bytes 399368 | tf_op jit(solution)/shard_map/ppermute | solution.py:397
  8.8 0.0 collective-permute-start.5
  8.8 3.0 %collective-permute-start.2 = (s16[520,128]{1,0:T(8,128)(2,1)}, s16[520,128]{1,0:T(8,128)(2,1)S(1)}, u32[]{:S(2)}, u32[]{:S(2)}) collective-permute-start(s16[520,128]{1,0:T(8,128)(2,1)} %get-tuple-element.31), channel_id=1, source_target_pairs={{0,8},{2,10},{4,12},{6,14},{8,0},{10,2},{12,4},{14,6},{1,9},{3,11}... | collective-permute-start | bytes 399368 | tf_op jit(solution)/shard_map/ppermute | solution.py:397
  11.8 1.3 %collective-permute-start.3 = (s16[520,128]{1,0:T(8,128)(2,1)}, s16[520,128]{1,0:T(8,128)(2,1)S(1)}, u32[]{:S(2)}, u32[]{:S(2)}) collective-permute-start(s16[520,128]{1,0:T(8,128)(2,1)} %get-tuple-element.32), channel_id=1, source_target_pairs={{0,10},{2,8},{4,14},{6,12},{8,2},{10,0},{12,6},{14,4},{1,11},{3,9}... | collective-permute-start | bytes 399368 | tf_op jit(solution)/shard_map/ppermute | solution.py:397
  13.1 0.0 collective-permute-done.1.refs_1_
  13.1 3.6 %collective-permute-start = (s16[520,128]{1,0:T(8,128)(2,1)S(1)}, s16[520,128]{1,0:T(8,128)(2,1)S(1)}, u32[]{:S(2)}, u32[]{:S(2)}) collective-permute-start(s16[520,128]{1,0:T(8,128)(2,1)S(1)} %get-tuple-element.33), channel_id=1, source_target_pairs={{0,12},{2,14},{4,8},{6,10},{8,4},{10,6},{12,0},{14,2},{1,13},{3,15... | collective-permute-start | bytes 399368 | tf_op jit(solution)/shard_map/ppermute | solution.py:397
  16.7 1.3 %collective-permute-done.4.refs_4_ = s16[520,128]{1,0:T(8,128)(2,1)S(1)} collective-permute-done((s16[520,128]{1,0:T(8,128)(2,1)S(1)}, s16[520,128]{1,0:T(8,128)(2,1)S(1)}, u32[]{:S(2)}, u32[]{:S(2)}) %collective-permute-start.4) | collective-permute-done | bytes 133152 | tf_op jit(solution)/shard_map/ppermute | solution.py:397
  18.0 0.5 collective-permute-start.6
  18.5 0.0 copy-start.2
  18.5 1.0 %copy-done.2 = bf16[2,2,256,256]{3,2,1,0:T(8,128)(2,1)S(1)} copy-done((bf16[2,2,256,256]{3,2,1,0:T(8,128)(2,1)S(1)}, bf16[2,2,256,256]{3,2,1,0:T(8,128)(2,1)}, u32[]{:S(2)}) %copy-start.2) | copy-done | bytes 524312
  19.5 0.0 copy-start.4
  19.5 0.9 %copy-done.4 = f32[2,128,256]{2,1,0:T(8,128)S(1)} copy-done((f32[2,128,256]{2,1,0:T(8,128)S(1)}, f32[2,128,256]{2,1,0:T(8,128)}, u32[]{:S(2)}) %copy-start.4) | copy-done | bytes 262168
  20.5 0.0 copy-start.5
  20.5 0.5 tables.1
  21.0 0.0 collective-permute-done.5.refs_5_
  21.0 0.0 collective-permute-done.2.refs_2_
  21.0 10.6 %collective-permute-done.3.refs_3_ = s16[520,128]{1,0:T(8,128)(2,1)S(1)} collective-permute-done((s16[520,128]{1,0:T(8,128)(2,1)}, s16[520,128]{1,0:T(8,128)(2,1)S(1)}, u32[]{:S(2)}, u32[]{:S(2)}) %collective-permute-start.3) | collective-permute-done | bytes 133152 | tf_op jit(solution)/shard_map/ppermute | solution.py:397
  31.6 0.0 collective-permute-done.refs_0_
  31.6 0.0 collective-permute-done.6.refs_6_
  31.6 1.2 %forward.1 = (bf16[8,2,512,128]{3,2,1,0:T(8,128)(2,1)S(1)}, bf16[2,512,128]{2,1,0:T(8,128)(2,1)S(1)}) custom-call(s32[1]{0:T(128)} %bitcast.me_ref, s32[1]{0:T(128)} %bitcast.2.rg_ref, bf16[2,2,256,256]{3,2,1,0:T(8,128)(2,1)S(1)} %get-tuple-element.37.table_ref, s16[520,128]{1,0:T(8,128)(2,1)S(1)} %collective-permute-done.refs_0_, ...), custom_call_target="tpu_custom_call" | custom-call | tf_op jit(solution)/shard_map/forward/pallas_call | solution.py:422
  32.9 0.1 collective-permute-start.7
  33.0 0.0 copy-done
  33.0 0.0 copy-done.5
  33.0 1.7 %inner.1.focus_ref = bf16[2,2,7,256,128]{4,3,2,1,0:T(8,128)(2,1)S(1)} custom-call(s32[1]{0:T(128)} %bitcast.2.rg_ref, s32[4,16]{1,0:T(4,128)S(1)} %copy-done.5, bf16[8,2,512,128]{3,2,1,0:T(8,128)(2,1)S(1)} %get-tuple-element.38.spectrum_ref, bf16[4,8,256,128]{3,2,1,0:T(8,128)(2,1)S(1)} %copy-done), custom_call_target="tpu_custom_call" | custom-call | tf_op jit(solution)/shard_map/inner/pallas_call | solution.py:430
  34.7 0.0 collective-permute-done.7.halo_ref
  34.7 2.4 %outer.1 = (s16[520,128]{1,0:T(8,128)(2,1)S(1)}, s16[520,128]{1,0:T(8,128)(2,1)S(1)}, s16[520,128]{1,0:T(8,128)(2,1)S(1)}, s16[520,128]{1,0:T(8,128)(2,1)S(1)}, ...) custom-call(s32[1]{0:T(128)} %bitcast.me_ref, ...), custom_call_target="tpu_custom_call" | custom-call | tf_op jit(solution)/shard_map/outer/pallas_call | solution.py:437
  37.0 3.3 %collective-permute-start.8 = (s16[520,128]{1,0:T(8,128)(2,1)S(1)}, s16[520,128]{1,0:T(8,128)(2,1)S(1)}, u32[]{:S(2)}, u32[]{:S(2)}) collective-permute-start(s16[520,128]{1,0:T(8,128)(2,1)S(1)} %get-tuple-element.41), channel_id=1, source_target_pairs={{0,12},{2,14},{4,8},{6,10},{8,4},{10,6},{12,0},{14,2},{1,13},{3,15... | collective-permute-start | bytes 399368 | tf_op jit(solution)/shard_map/ppermute | solution.py:397
  40.3 1.0 %collective-permute-start.9 = (s16[520,128]{1,0:T(8,128)(2,1)S(1)}, s16[520,128]{1,0:T(8,128)(2,1)S(1)}, u32[]{:S(2)}, u32[]{:S(2)}) collective-permute-start(s16[520,128]{1,0:T(8,128)(2,1)S(1)} %get-tuple-element.42), channel_id=1, source_target_pairs={{0,2},{2,0},{4,6},{6,4},{8,10},{10,8},{12,14},{14,12},{1,3},{3,1},... | collective-permute-start | bytes 399368 | tf_op jit(solution)/shard_map/ppermute | solution.py:397
  41.4 3.1 %collective-permute-start.10 = (s16[520,128]{1,0:T(8,128)(2,1)S(1)}, s16[520,128]{1,0:T(8,128)(2,1)S(1)}, u32[]{:S(2)}, u32[]{:S(2)}) collective-permute-start(s16[520,128]{1,0:T(8,128)(2,1)S(1)} %get-tuple-element.43), channel_id=1, source_target_pairs={{0,8},{2,10},{4,12},{6,14},{8,0},{10,2},{12,4},{14,6},{1,9},{3,11}... | collective-permute-start | bytes 399368 | tf_op jit(solution)/shard_map/ppermute | solution.py:397
  44.5 0.9 %collective-permute-start.11 = (s16[520,128]{1,0:T(8,128)(2,1)S(1)}, s16[520,128]{1,0:T(8,128)(2,1)S(1)}, u32[]{:S(2)}, u32[]{:S(2)}) collective-permute-start(s16[520,128]{1,0:T(8,128)(2,1)S(1)} %get-tuple-element.44), channel_id=1, source_target_pairs={{0,10},{2,8},{4,14},{6,12},{8,2},{10,0},{12,6},{14,4},{1,11},{3,9}... | collective-permute-start | bytes 399368 | tf_op jit(solution)/shard_map/ppermute | solution.py:397
  45.4 3.4 %collective-permute-start.12 = (s16[520,128]{1,0:T(8,128)(2,1)S(1)}, s16[520,128]{1,0:T(8,128)(2,1)S(1)}, u32[]{:S(2)}, u32[]{:S(2)}) collective-permute-start(s16[520,128]{1,0:T(8,128)(2,1)S(1)} %get-tuple-element.45), channel_id=1, source_target_pairs={{0,4},{2,6},{4,0},{6,2},{8,12},{10,14},{12,8},{14,10},{1,5},{3,7},... | collective-permute-start | bytes 399368 | tf_op jit(solution)/shard_map/ppermute | solution.py:397
  48.8 0.0 collective-permute-done.8.refs_0_
  48.8 5.5 %collective-permute-start.13 = (s16[520,128]{1,0:T(8,128)(2,1)S(1)}, s16[520,128]{1,0:T(8,128)(2,1)S(1)}, u32[]{:S(2)}, u32[]{:S(2)}) collective-permute-start(s16[520,128]{1,0:T(8,128)(2,1)S(1)} %get-tuple-element.46), channel_id=1, source_target_pairs={{0,6},{2,4},{4,2},{6,0},{8,14},{10,12},{12,10},{14,8},{1,7},{3,5},... | collective-permute-start | bytes 399368 | tf_op jit(solution)/shard_map/ppermute | solution.py:397
  54.3 0.0 collective-permute-done.9.refs_1_
  54.3 4.0 %collective-permute-start.14 = (s16[520,128]{1,0:T(8,128)(2,1)S(1)}, s16[520,128]{1,0:T(8,128)(2,1)S(1)}, u32[]{:S(2)}, u32[]{:S(2)}) collective-permute-start(s16[520,128]{1,0:T(8,128)(2,1)S(1)} %get-tuple-element.47), channel_id=1, source_target_pairs={{0,14},{2,12},{4,10},{6,8},{8,6},{10,4},{12,2},{14,0},{1,15},{3,13... | collective-permute-start | bytes 399368 | tf_op jit(solution)/shard_map/ppermute | solution.py:397
  58.3 0.0 collective-permute-done.10.refs_2_
  58.3 1.4 %collective-permute-done.11.refs_3_ = s16[520,128]{1,0:T(8,128)(2,1)S(1)} collective-permute-done((s16[520,128]{1,0:T(8,128)(2,1)S(1)}, s16[520,128]{1,0:T(8,128)(2,1)S(1)}, u32[]{:S(2)}, u32[]{:S(2)}) %collective-permute-start.11) | collective-permute-done | bytes 133152 | tf_op jit(solution)/shard_map/ppermute | solution.py:397
  59.7 0.0 collective-permute-done.12.refs_4_
  59.7 5.2 %collective-permute-done.13.refs_5_ = s16[520,128]{1,0:T(8,128)(2,1)S(1)} collective-permute-done((s16[520,128]{1,0:T(8,128)(2,1)S(1)}, s16[520,128]{1,0:T(8,128)(2,1)S(1)}, u32[]{:S(2)}, u32[]{:S(2)}) %collective-permute-start.13) | collective-permute-done | bytes 133152 | tf_op jit(solution)/shard_map/ppermute | solution.py:397
  64.9 0.0 collective-permute-done.14.refs_6_
  64.9 2.1 %image.1 = bf16[512,1024]{1,0:T(8,128)(2,1)} custom-call(bf16[2,256,256]{2,1,0:T(8,128)(2,1)S(1)} %get-tuple-element.36.table_ref, s16[520,128]{1,0:T(8,128)(2,1)S(1)} %collective-permute-done.8.refs_0_, s16[520,128]{1,0:T(8,128)(2,1)S(1)} %collective-permute-done.9.refs_1_, s16[520,128]{1,0:T(8,128)(2,1)S(1)} %collective-permute-done.10.refs_2_, ...), custom_call_target="tpu_custom_call" | custom-call | tf_op jit(solution)/shard_map/image/pallas_call | solution.py:446
Async XLA Ops:
  0.0 33.0 %copy-start = (bf16[4,8,256,128]{3,2,1,0:T(8,128)(2,1)S(1)}, bf16[4,8,256,128]{3,2,1,0:T(8,128)(2,1)}, u32[]{:S(2)}) copy-start(bf16[4,8,256,128]{3,2,1,0:T(8,128)(2,1)} %weights_ref.3) | copy-start | bytes 6291460
  0.0 1.2 %copy-start.1 = (bf16[2,2,256,256]{3,2,1,0:T(8,128)(2,1)S(1)}, bf16[2,2,256,256]{3,2,1,0:T(8,128)(2,1)}, u32[]{:S(2)}) copy-start(bf16[2,2,256,256]{3,2,1,0:T(8,128)(2,1)} %constant.12.clone.table_ref.short_ref) | copy-start | bytes 1572868
  1.2 1.2 %copy-start.3 = (bf16[2,32,8,1024]{3,2,1,0:T(8,128)(2,1)S(1)}, bf16[2,32,8,1024]{3,2,1,0:T(8,128)(2,1)}, u32[]{:S(2)}) copy-start(bf16[2,32,8,1024]{3,2,1,0:T(8,128)(2,1)} %param.5) | copy-start | bytes 3145732
  4.3 8.8 %collective-permute-start.1 = (s16[520,128]{1,0:T(8,128)(2,1)S(1)}, s16[520,128]{1,0:T(8,128)(2,1)S(1)}, u32[]{:S(2)}, u32[]{:S(2)}) collective-permute-start(s16[520,128]{1,0:T(8,128)(2,1)S(1)} %get-tuple-element.28), channel_id=1, source_target_pairs={{0,2},{2,0},{4,6},{6,4},{8,10},{10,8},{12,14},{14,12},{1,3},{3,1},... | collective-permute-start | bytes 399368 | tf_op jit(solution)/shard_map/ppermute | solution.py:397
  7.2 10.8 %collective-permute-start.4 = (s16[520,128]{1,0:T(8,128)(2,1)S(1)}, s16[520,128]{1,0:T(8,128)(2,1)S(1)}, u32[]{:S(2)}, u32[]{:S(2)}) collective-permute-start(s16[520,128]{1,0:T(8,128)(2,1)S(1)} %get-tuple-element.29), channel_id=1, source_target_pairs={{0,4},{2,6},{4,0},{6,2},{8,12},{10,14},{12,8},{14,10},{1,5},{3,7},... | collective-permute-start | bytes 399368 | tf_op jit(solution)/shard_map/ppermute | solution.py:397
  8.8 12.2 %collective-permute-start.5 = (s16[520,128]{1,0:T(8,128)(2,1)}, s16[520,128]{1,0:T(8,128)(2,1)S(1)}, u32[]{:S(2)}, u32[]{:S(2)}) collective-permute-start(s16[520,128]{1,0:T(8,128)(2,1)} %get-tuple-element.30), channel_id=1, source_target_pairs={{0,6},{2,4},{4,2},{6,0},{8,14},{10,12},{12,10},{14,8},{1,7},{3,5},... | collective-permute-start | bytes 399368 | tf_op jit(solution)/shard_map/ppermute | solution.py:397
  8.8 12.2 %collective-permute-start.2 = (s16[520,128]{1,0:T(8,128)(2,1)}, s16[520,128]{1,0:T(8,128)(2,1)S(1)}, u32[]{:S(2)}, u32[]{:S(2)}) collective-permute-start(s16[520,128]{1,0:T(8,128)(2,1)} %get-tuple-element.31), channel_id=1, source_target_pairs={{0,8},{2,10},{4,12},{6,14},{8,0},{10,2},{12,4},{14,6},{1,9},{3,11}... | collective-permute-start | bytes 399368 | tf_op jit(solution)/shard_map/ppermute | solution.py:397
  11.8 19.8 %collective-permute-start.3 = (s16[520,128]{1,0:T(8,128)(2,1)}, s16[520,128]{1,0:T(8,128)(2,1)S(1)}, u32[]{:S(2)}, u32[]{:S(2)}) collective-permute-start(s16[520,128]{1,0:T(8,128)(2,1)} %get-tuple-element.32), channel_id=1, source_target_pairs={{0,10},{2,8},{4,14},{6,12},{8,2},{10,0},{12,6},{14,4},{1,11},{3,9}... | collective-permute-start | bytes 399368 | tf_op jit(solution)/shard_map/ppermute | solution.py:397
  13.1 18.6 %collective-permute-start = (s16[520,128]{1,0:T(8,128)(2,1)S(1)}, s16[520,128]{1,0:T(8,128)(2,1)S(1)}, u32[]{:S(2)}, u32[]{:S(2)}) collective-permute-start(s16[520,128]{1,0:T(8,128)(2,1)S(1)} %get-tuple-element.33), channel_id=1, source_target_pairs={{0,12},{2,14},{4,8},{6,10},{8,4},{10,6},{12,0},{14,2},{1,13},{3,15... | collective-permute-start | bytes 399368 | tf_op jit(solution)/shard_map/ppermute | solution.py:397
  18.0 13.7 %collective-permute-start.6 = (s16[520,128]{1,0:T(8,128)(2,1)S(1)}, s16[520,128]{1,0:T(8,128)(2,1)S(1)}, u32[]{:S(2)}, u32[]{:S(2)}) collective-permute-start(s16[520,128]{1,0:T(8,128)(2,1)S(1)} %get-tuple-element.34), channel_id=1, source_target_pairs={{0,14},{2,12},{4,10},{6,8},{8,6},{10,4},{12,2},{14,0},{1,15},{3,13... | collective-permute-start | bytes 399368 | tf_op jit(solution)/shard_map/ppermute | solution.py:397
  18.5 1.0 %copy-start.2 = (bf16[2,2,256,256]{3,2,1,0:T(8,128)(2,1)S(1)}, bf16[2,2,256,256]{3,2,1,0:T(8,128)(2,1)}, u32[]{:S(2)}) copy-start(bf16[2,2,256,256]{3,2,1,0:T(8,128)(2,1)} %constant.12.clone.table_ref.short_ref) | copy-start | bytes 1572868
  19.5 0.9 %copy-start.4 = (f32[2,128,256]{2,1,0:T(8,128)S(1)}, f32[2,128,256]{2,1,0:T(8,128)}, u32[]{:S(2)}) copy-start(f32[2,128,256]{2,1,0:T(8,128)} %constant.13.clone.base_ref) | copy-start | bytes 786436
  20.5 12.5 %copy-start.5 = (s32[4,16]{1,0:T(4,128)S(1)}, s32[4,16]{1,0:T(4,128)}, u32[]{:S(2)}) copy-start(s32[4,16]{1,0:T(4,128)} %starts_ref.3) | copy-start | bytes 772
  32.9 1.8 %collective-permute-start.7 = (bf16[2,512,128]{2,1,0:T(8,128)(2,1)S(1)}, bf16[2,512,128]{2,1,0:T(8,128)(2,1)S(1)}, u32[]{:S(2)}, u32[]{:S(2)}) collective-permute-start(bf16[2,512,128]{2,1,0:T(8,128)(2,1)S(1)} %get-tuple-element.39), channel_id=1, source_target_pairs={{0,1},{1,0},{2,3},{3,2},{4,5},{5,4},{6,7},{7,6},{8,9},{9,8},{10,11... | collective-permute-start | bytes 786440 | tf_op jit(solution)/shard_map/ppermute | solution.py:429
  37.0 11.8 %collective-permute-start.8 = (s16[520,128]{1,0:T(8,128)(2,1)S(1)}, s16[520,128]{1,0:T(8,128)(2,1)S(1)}, u32[]{:S(2)}, u32[]{:S(2)}) collective-permute-start(s16[520,128]{1,0:T(8,128)(2,1)S(1)} %get-tuple-element.41), channel_id=1, source_target_pairs={{0,12},{2,14},{4,8},{6,10},{8,4},{10,6},{12,0},{14,2},{1,13},{3,15... | collective-permute-start | bytes 399368 | tf_op jit(solution)/shard_map/ppermute | solution.py:397
  40.3 14.0 %collective-permute-start.9 = (s16[520,128]{1,0:T(8,128)(2,1)S(1)}, s16[520,128]{1,0:T(8,128)(2,1)S(1)}, u32[]{:S(2)}, u32[]{:S(2)}) collective-permute-start(s16[520,128]{1,0:T(8,128)(2,1)S(1)} %get-tuple-element.42), channel_id=1, source_target_pairs={{0,2},{2,0},{4,6},{6,4},{8,10},{10,8},{12,14},{14,12},{1,3},{3,1},... | collective-permute-start | bytes 399368 | tf_op jit(solution)/shard_map/ppermute | solution.py:397
  41.4 17.0 %collective-permute-start.10 = (s16[520,128]{1,0:T(8,128)(2,1)S(1)}, s16[520,128]{1,0:T(8,128)(2,1)S(1)}, u32[]{:S(2)}, u32[]{:S(2)}) collective-permute-start(s16[520,128]{1,0:T(8,128)(2,1)S(1)} %get-tuple-element.43), channel_id=1, source_target_pairs={{0,8},{2,10},{4,12},{6,14},{8,0},{10,2},{12,4},{14,6},{1,9},{3,11}... | collective-permute-start | bytes 399368 | tf_op jit(solution)/shard_map/ppermute | solution.py:397
  44.5 15.2 %collective-permute-start.11 = (s16[520,128]{1,0:T(8,128)(2,1)S(1)}, s16[520,128]{1,0:T(8,128)(2,1)S(1)}, u32[]{:S(2)}, u32[]{:S(2)}) collective-permute-start(s16[520,128]{1,0:T(8,128)(2,1)S(1)} %get-tuple-element.44), channel_id=1, source_target_pairs={{0,10},{2,8},{4,14},{6,12},{8,2},{10,0},{12,6},{14,4},{1,11},{3,9}... | collective-permute-start | bytes 399368 | tf_op jit(solution)/shard_map/ppermute | solution.py:397
  45.4 14.3 %collective-permute-start.12 = (s16[520,128]{1,0:T(8,128)(2,1)S(1)}, s16[520,128]{1,0:T(8,128)(2,1)S(1)}, u32[]{:S(2)}, u32[]{:S(2)}) collective-permute-start(s16[520,128]{1,0:T(8,128)(2,1)S(1)} %get-tuple-element.45), channel_id=1, source_target_pairs={{0,4},{2,6},{4,0},{6,2},{8,12},{10,14},{12,8},{14,10},{1,5},{3,7},... | collective-permute-start | bytes 399368 | tf_op jit(solution)/shard_map/ppermute | solution.py:397
  48.8 16.1 %collective-permute-start.13 = (s16[520,128]{1,0:T(8,128)(2,1)S(1)}, s16[520,128]{1,0:T(8,128)(2,1)S(1)}, u32[]{:S(2)}, u32[]{:S(2)}) collective-permute-start(s16[520,128]{1,0:T(8,128)(2,1)S(1)} %get-tuple-element.46), channel_id=1, source_target_pairs={{0,6},{2,4},{4,2},{6,0},{8,14},{10,12},{12,10},{14,8},{1,7},{3,5},... | collective-permute-start | bytes 399368 | tf_op jit(solution)/shard_map/ppermute | solution.py:397
  54.3 10.6 %collective-permute-start.14 = (s16[520,128]{1,0:T(8,128)(2,1)S(1)}, s16[520,128]{1,0:T(8,128)(2,1)S(1)}, u32[]{:S(2)}, u32[]{:S(2)}) collective-permute-start(s16[520,128]{1,0:T(8,128)(2,1)S(1)} %get-tuple-element.47), channel_id=1, source_target_pairs={{0,14},{2,12},{4,10},{6,8},{8,6},{10,4},{12,2},{14,0},{1,15},{3,13... | collective-permute-start | bytes 399368 | tf_op jit(solution)/shard_map/ppermute | solution.py:397

commit v4 on v3

--- a/solution.py
+++ b/solution.py
@@ -128,8 +128,8 @@
 TILES = 8
 LINES = 2 * LINES_DEV
 SIDE = LINES_DEV // 2
-ORDER = (6, 1, 4, 5, 2, 3, 7, 0)
-PLACE = tuple(ORDER.index(i) for i in range(NDEV))
+OUT_ORDER = (6, 2, 4, 5, 1, 3, 7, 0)
+BACK_ORDER = (6, 2, 4, 5, 1, 3, 7, 0)
 VMEM_LIMIT = 20 * 1024 * 1024
 
 
@@ -215,8 +215,8 @@
     return [(t, t + 1) for t in range(0, tiles, 2)]
 
 
-def in_order(refs):
-    return [refs[at] for at in PLACE]
+def in_order(refs, order):
+    return [refs[order.index(i)] for i in range(NDEV)]
 
 
 def sign_of(me):
@@ -270,7 +270,7 @@
 
 
 def forward_kernel(me_ref, rg_ref, table_ref, *refs):
-    in_refs, (out_ref, edge_ref) = in_order(refs[:NDEV]), refs[NDEV:]
+    in_refs, (out_ref, edge_ref) = in_order(refs[:NDEV], OUT_ORDER), refs[NDEV:]
     sign = sign_of(me_ref[0])
     scales = [load_scales(ref) for ref in in_refs]
     for tiles in tile_pairs(TILES):
@@ -360,7 +360,7 @@
 
 
 def image_kernel(table_ref, *refs):
-    in_refs, out_ref = in_order(refs[:NDEV]), refs[NDEV]
+    in_refs, out_ref = in_order(refs[:NDEV], BACK_ORDER), refs[NDEV]
     scales = [load_scales(ref) for ref in in_refs]
     for tiles in tile_pairs(TILES):
         values = [load_columns(ref, scale, tiles) for ref, scale in zip(in_refs, scales)]
@@ -392,10 +392,10 @@
     return lax.optimization_barrier((value, *others))[0]
 
 
-def exchange(messages):
+def exchange(messages, order):
     return [
         lax.ppermute(messages[i], "az", [(d, d ^ i) for d in range(NDEV)]) if i else messages[0]
-        for i in ORDER
+        for i in order
     ]
 
 
@@ -410,14 +410,14 @@
     sent = vmem_call(spread_kernel, "spread", [message] * NDEV, smem=1, vmem=2)(
         me, raw.reshape(LINES, bins), short
     )
-    got = exchange(sent)
+    got = exchange(sent, OUT_ORDER)
     forward_table, inverse_table, image_table = vmem_call(
         tables_kernel,
         "tables",
         [long_shape, long_shape, jax.ShapeDtypeStruct((2, 256, 256), BF16)],
         smem=1,
         vmem=2,
-    )(after(me, *sent), jnp.asarray(long_base()), short)
+    )(after(me, sent[0]), jnp.asarray(long_base()), short)
 
     spectrum, edge = vmem_call(
         forward_kernel,
@@ -442,7 +442,7 @@
         vmem=5,
         scratch=[pltpu.VMEM((3, 2, LINES, TILE), BF16)],
     )(me, rg, band_start, spectrum, halo, stolt_weights, inverse_table, focus)
-    lines = exchange(back)
+    lines = exchange(back, BACK_ORDER)
     image = vmem_call(image_kernel, "image", jax.ShapeDtypeStruct((LINES, bins), BF16), vmem=1 + NDEV)(
         image_table, *lines
     )

time: 67.2 us -> 64.3 us (0.957)
  starting transfers between devices: 34.3 us -> 30.2 us
    ppermute x14, starting transfers between devices: 34.2 us -> 30.2 us  [exchange(): lax.ppermute(messages[i], 'az', [(d, d ^ i) for d in range(NDEV)])]
where the time goes in v4:
time: 64.3 us; the launch traced here: 63.5 us
  starting transfers between devices  30.2 us (47%)
  waiting for transfers between devices  19 us (30%)
  Pallas kernels  9.68 us (15%)
  local copies, waits for them, and re-layouts  4.41 us (7%)
    ppermute x14, starting transfers between devices, exchange(): lax.ppermute(messages[i], 'az', [(d, d ^ i) for d in range(NDEV)])  30.2 us
    ppermute x14, waiting for transfers between devices, exchange(): lax.ppermute(messages[i], 'az', [(d, d ^ i) for d in range(NDEV)])  19 us
    unnamed x12, local copies, waits for them, and re-layouts  4.41 us
    pallas_call x1, Pallas kernels, fast_body(): vmem_call(outer_kernel, 'outer', [message] * NDEV, smem=3, vmem=5, scratc...  2.35 us
    pallas_call x1, Pallas kernels, fast_body(): vmem_call(image_kernel, 'image', jax.ShapeDtypeStruct((LINES, bins), BF16...  2.07 us
    pallas_call x1, Pallas kernels, fast_body(): vmem_call(spread_kernel, 'spread', [message] * NDEV, smem=1, vmem=2)  1.86 us
    pallas_call x1, Pallas kernels, fast_body(): vmem_call(inner_kernel, 'inner', jax.ShapeDtypeStruct((2, 2, TILES - 1, L...  1.68 us
  transfers between devices with their start and end apart: 15, of which 4 were waited for; matrix products, arithmetic and copies ran while one was open for 0% of the time, Pallas kernels for 3%

profile of v4, /device:TPU:0, one launch (start us, length us, event | category | flops | bytes accessed | tf_op | source)
XLA Modules:
  0.0 63.5 jit_solution(9407291981217922245)
XLA Ops:
  0.0 0.0 copy-start
  0.0 0.0 copy-start.1
  0.0 1.2 %copy-done.1 = bf16[2,2,256,256]{3,2,1,0:T(8,128)(2,1)S(1)} copy-done((bf16[2,2,256,256]{3,2,1,0:T(8,128)(2,1)S(1)}, bf16[2,2,256,256]{3,2,1,0:T(8,128)(2,1)}, u32[]{:S(2)}) %copy-start.1) | copy-done | bytes 524312
  1.2 0.0 copy-start.3
  1.2 1.2 %copy-done.3 = bf16[2,32,8,1024]{3,2,1,0:T(8,128)(2,1)S(1)} copy-done((bf16[2,32,8,1024]{3,2,1,0:T(8,128)(2,1)S(1)}, bf16[2,32,8,1024]{3,2,1,0:T(8,128)(2,1)}, u32[]{:S(2)}) %copy-start.3) | copy-done | bytes 1048600
  2.4 1.9 %spread.1 = (s16[520,128]{1,0:T(8,128)(2,1)S(1)}, s16[520,128]{1,0:T(8,128)(2,1)}, s16[520,128]{1,0:T(8,128)(2,1)S(1)}, s16[520,128]{1,0:T(8,128)(2,1)S(1)}, s16...) custom-call(s32[1]{0:T(128)} %bitcast.me_ref, ...), custom_call_target="tpu_custom_call" | custom-call | tf_op jit(solution)/shard_map/spread/pallas_call | solution.py:410
  4.3 5.0 %collective-permute-start = (s16[520,128]{1,0:T(8,128)(2,1)S(1)}, s16[520,128]{1,0:T(8,128)(2,1)S(1)}, u32[]{:S(2)}, u32[]{:S(2)}) collective-permute-start(s16[520,128]{1,0:T(8,128)(2,1)S(1)} %get-tuple-element.31), channel_id=1, source_target_pairs={{0,12},{2,14},{4,8},{6,10},{8,4},{10,6},{12,0},{14,2},{1,13},{3,15... | collective-permute-start | bytes 399368 | tf_op jit(solution)/shard_map/ppermute | solution.py:397
  9.3 0.0 collective-permute-start.1
  9.3 0.6 collective-permute-start.2
  9.9 3.3 %collective-permute-start.3 = (s16[520,128]{1,0:T(8,128)(2,1)}, s16[520,128]{1,0:T(8,128)(2,1)S(1)}, u32[]{:S(2)}, u32[]{:S(2)}) collective-permute-start(s16[520,128]{1,0:T(8,128)(2,1)} %get-tuple-element.34), channel_id=1, source_target_pairs={{0,10},{2,8},{4,14},{6,12},{8,2},{10,0},{12,6},{14,4},{1,11},{3,9}... | collective-permute-start | bytes 399368 | tf_op jit(solution)/shard_map/ppermute | solution.py:397
  13.2 0.5 collective-permute-start.4
  13.7 0.0 collective-permute-done.refs_0_
  13.7 4.6 %collective-permute-start.5 = (s16[520,128]{1,0:T(8,128)(2,1)S(1)}, s16[520,128]{1,0:T(8,128)(2,1)S(1)}, u32[]{:S(2)}, u32[]{:S(2)}) collective-permute-start(s16[520,128]{1,0:T(8,128)(2,1)S(1)} %get-tuple-element.36), channel_id=1, source_target_pairs={{0,6},{2,4},{4,2},{6,0},{8,14},{10,12},{12,10},{14,8},{1,7},{3,5},... | collective-permute-start | bytes 399368 | tf_op jit(solution)/shard_map/ppermute | solution.py:397
  18.4 0.0 collective-permute-done.1.refs_1_
  18.4 1.2 %collective-permute-start.6 = (s16[520,128]{1,0:T(8,128)(2,1)S(1)}, s16[520,128]{1,0:T(8,128)(2,1)S(1)}, u32[]{:S(2)}, u32[]{:S(2)}) collective-permute-start(s16[520,128]{1,0:T(8,128)(2,1)S(1)} %get-tuple-element.37), channel_id=1, source_target_pairs={{0,14},{2,12},{4,10},{6,8},{8,6},{10,4},{12,2},{14,0},{1,15},{3,13... | collective-permute-start | bytes 399368 | tf_op jit(solution)/shard_map/ppermute | solution.py:397
  19.6 0.0 copy-start.2
  19.6 1.0 %copy-done.2 = bf16[2,2,256,256]{3,2,1,0:T(8,128)(2,1)S(1)} copy-done((bf16[2,2,256,256]{3,2,1,0:T(8,128)(2,1)S(1)}, bf16[2,2,256,256]{3,2,1,0:T(8,128)(2,1)}, u32[]{:S(2)}) %copy-start.2) | copy-done | bytes 524312
  20.7 0.0 copy-start.4
  20.7 0.9 %copy-done.4 = f32[2,128,256]{2,1,0:T(8,128)S(1)} copy-done((f32[2,128,256]{2,1,0:T(8,128)S(1)}, f32[2,128,256]{2,1,0:T(8,128)}, u32[]{:S(2)}) %copy-start.4) | copy-done | bytes 262168
  21.6 0.0 copy-start.5
  21.6 0.5 tables.1
  22.1 2.7 %collective-permute-done.2.refs_2_ = s16[520,128]{1,0:T(8,128)(2,1)S(1)} collective-permute-done((s16[520,128]{1,0:T(8,128)(2,1)}, s16[520,128]{1,0:T(8,128)(2,1)S(1)}, u32[]{:S(2)}, u32[]{:S(2)}) %collective-permute-start.2) | collective-permute-done | bytes 133152 | tf_op jit(solution)/shard_map/ppermute | solution.py:397
  24.8 6.2 %collective-permute-done.3.refs_3_ = s16[520,128]{1,0:T(8,128)(2,1)S(1)} collective-permute-done((s16[520,128]{1,0:T(8,128)(2,1)}, s16[520,128]{1,0:T(8,128)(2,1)S(1)}, u32[]{:S(2)}, u32[]{:S(2)}) %collective-permute-start.3) | collective-permute-done | bytes 133152 | tf_op jit(solution)/shard_map/ppermute | solution.py:397
  31.0 0.0 collective-permute-done.4.refs_4_
  31.0 0.0 collective-permute-done.5.refs_5_
  31.0 0.0 collective-permute-done.6.refs_6_
  31.0 1.2 %forward.1 = (bf16[8,2,512,128]{3,2,1,0:T(8,128)(2,1)S(1)}, bf16[2,512,128]{2,1,0:T(8,128)(2,1)S(1)}) custom-call(s32[1]{0:T(128)} %bitcast.me_ref, s32[1]{0:T(128)} %bitcast.2.rg_ref, bf16[2,2,256,256]{3,2,1,0:T(8,128)(2,1)S(1)} %get-tuple-element.30.table_ref, s16[520,128]{1,0:T(8,128)(2,1)S(1)} %collective-permute-done.refs_0_, ...), custom_call_target="tpu_custom_call" | custom-call | tf_op jit(solution)/shard_map/forward/pallas_call | solution.py:422
  32.3 0.1 collective-permute-start.7
  32.4 0.0 copy-done
  32.4 0.0 copy-done.5
  32.4 1.7 %inner.1.focus_ref = bf16[2,2,7,256,128]{4,3,2,1,0:T(8,128)(2,1)S(1)} custom-call(s32[1]{0:T(128)} %bitcast.2.rg_ref, s32[4,16]{1,0:T(4,128)S(1)} %copy-done.5, bf16[8,2,512,128]{3,2,1,0:T(8,128)(2,1)S(1)} %get-tuple-element.38.spectrum_ref, bf16[4,8,256,128]{3,2,1,0:T(8,128)(2,1)S(1)} %copy-done), custom_call_target="tpu_custom_call" | custom-call | tf_op jit(solution)/shard_map/inner/pallas_call | solution.py:430
  34.1 0.0 collective-permute-done.7.halo_ref
  34.1 2.4 %outer.1 = (s16[520,128]{1,0:T(8,128)(2,1)S(1)}, s16[520,128]{1,0:T(8,128)(2,1)S(1)}, s16[520,128]{1,0:T(8,128)(2,1)S(1)}, s16[520,128]{1,0:T(8,128)(2,1)S(1)}, ...) custom-call(s32[1]{0:T(128)} %bitcast.me_ref, ...), custom_call_target="tpu_custom_call" | custom-call | tf_op jit(solution)/shard_map/outer/pallas_call | solution.py:437
  36.4 2.4 %collective-permute-start.8 = (s16[520,128]{1,0:T(8,128)(2,1)S(1)}, s16[520,128]{1,0:T(8,128)(2,1)S(1)}, u32[]{:S(2)}, u32[]{:S(2)}) collective-permute-start(s16[520,128]{1,0:T(8,128)(2,1)S(1)} %get-tuple-element.41), channel_id=1, source_target_pairs={{0,12},{2,14},{4,8},{6,10},{8,4},{10,6},{12,0},{14,2},{1,13},{3,15... | collective-permute-start | bytes 399368 | tf_op jit(solution)/shard_map/ppermute | solution.py:397
  38.8 1.7 %collective-permute-start.9 = (s16[520,128]{1,0:T(8,128)(2,1)S(1)}, s16[520,128]{1,0:T(8,128)(2,1)S(1)}, u32[]{:S(2)}, u32[]{:S(2)}) collective-permute-start(s16[520,128]{1,0:T(8,128)(2,1)S(1)} %get-tuple-element.42), channel_id=1, source_target_pairs={{0,4},{2,6},{4,0},{6,2},{8,12},{10,14},{12,8},{14,10},{1,5},{3,7},... | collective-permute-start | bytes 399368 | tf_op jit(solution)/shard_map/ppermute | solution.py:397
  40.5 0.4 collective-permute-start.10
  40.9 2.5 %collective-permute-start.11 = (s16[520,128]{1,0:T(8,128)(2,1)S(1)}, s16[520,128]{1,0:T(8,128)(2,1)S(1)}, u32[]{:S(2)}, u32[]{:S(2)}) collective-permute-start(s16[520,128]{1,0:T(8,128)(2,1)S(1)} %get-tuple-element.44), channel_id=1, source_target_pairs={{0,10},{2,8},{4,14},{6,12},{8,2},{10,0},{12,6},{14,4},{1,11},{3,9}... | collective-permute-start | bytes 399368 | tf_op jit(solution)/shard_map/ppermute | solution.py:397
  43.4 1.5 %collective-permute-start.12 = (s16[520,128]{1,0:T(8,128)(2,1)S(1)}, s16[520,128]{1,0:T(8,128)(2,1)S(1)}, u32[]{:S(2)}, u32[]{:S(2)}) collective-permute-start(s16[520,128]{1,0:T(8,128)(2,1)S(1)} %get-tuple-element.45), channel_id=1, source_target_pairs={{0,2},{2,0},{4,6},{6,4},{8,10},{10,8},{12,14},{14,12},{1,3},{3,1},... | collective-permute-start | bytes 399368 | tf_op jit(solution)/shard_map/ppermute | solution.py:397
  44.9 0.0 collective-permute-done.8.refs_0_
  44.9 3.2 %collective-permute-start.13 = (s16[520,128]{1,0:T(8,128)(2,1)S(1)}, s16[520,128]{1,0:T(8,128)(2,1)S(1)}, u32[]{:S(2)}, u32[]{:S(2)}) collective-permute-start(s16[520,128]{1,0:T(8,128)(2,1)S(1)} %get-tuple-element.46), channel_id=1, source_target_pairs={{0,6},{2,4},{4,2},{6,0},{8,14},{10,12},{12,10},{14,8},{1,7},{3,5},... | collective-permute-start | bytes 399368 | tf_op jit(solution)/shard_map/ppermute | solution.py:397
  48.1 0.0 collective-permute-done.9.refs_1_
  48.1 3.2 %collective-permute-start.14 = (s16[520,128]{1,0:T(8,128)(2,1)S(1)}, s16[520,128]{1,0:T(8,128)(2,1)S(1)}, u32[]{:S(2)}, u32[]{:S(2)}) collective-permute-start(s16[520,128]{1,0:T(8,128)(2,1)S(1)} %get-tuple-element.47), channel_id=1, source_target_pairs={{0,14},{2,12},{4,10},{6,8},{8,6},{10,4},{12,2},{14,0},{1,15},{3,13... | collective-permute-start | bytes 399368 | tf_op jit(solution)/shard_map/ppermute | solution.py:397
  51.3 4.4 %collective-permute-done.10.refs_2_ = s16[520,128]{1,0:T(8,128)(2,1)S(1)} collective-permute-done((s16[520,128]{1,0:T(8,128)(2,1)S(1)}, s16[520,128]{1,0:T(8,128)(2,1)S(1)}, u32[]{:S(2)}, u32[]{:S(2)}) %collective-permute-start.10) | collective-permute-done | bytes 133152 | tf_op jit(solution)/shard_map/ppermute | solution.py:397
  55.7 5.7 %collective-permute-done.11.refs_3_ = s16[520,128]{1,0:T(8,128)(2,1)S(1)} collective-permute-done((s16[520,128]{1,0:T(8,128)(2,1)S(1)}, s16[520,128]{1,0:T(8,128)(2,1)S(1)}, u32[]{:S(2)}, u32[]{:S(2)}) %collective-permute-start.11) | collective-permute-done | bytes 133152 | tf_op jit(solution)/shard_map/ppermute | solution.py:397
  61.4 0.0 collective-permute-done.12.refs_4_
  61.4 0.0 collective-permute-done.13.refs_5_
  61.4 0.0 collective-permute-done.14.refs_6_
  61.4 2.1 %image.1 = bf16[512,1024]{1,0:T(8,128)(2,1)} custom-call(bf16[2,256,256]{2,1,0:T(8,128)(2,1)S(1)} %get-tuple-element.29.table_ref, s16[520,128]{1,0:T(8,128)(2,1)S(1)} %collective-permute-done.8.refs_0_, s16[520,128]{1,0:T(8,128)(2,1)S(1)} %collective-permute-done.9.refs_1_, s16[520,128]{1,0:T(8,128)(2,1)S(1)} %collective-permute-done.10.refs_2_, ...), custom_call_target="tpu_custom_call" | custom-call | tf_op jit(solution)/shard_map/image/pallas_call | solution.py:446
Async XLA Ops:
  0.0 32.4 %copy-start = (bf16[4,8,256,128]{3,2,1,0:T(8,128)(2,1)S(1)}, bf16[4,8,256,128]{3,2,1,0:T(8,128)(2,1)}, u32[]{:S(2)}) copy-start(bf16[4,8,256,128]{3,2,1,0:T(8,128)(2,1)} %weights_ref.3) | copy-start | bytes 6291460
  0.0 1.2 %copy-start.1 = (bf16[2,2,256,256]{3,2,1,0:T(8,128)(2,1)S(1)}, bf16[2,2,256,256]{3,2,1,0:T(8,128)(2,1)}, u32[]{:S(2)}) copy-start(bf16[2,2,256,256]{3,2,1,0:T(8,128)(2,1)} %constant.12.clone.table_ref.short_ref) | copy-start | bytes 1572868
  1.2 1.2 %copy-start.3 = (bf16[2,32,8,1024]{3,2,1,0:T(8,128)(2,1)S(1)}, bf16[2,32,8,1024]{3,2,1,0:T(8,128)(2,1)}, u32[]{:S(2)}) copy-start(bf16[2,32,8,1024]{3,2,1,0:T(8,128)(2,1)} %param.5) | copy-start | bytes 3145732
  4.3 9.5 %collective-permute-start = (s16[520,128]{1,0:T(8,128)(2,1)S(1)}, s16[520,128]{1,0:T(8,128)(2,1)S(1)}, u32[]{:S(2)}, u32[]{:S(2)}) collective-permute-start(s16[520,128]{1,0:T(8,128)(2,1)S(1)} %get-tuple-element.31), channel_id=1, source_target_pairs={{0,12},{2,14},{4,8},{6,10},{8,4},{10,6},{12,0},{14,2},{1,13},{3,15... | collective-permute-start | bytes 399368 | tf_op jit(solution)/shard_map/ppermute | solution.py:397
  9.3 9.0 %collective-permute-start.1 = (s16[520,128]{1,0:T(8,128)(2,1)S(1)}, s16[520,128]{1,0:T(8,128)(2,1)S(1)}, u32[]{:S(2)}, u32[]{:S(2)}) collective-permute-start(s16[520,128]{1,0:T(8,128)(2,1)S(1)} %get-tuple-element.32), channel_id=1, source_target_pairs={{0,4},{2,6},{4,0},{6,2},{8,12},{10,14},{12,8},{14,10},{1,5},{3,7},... | collective-permute-start | bytes 399368 | tf_op jit(solution)/shard_map/ppermute | solution.py:397
  9.3 15.5 %collective-permute-start.2 = (s16[520,128]{1,0:T(8,128)(2,1)}, s16[520,128]{1,0:T(8,128)(2,1)S(1)}, u32[]{:S(2)}, u32[]{:S(2)}) collective-permute-start(s16[520,128]{1,0:T(8,128)(2,1)} %get-tuple-element.33), channel_id=1, source_target_pairs={{0,8},{2,10},{4,12},{6,14},{8,0},{10,2},{12,4},{14,6},{1,9},{3,11}... | collective-permute-start | bytes 399368 | tf_op jit(solution)/shard_map/ppermute | solution.py:397
  9.9 21.1 %collective-permute-start.3 = (s16[520,128]{1,0:T(8,128)(2,1)}, s16[520,128]{1,0:T(8,128)(2,1)S(1)}, u32[]{:S(2)}, u32[]{:S(2)}) collective-permute-start(s16[520,128]{1,0:T(8,128)(2,1)} %get-tuple-element.34), channel_id=1, source_target_pairs={{0,10},{2,8},{4,14},{6,12},{8,2},{10,0},{12,6},{14,4},{1,11},{3,9}... | collective-permute-start | bytes 399368 | tf_op jit(solution)/shard_map/ppermute | solution.py:397
  13.2 17.8 %collective-permute-start.4 = (s16[520,128]{1,0:T(8,128)(2,1)}, s16[520,128]{1,0:T(8,128)(2,1)S(1)}, u32[]{:S(2)}, u32[]{:S(2)}) collective-permute-start(s16[520,128]{1,0:T(8,128)(2,1)} %get-tuple-element.35), channel_id=1, source_target_pairs={{0,2},{2,0},{4,6},{6,4},{8,10},{10,8},{12,14},{14,12},{1,3},{3,1},... | collective-permute-start | bytes 399368 | tf_op jit(solution)/shard_map/ppermute | solution.py:397
  13.7 17.3 %collective-permute-start.5 = (s16[520,128]{1,0:T(8,128)(2,1)S(1)}, s16[520,128]{1,0:T(8,128)(2,1)S(1)}, u32[]{:S(2)}, u32[]{:S(2)}) collective-permute-start(s16[520,128]{1,0:T(8,128)(2,1)S(1)} %get-tuple-element.36), channel_id=1, source_target_pairs={{0,6},{2,4},{4,2},{6,0},{8,14},{10,12},{12,10},{14,8},{1,7},{3,5},... | collective-permute-start | bytes 399368 | tf_op jit(solution)/shard_map/ppermute | solution.py:397
  18.4 12.7 %collective-permute-start.6 = (s16[520,128]{1,0:T(8,128)(2,1)S(1)}, s16[520,128]{1,0:T(8,128)(2,1)S(1)}, u32[]{:S(2)}, u32[]{:S(2)}) collective-permute-start(s16[520,128]{1,0:T(8,128)(2,1)S(1)} %get-tuple-element.37), channel_id=1, source_target_pairs={{0,14},{2,12},{4,10},{6,8},{8,6},{10,4},{12,2},{14,0},{1,15},{3,13... | collective-permute-start | bytes 399368 | tf_op jit(solution)/shard_map/ppermute | solution.py:397
  19.6 1.0 %copy-start.2 = (bf16[2,2,256,256]{3,2,1,0:T(8,128)(2,1)S(1)}, bf16[2,2,256,256]{3,2,1,0:T(8,128)(2,1)}, u32[]{:S(2)}) copy-start(bf16[2,2,256,256]{3,2,1,0:T(8,128)(2,1)} %constant.12.clone.table_ref.short_ref) | copy-start | bytes 1572868
  20.7 0.9 %copy-start.4 = (f32[2,128,256]{2,1,0:T(8,128)S(1)}, f32[2,128,256]{2,1,0:T(8,128)}, u32[]{:S(2)}) copy-start(f32[2,128,256]{2,1,0:T(8,128)} %constant.13.clone.base_ref) | copy-start | bytes 786436
  21.6 10.8 %copy-start.5 = (s32[4,16]{1,0:T(4,128)S(1)}, s32[4,16]{1,0:T(4,128)}, u32[]{:S(2)}) copy-start(s32[4,16]{1,0:T(4,128)} %starts_ref.3) | copy-start | bytes 772
  32.3 1.8 %collective-permute-start.7 = (bf16[2,512,128]{2,1,0:T(8,128)(2,1)S(1)}, bf16[2,512,128]{2,1,0:T(8,128)(2,1)S(1)}, u32[]{:S(2)}, u32[]{:S(2)}) collective-permute-start(bf16[2,512,128]{2,1,0:T(8,128)(2,1)S(1)} %get-tuple-element.39), channel_id=1, source_target_pairs={{0,1},{1,0},{2,3},{3,2},{4,5},{5,4},{6,7},{7,6},{8,9},{9,8},{10,11... | collective-permute-start | bytes 786440 | tf_op jit(solution)/shard_map/ppermute | solution.py:429
  36.4 8.5 %collective-permute-start.8 = (s16[520,128]{1,0:T(8,128)(2,1)S(1)}, s16[520,128]{1,0:T(8,128)(2,1)S(1)}, u32[]{:S(2)}, u32[]{:S(2)}) collective-permute-start(s16[520,128]{1,0:T(8,128)(2,1)S(1)} %get-tuple-element.41), channel_id=1, source_target_pairs={{0,12},{2,14},{4,8},{6,10},{8,4},{10,6},{12,0},{14,2},{1,13},{3,15... | collective-permute-start | bytes 399368 | tf_op jit(solution)/shard_map/ppermute | solution.py:397
  38.8 9.3 %collective-permute-start.9 = (s16[520,128]{1,0:T(8,128)(2,1)S(1)}, s16[520,128]{1,0:T(8,128)(2,1)S(1)}, u32[]{:S(2)}, u32[]{:S(2)}) collective-permute-start(s16[520,128]{1,0:T(8,128)(2,1)S(1)} %get-tuple-element.42), channel_id=1, source_target_pairs={{0,4},{2,6},{4,0},{6,2},{8,12},{10,14},{12,8},{14,10},{1,5},{3,7},... | collective-permute-start | bytes 399368 | tf_op jit(solution)/shard_map/ppermute | solution.py:397
  40.5 15.2 %collective-permute-start.10 = (s16[520,128]{1,0:T(8,128)(2,1)S(1)}, s16[520,128]{1,0:T(8,128)(2,1)S(1)}, u32[]{:S(2)}, u32[]{:S(2)}) collective-permute-start(s16[520,128]{1,0:T(8,128)(2,1)S(1)} %get-tuple-element.43), channel_id=1, source_target_pairs={{0,8},{2,10},{4,12},{6,14},{8,0},{10,2},{12,4},{14,6},{1,9},{3,11}... | collective-permute-start | bytes 399368 | tf_op jit(solution)/shard_map/ppermute | solution.py:397
  40.9 20.5 %collective-permute-start.11 = (s16[520,128]{1,0:T(8,128)(2,1)S(1)}, s16[520,128]{1,0:T(8,128)(2,1)S(1)}, u32[]{:S(2)}, u32[]{:S(2)}) collective-permute-start(s16[520,128]{1,0:T(8,128)(2,1)S(1)} %get-tuple-element.44), channel_id=1, source_target_pairs={{0,10},{2,8},{4,14},{6,12},{8,2},{10,0},{12,6},{14,4},{1,11},{3,9}... | collective-permute-start | bytes 399368 | tf_op jit(solution)/shard_map/ppermute | solution.py:397
  43.4 17.9 %collective-permute-start.12 = (s16[520,128]{1,0:T(8,128)(2,1)S(1)}, s16[520,128]{1,0:T(8,128)(2,1)S(1)}, u32[]{:S(2)}, u32[]{:S(2)}) collective-permute-start(s16[520,128]{1,0:T(8,128)(2,1)S(1)} %get-tuple-element.45), channel_id=1, source_target_pairs={{0,2},{2,0},{4,6},{6,4},{8,10},{10,8},{12,14},{14,12},{1,3},{3,1},... | collective-permute-start | bytes 399368 | tf_op jit(solution)/shard_map/ppermute | solution.py:397
  44.9 16.5 %collective-permute-start.13 = (s16[520,128]{1,0:T(8,128)(2,1)S(1)}, s16[520,128]{1,0:T(8,128)(2,1)S(1)}, u32[]{:S(2)}, u32[]{:S(2)}) collective-permute-start(s16[520,128]{1,0:T(8,128)(2,1)S(1)} %get-tuple-element.46), channel_id=1, source_target_pairs={{0,6},{2,4},{4,2},{6,0},{8,14},{10,12},{12,10},{14,8},{1,7},{3,5},... | collective-permute-start | bytes 399368 | tf_op jit(solution)/shard_map/ppermute | solution.py:397
  48.1 13.3 %collective-permute-start.14 = (s16[520,128]{1,0:T(8,128)(2,1)S(1)}, s16[520,128]{1,0:T(8,128)(2,1)S(1)}, u32[]{:S(2)}, u32[]{:S(2)}) collective-permute-start(s16[520,128]{1,0:T(8,128)(2,1)S(1)} %get-tuple-element.47), channel_id=1, source_target_pairs={{0,14},{2,12},{4,10},{6,8},{8,6},{10,4},{12,2},{14,0},{1,15},{3,13... | collective-permute-start | bytes 399368 | tf_op jit(solution)/shard_map/ppermute | solution.py:397

commit v5 on v4

--- a/solution.py
+++ b/solution.py
@@ -147,20 +147,16 @@
     return mm(table[0], pair[0]) + mm(table[0], pair[1]) + mm(table[1], pair[0])
 
 
-def table_pair(table):
-    hi = table.astype(jnp.bfloat16)
-    return np.stack([hi, (table - hi.astype(np.float32)).astype(jnp.bfloat16)])
-
-
-def short_table(upper):
-    k1, co, mo = np.meshgrid(np.arange(8), np.arange(2), np.arange(HALF), indexing="ij")
-    ci, mi, p = np.meshgrid(np.arange(2), np.arange(HALF), np.arange(8), indexing="ij")
-    k1, co, mo = (v.reshape(-1, 1) for v in (k1, co, mo))
-    ci, mi, p = (v.reshape(1, -1) for v in (ci, mi, p))
-    turn = (k1 * (2 * p + upper) + 4 * (co - ci)) % 16
-    unit = np.cos(2 * np.pi * np.arange(16) / 16)
-    unit[[4, 12]] = 0.0
-    return np.where(mo == mi, unit[turn], 0.0).astype(np.float32)
+def short_table(me):
+    row = lax.broadcasted_iota(jnp.int32, (16, 256), 0)
+    column = lax.broadcasted_iota(jnp.int32, (16, 256), 1)
+    residue = (row // 2) ^ me
+    quarter = row % 2 - column // 128
+    turn = (residue * (2 * (column % 8) + me // 4) + 4 * quarter + 16) % 16
+    value = jnp.cos(turn.astype(F32) * (2.0 * math.pi / 16))
+    line = lax.broadcasted_iota(jnp.int32, (HALF, 256), 1) // 8 % HALF
+    same = line == lax.broadcasted_iota(jnp.int32, (HALF, 256), 0)
+    return jnp.concatenate([jnp.where(same, value[n : n + 1], 0.0) for n in range(16)], 0)
 
 
 def long_base():
@@ -223,12 +219,8 @@
     return (1 - 2 * (me // 4)).astype(F32)
 
 
-def spread_kernel(me_ref, x_ref, table_ref, *out_refs):
-    me = me_ref[0]
-    hi, lo = [
-        jnp.concatenate([table_ref[me // 4, part, rows_at(me ^ i, 32), :] for i in range(NDEV)], 0)
-        for part in range(2)
-    ]
+def spread_kernel(me_ref, x_ref, *out_refs):
+    hi, lo = split2(short_table(me_ref[0]))
     halves = []
     for h in range(2):
         at = h * 128
@@ -243,7 +235,7 @@
         store_coded(out_ref, pieces)
 
 
-def tables_kernel(me_ref, base_ref, short_ref, forward_ref, inverse_ref, image_ref):
+def tables_kernel(me_ref, band_ref, base_ref, forward_ref, inverse_ref, image_ref, starts_ref):
     me = me_ref[0]
     step = 2.0 * math.pi / (NDEV * LINES_DEV)
     blocks = []
@@ -264,9 +256,8 @@
         forward = jnp.concatenate([jnp.concatenate([ct, st], 1), jnp.concatenate([-st, ct], 1)], 0)
         for ref, value in ((inverse_ref, inverse), (forward_ref, forward)):
             ref[0, parity], ref[1, parity] = split2(value)
-    for part in range(2):
-        rows = [short_ref[me // 4, part, rows_at(me ^ i, 32), :] for i in range(NDEV)]
-        image_ref[part] = jnp.concatenate(rows, 0).astype(F32).T.astype(BF16)
+    image_ref[0], image_ref[1] = split2(short_table(me).T)
+    starts_ref[...] = band_ref[...]
 
 
 def forward_kernel(me_ref, rg_ref, table_ref, *refs):
@@ -404,20 +395,24 @@
     rg = lax.axis_index("rg").astype(jnp.int32)[None]
     bins = raw.shape[3]
     message = jax.ShapeDtypeStruct((TILES * ROWS + TAIL, TILE), jnp.int16)
-    short = jnp.asarray(np.stack([table_pair(short_table(upper)) for upper in range(2)]))
     long_shape = jax.ShapeDtypeStruct((2, 2, LINES_DEV, LINES_DEV), BF16)
 
-    sent = vmem_call(spread_kernel, "spread", [message] * NDEV, smem=1, vmem=2)(
-        me, raw.reshape(LINES, bins), short
+    sent = vmem_call(spread_kernel, "spread", [message] * NDEV, smem=1, vmem=1)(
+        me, raw.reshape(LINES, bins)
     )
     got = exchange(sent, OUT_ORDER)
-    forward_table, inverse_table, image_table = vmem_call(
+    forward_table, inverse_table, image_table, starts = vmem_call(
         tables_kernel,
         "tables",
-        [long_shape, long_shape, jax.ShapeDtypeStruct((2, 256, 256), BF16)],
+        [
+            long_shape,
+            long_shape,
+            jax.ShapeDtypeStruct((2, 256, 256), BF16),
+            jax.ShapeDtypeStruct(band_start.shape, band_start.dtype),
+        ],
         smem=1,
         vmem=2,
-    )(after(me, sent[0]), jnp.asarray(long_base()), short)
+    )(after(me, sent[0]), band_start, jnp.asarray(long_base()))
 
     spectrum, edge = vmem_call(
         forward_kernel,
@@ -433,7 +428,7 @@
         jax.ShapeDtypeStruct((2, 2, TILES - 1, LINES_DEV, TILE), BF16),
         smem=2,
         vmem=2,
-    )(rg, band_start, spectrum, stolt_weights)
+    )(rg, starts, spectrum, stolt_weights)
     back = vmem_call(
         outer_kernel,
         "outer",
@@ -441,7 +436,7 @@
         smem=3,
         vmem=5,
         scratch=[pltpu.VMEM((3, 2, LINES, TILE), BF16)],
-    )(me, rg, band_start, spectrum, halo, stolt_weights, inverse_table, focus)
+    )(me, rg, starts, spectrum, halo, stolt_weights, inverse_table, focus)
     lines = exchange(back, BACK_ORDER)
     image = vmem_call(image_kernel, "image", jax.ShapeDtypeStruct((LINES, bins), BF16), vmem=1 + NDEV)(
         image_table, *lines

time: 64.3 us -> 63.2 us (0.983)
  local copies, waits for them, and re-layouts: 4.41 us -> 3.01 us
    unnamed x12 -> x8, local copies, waits for them, and re-layouts: 4.41 us -> 3.01 us
  transfers between devices with their start and end apart: 15 -> 15, of which waited for: 4 -> 4; matrix products, arithmetic and copies ran while one was open for 0% -> 0% of each run, Pallas kernels for 3% -> 4%
where the time goes in v5:
time: 63.2 us; the launch traced here: 62.5 us
  starting transfers between devices  30.3 us (48%)
  waiting for transfers between devices  19.3 us (31%)
  Pallas kernels  9.85 us (16%)
  local copies, waits for them, and re-layouts  3.01 us (5%)
    ppermute x14, starting transfers between devices, exchange(): lax.ppermute(messages[i], 'az', [(d, d ^ i) for d in range(NDEV)])  30.2 us
    ppermute x14, waiting for transfers between devices, exchange(): lax.ppermute(messages[i], 'az', [(d, d ^ i) for d in range(NDEV)])  19.3 us
    unnamed x8, local copies, waits for them, and re-layouts  3.01 us
    pallas_call x1, Pallas kernels, fast_body(): vmem_call(outer_kernel, 'outer', [message] * NDEV, smem=3, vmem=5, scratc...  2.35 us
    pallas_call x1, Pallas kernels, fast_body(): vmem_call(image_kernel, 'image', jax.ShapeDtypeStruct((LINES, bins), BF16...  2.06 us
    pallas_call x1, Pallas kernels, fast_body(): vmem_call(spread_kernel, 'spread', [message] * NDEV, smem=1, vmem=1)  1.95 us
    pallas_call x1, Pallas kernels, fast_body(): vmem_call(inner_kernel, 'inner', jax.ShapeDtypeStruct((2, 2, TILES - 1, L...  1.69 us
  transfers between devices with their start and end apart: 15, of which 4 were waited for; matrix products, arithmetic and copies ran while one was open for 0% of the time, Pallas kernels for 4%

profile of v5, /device:TPU:0, one launch (start us, length us, event | category | flops | bytes accessed | tf_op | source)
XLA Modules:
  0.0 62.5 jit_solution(536368869610179)
XLA Ops:
  0.0 0.0 copy-start
  0.0 0.0 copy-start.1
  0.0 1.4 %copy-done.1 = bf16[2,32,8,1024]{3,2,1,0:T(8,128)(2,1)S(1)} copy-done((bf16[2,32,8,1024]{3,2,1,0:T(8,128)(2,1)S(1)}, bf16[2,32,8,1024]{3,2,1,0:T(8,128)(2,1)}, u32[]{:S(2)}) %copy-start.1) | copy-done | bytes 1048600
  1.4 1.9 %spread.1 = (s16[520,128]{1,0:T(8,128)(2,1)S(1)}, s16[520,128]{1,0:T(8,128)(2,1)}, s16[520,128]{1,0:T(8,128)(2,1)S(1)}, s16[520,128]{1,0:T(8,128)(2,1)S(1)}, s16...) custom-call(s32[1]{0:T(128)} %bitcast.me_ref, ...), custom_call_target="tpu_custom_call" | custom-call | tf_op jit(solution)/shard_map/spread/pallas_call | solution.py:400
  3.3 5.1 %collective-permute-start = (s16[520,128]{1,0:T(8,128)(2,1)S(1)}, s16[520,128]{1,0:T(8,128)(2,1)S(1)}, u32[]{:S(2)}, u32[]{:S(2)}) collective-permute-start(s16[520,128]{1,0:T(8,128)(2,1)S(1)} %get-tuple-element.33), channel_id=1, source_target_pairs={{0,12},{2,14},{4,8},{6,10},{8,4},{10,6},{12,0},{14,2},{1,13},{3,15... | collective-permute-start | bytes 399368 | tf_op jit(solution)/shard_map/ppermute | solution.py:388
  8.4 0.0 collective-permute-start.1
  8.4 0.6 collective-permute-start.2
  8.9 3.3 %collective-permute-start.3 = (s16[520,128]{1,0:T(8,128)(2,1)}, s16[520,128]{1,0:T(8,128)(2,1)S(1)}, u32[]{:S(2)}, u32[]{:S(2)}) collective-permute-start(s16[520,128]{1,0:T(8,128)(2,1)} %get-tuple-element.36), channel_id=1, source_target_pairs={{0,10},{2,8},{4,14},{6,12},{8,2},{10,0},{12,6},{14,4},{1,11},{3,9}... | collective-permute-start | bytes 399368 | tf_op jit(solution)/shard_map/ppermute | solution.py:388
  12.2 0.5 collective-permute-start.4
  12.8 0.0 collective-permute-done.refs_0_
  12.8 4.6 %collective-permute-start.5 = (s16[520,128]{1,0:T(8,128)(2,1)S(1)}, s16[520,128]{1,0:T(8,128)(2,1)S(1)}, u32[]{:S(2)}, u32[]{:S(2)}) collective-permute-start(s16[520,128]{1,0:T(8,128)(2,1)S(1)} %get-tuple-element.38), channel_id=1, source_target_pairs={{0,6},{2,4},{4,2},{6,0},{8,14},{10,12},{12,10},{14,8},{1,7},{3,5},... | collective-permute-start | bytes 399368 | tf_op jit(solution)/shard_map/ppermute | solution.py:388
  17.4 0.0 collective-permute-done.1.refs_1_
  17.4 1.3 %collective-permute-start.6 = (s16[520,128]{1,0:T(8,128)(2,1)S(1)}, s16[520,128]{1,0:T(8,128)(2,1)S(1)}, u32[]{:S(2)}, u32[]{:S(2)}) collective-permute-start(s16[520,128]{1,0:T(8,128)(2,1)S(1)} %get-tuple-element.39), channel_id=1, source_target_pairs={{0,14},{2,12},{4,10},{6,8},{8,6},{10,4},{12,2},{14,0},{1,15},{3,13... | collective-permute-start | bytes 399368 | tf_op jit(solution)/shard_map/ppermute | solution.py:388
  18.7 0.0 copy-start.2
  18.7 0.9 %copy-done.2 = f32[2,128,256]{2,1,0:T(8,128)S(1)} copy-done((f32[2,128,256]{2,1,0:T(8,128)S(1)}, f32[2,128,256]{2,1,0:T(8,128)}, u32[]{:S(2)}) %copy-start.2) | copy-done | bytes 262168
  19.6 0.0 copy-start.3
  19.6 0.7 %copy-done.3 = s32[4,16]{1,0:T(4,128)S(1)} copy-done((s32[4,16]{1,0:T(4,128)S(1)}, s32[4,16]{1,0:T(4,128)}, u32[]{:S(2)}) %copy-start.3) | copy-done | bytes 280
  20.3 0.6 tables.1
  20.9 3.0 %collective-permute-done.2.refs_2_ = s16[520,128]{1,0:T(8,128)(2,1)S(1)} collective-permute-done((s16[520,128]{1,0:T(8,128)(2,1)}, s16[520,128]{1,0:T(8,128)(2,1)S(1)}, u32[]{:S(2)}, u32[]{:S(2)}) %collective-permute-start.2) | collective-permute-done | bytes 133152 | tf_op jit(solution)/shard_map/ppermute | solution.py:388
  23.9 6.2 %collective-permute-done.3.refs_3_ = s16[520,128]{1,0:T(8,128)(2,1)S(1)} collective-permute-done((s16[520,128]{1,0:T(8,128)(2,1)}, s16[520,128]{1,0:T(8,128)(2,1)S(1)}, u32[]{:S(2)}, u32[]{:S(2)}) %collective-permute-start.3) | collective-permute-done | bytes 133152 | tf_op jit(solution)/shard_map/ppermute | solution.py:388
  30.1 0.0 collective-permute-done.4.refs_4_
  30.1 0.0 collective-permute-done.5.refs_5_
  30.1 0.0 collective-permute-done.6.refs_6_
  30.1 1.2 %forward.1 = (bf16[8,2,512,128]{3,2,1,0:T(8,128)(2,1)S(1)}, bf16[2,512,128]{2,1,0:T(8,128)(2,1)S(1)}) custom-call(s32[1]{0:T(128)} %bitcast.me_ref, s32[1]{0:T(128)} %bitcast.2.rg_ref, bf16[2,2,256,256]{3,2,1,0:T(8,128)(2,1)S(1)} %get-tuple-element.32.table_ref, s16[520,128]{1,0:T(8,128)(2,1)S(1)} %collective-permute-done.refs_0_, ...), custom_call_target="tpu_custom_call" | custom-call | tf_op jit(solution)/shard_map/forward/pallas_call | solution.py:417
  31.3 0.1 collective-permute-start.7
  31.4 0.0 copy-done
  31.4 1.7 %inner.1.focus_ref = bf16[2,2,7,256,128]{4,3,2,1,0:T(8,128)(2,1)S(1)} custom-call(s32[1]{0:T(128)} %bitcast.2.rg_ref, s32[4,16]{1,0:T(4,128)S(1)} %get-tuple-element.31.starts_ref, bf16[8,2,512,128]{3,2,1,0:T(8,128)(2,1)S(1)} %get-tuple-element.40.spectrum_ref, bf16[4,8,256,128]{3,2,1,0:T(8,128)(2,1)S(1)} %copy-done), custom_call_target="tpu_custom_call" | custom-call | tf_op jit(solution)/shard_map/inner/pallas_call | solution.py:425
  33.1 0.0 collective-permute-done.7.halo_ref
  33.1 2.3 %outer.1 = (s16[520,128]{1,0:T(8,128)(2,1)S(1)}, s16[520,128]{1,0:T(8,128)(2,1)S(1)}, s16[520,128]{1,0:T(8,128)(2,1)S(1)}, s16[520,128]{1,0:T(8,128)(2,1)S(1)}, ...) custom-call(s32[1]{0:T(128)} %bitcast.me_ref, ...), custom_call_target="tpu_custom_call" | custom-call | tf_op jit(solution)/shard_map/outer/pallas_call | solution.py:432
  35.5 2.4 %collective-permute-start.8 = (s16[520,128]{1,0:T(8,128)(2,1)S(1)}, s16[520,128]{1,0:T(8,128)(2,1)S(1)}, u32[]{:S(2)}, u32[]{:S(2)}) collective-permute-start(s16[520,128]{1,0:T(8,128)(2,1)S(1)} %get-tuple-element.43), channel_id=1, source_target_pairs={{0,12},{2,14},{4,8},{6,10},{8,4},{10,6},{12,0},{14,2},{1,13},{3,15... | collective-permute-start | bytes 399368 | tf_op jit(solution)/shard_map/ppermute | solution.py:388
  37.9 1.7 %collective-permute-start.9 = (s16[520,128]{1,0:T(8,128)(2,1)S(1)}, s16[520,128]{1,0:T(8,128)(2,1)S(1)}, u32[]{:S(2)}, u32[]{:S(2)}) collective-permute-start(s16[520,128]{1,0:T(8,128)(2,1)S(1)} %get-tuple-element.44), channel_id=1, source_target_pairs={{0,4},{2,6},{4,0},{6,2},{8,12},{10,14},{12,8},{14,10},{1,5},{3,7},... | collective-permute-start | bytes 399368 | tf_op jit(solution)/shard_map/ppermute | solution.py:388
  39.6 0.4 collective-permute-start.10
  39.9 2.5 %collective-permute-start.11 = (s16[520,128]{1,0:T(8,128)(2,1)S(1)}, s16[520,128]{1,0:T(8,128)(2,1)S(1)}, u32[]{:S(2)}, u32[]{:S(2)}) collective-permute-start(s16[520,128]{1,0:T(8,128)(2,1)S(1)} %get-tuple-element.46), channel_id=1, source_target_pairs={{0,10},{2,8},{4,14},{6,12},{8,2},{10,0},{12,6},{14,4},{1,11},{3,9}... | collective-permute-start | bytes 399368 | tf_op jit(solution)/shard_map/ppermute | solution.py:388
  42.5 1.5 %collective-permute-start.12 = (s16[520,128]{1,0:T(8,128)(2,1)S(1)}, s16[520,128]{1,0:T(8,128)(2,1)S(1)}, u32[]{:S(2)}, u32[]{:S(2)}) collective-permute-start(s16[520,128]{1,0:T(8,128)(2,1)S(1)} %get-tuple-element.47), channel_id=1, source_target_pairs={{0,2},{2,0},{4,6},{6,4},{8,10},{10,8},{12,14},{14,12},{1,3},{3,1},... | collective-permute-start | bytes 399368 | tf_op jit(solution)/shard_map/ppermute | solution.py:388
  44.0 0.0 collective-permute-done.8.refs_0_
  44.0 3.1 %collective-permute-start.13 = (s16[520,128]{1,0:T(8,128)(2,1)S(1)}, s16[520,128]{1,0:T(8,128)(2,1)S(1)}, u32[]{:S(2)}, u32[]{:S(2)}) collective-permute-start(s16[520,128]{1,0:T(8,128)(2,1)S(1)} %get-tuple-element.48), channel_id=1, source_target_pairs={{0,6},{2,4},{4,2},{6,0},{8,14},{10,12},{12,10},{14,8},{1,7},{3,5},... | collective-permute-start | bytes 399368 | tf_op jit(solution)/shard_map/ppermute | solution.py:388
  47.1 0.0 collective-permute-done.9.refs_1_
  47.1 3.3 %collective-permute-start.14 = (s16[520,128]{1,0:T(8,128)(2,1)S(1)}, s16[520,128]{1,0:T(8,128)(2,1)S(1)}, u32[]{:S(2)}, u32[]{:S(2)}) collective-permute-start(s16[520,128]{1,0:T(8,128)(2,1)S(1)} %get-tuple-element.49), channel_id=1, source_target_pairs={{0,14},{2,12},{4,10},{6,8},{8,6},{10,4},{12,2},{14,0},{1,15},{3,13... | collective-permute-start | bytes 399368 | tf_op jit(solution)/shard_map/ppermute | solution.py:388
  50.4 4.4 %collective-permute-done.10.refs_2_ = s16[520,128]{1,0:T(8,128)(2,1)S(1)} collective-permute-done((s16[520,128]{1,0:T(8,128)(2,1)S(1)}, s16[520,128]{1,0:T(8,128)(2,1)S(1)}, u32[]{:S(2)}, u32[]{:S(2)}) %collective-permute-start.10) | collective-permute-done | bytes 133152 | tf_op jit(solution)/shard_map/ppermute | solution.py:388
  54.7 5.7 %collective-permute-done.11.refs_3_ = s16[520,128]{1,0:T(8,128)(2,1)S(1)} collective-permute-done((s16[520,128]{1,0:T(8,128)(2,1)S(1)}, s16[520,128]{1,0:T(8,128)(2,1)S(1)}, u32[]{:S(2)}, u32[]{:S(2)}) %collective-permute-start.11) | collective-permute-done | bytes 133152 | tf_op jit(solution)/shard_map/ppermute | solution.py:388
  60.4 0.0 collective-permute-done.12.refs_4_
  60.4 0.0 collective-permute-done.13.refs_5_
  60.4 0.0 collective-permute-done.14.refs_6_
  60.4 2.1 %image.1 = bf16[512,1024]{1,0:T(8,128)(2,1)} custom-call(bf16[2,256,256]{2,1,0:T(8,128)(2,1)S(1)} %get-tuple-element.30.table_ref, s16[520,128]{1,0:T(8,128)(2,1)S(1)} %collective-permute-done.8.refs_0_, s16[520,128]{1,0:T(8,128)(2,1)S(1)} %collective-permute-done.9.refs_1_, s16[520,128]{1,0:T(8,128)(2,1)S(1)} %collective-permute-done.10.refs_2_, ...), custom_call_target="tpu_custom_call" | custom-call | tf_op jit(solution)/shard_map/image/pallas_call | solution.py:441
Async XLA Ops:
  0.0 31.4 %copy-start = (bf16[4,8,256,128]{3,2,1,0:T(8,128)(2,1)S(1)}, bf16[4,8,256,128]{3,2,1,0:T(8,128)(2,1)}, u32[]{:S(2)}) copy-start(bf16[4,8,256,128]{3,2,1,0:T(8,128)(2,1)} %weights_ref.3) | copy-start | bytes 6291460
  0.0 1.4 %copy-start.1 = (bf16[2,32,8,1024]{3,2,1,0:T(8,128)(2,1)S(1)}, bf16[2,32,8,1024]{3,2,1,0:T(8,128)(2,1)}, u32[]{:S(2)}) copy-start(bf16[2,32,8,1024]{3,2,1,0:T(8,128)(2,1)} %param.4) | copy-start | bytes 3145732
  3.3 9.5 %collective-permute-start = (s16[520,128]{1,0:T(8,128)(2,1)S(1)}, s16[520,128]{1,0:T(8,128)(2,1)S(1)}, u32[]{:S(2)}, u32[]{:S(2)}) collective-permute-start(s16[520,128]{1,0:T(8,128)(2,1)S(1)} %get-tuple-element.33), channel_id=1, source_target_pairs={{0,12},{2,14},{4,8},{6,10},{8,4},{10,6},{12,0},{14,2},{1,13},{3,15... | collective-permute-start | bytes 399368 | tf_op jit(solution)/shard_map/ppermute | solution.py:388
  8.4 9.0 %collective-permute-start.1 = (s16[520,128]{1,0:T(8,128)(2,1)S(1)}, s16[520,128]{1,0:T(8,128)(2,1)S(1)}, u32[]{:S(2)}, u32[]{:S(2)}) collective-permute-start(s16[520,128]{1,0:T(8,128)(2,1)S(1)} %get-tuple-element.34), channel_id=1, source_target_pairs={{0,4},{2,6},{4,0},{6,2},{8,12},{10,14},{12,8},{14,10},{1,5},{3,7},... | collective-permute-start | bytes 399368 | tf_op jit(solution)/shard_map/ppermute | solution.py:388
  8.4 15.5 %collective-permute-start.2 = (s16[520,128]{1,0:T(8,128)(2,1)}, s16[520,128]{1,0:T(8,128)(2,1)S(1)}, u32[]{:S(2)}, u32[]{:S(2)}) collective-permute-start(s16[520,128]{1,0:T(8,128)(2,1)} %get-tuple-element.35), channel_id=1, source_target_pairs={{0,8},{2,10},{4,12},{6,14},{8,0},{10,2},{12,4},{14,6},{1,9},{3,11}... | collective-permute-start | bytes 399368 | tf_op jit(solution)/shard_map/ppermute | solution.py:388
  8.9 21.1 %collective-permute-start.3 = (s16[520,128]{1,0:T(8,128)(2,1)}, s16[520,128]{1,0:T(8,128)(2,1)S(1)}, u32[]{:S(2)}, u32[]{:S(2)}) collective-permute-start(s16[520,128]{1,0:T(8,128)(2,1)} %get-tuple-element.36), channel_id=1, source_target_pairs={{0,10},{2,8},{4,14},{6,12},{8,2},{10,0},{12,6},{14,4},{1,11},{3,9}... | collective-permute-start | bytes 399368 | tf_op jit(solution)/shard_map/ppermute | solution.py:388
  12.2 17.8 %collective-permute-start.4 = (s16[520,128]{1,0:T(8,128)(2,1)}, s16[520,128]{1,0:T(8,128)(2,1)S(1)}, u32[]{:S(2)}, u32[]{:S(2)}) collective-permute-start(s16[520,128]{1,0:T(8,128)(2,1)} %get-tuple-element.37), channel_id=1, source_target_pairs={{0,2},{2,0},{4,6},{6,4},{8,10},{10,8},{12,14},{14,12},{1,3},{3,1},... | collective-permute-start | bytes 399368 | tf_op jit(solution)/shard_map/ppermute | solution.py:388
  12.8 17.3 %collective-permute-start.5 = (s16[520,128]{1,0:T(8,128)(2,1)S(1)}, s16[520,128]{1,0:T(8,128)(2,1)S(1)}, u32[]{:S(2)}, u32[]{:S(2)}) collective-permute-start(s16[520,128]{1,0:T(8,128)(2,1)S(1)} %get-tuple-element.38), channel_id=1, source_target_pairs={{0,6},{2,4},{4,2},{6,0},{8,14},{10,12},{12,10},{14,8},{1,7},{3,5},... | collective-permute-start | bytes 399368 | tf_op jit(solution)/shard_map/ppermute | solution.py:388
  17.4 12.7 %collective-permute-start.6 = (s16[520,128]{1,0:T(8,128)(2,1)S(1)}, s16[520,128]{1,0:T(8,128)(2,1)S(1)}, u32[]{:S(2)}, u32[]{:S(2)}) collective-permute-start(s16[520,128]{1,0:T(8,128)(2,1)S(1)} %get-tuple-element.39), channel_id=1, source_target_pairs={{0,14},{2,12},{4,10},{6,8},{8,6},{10,4},{12,2},{14,0},{1,15},{3,13... | collective-permute-start | bytes 399368 | tf_op jit(solution)/shard_map/ppermute | solution.py:388
  18.7 0.9 %copy-start.2 = (f32[2,128,256]{2,1,0:T(8,128)S(1)}, f32[2,128,256]{2,1,0:T(8,128)}, u32[]{:S(2)}) copy-start(f32[2,128,256]{2,1,0:T(8,128)} %constant.10.clone.base_ref) | copy-start | bytes 786436
  19.6 0.7 %copy-start.3 = (s32[4,16]{1,0:T(4,128)S(1)}, s32[4,16]{1,0:T(4,128)}, u32[]{:S(2)}) copy-start(s32[4,16]{1,0:T(4,128)} %band_ref.1) | copy-start | bytes 772
  31.3 1.8 %collective-permute-start.7 = (bf16[2,512,128]{2,1,0:T(8,128)(2,1)S(1)}, bf16[2,512,128]{2,1,0:T(8,128)(2,1)S(1)}, u32[]{:S(2)}, u32[]{:S(2)}) collective-permute-start(bf16[2,512,128]{2,1,0:T(8,128)(2,1)S(1)} %get-tuple-element.41), channel_id=1, source_target_pairs={{0,1},{1,0},{2,3},{3,2},{4,5},{5,4},{6,7},{7,6},{8,9},{9,8},{10,11... | collective-permute-start | bytes 786440 | tf_op jit(solution)/shard_map/ppermute | solution.py:424
  35.5 8.5 %collective-permute-start.8 = (s16[520,128]{1,0:T(8,128)(2,1)S(1)}, s16[520,128]{1,0:T(8,128)(2,1)S(1)}, u32[]{:S(2)}, u32[]{:S(2)}) collective-permute-start(s16[520,128]{1,0:T(8,128)(2,1)S(1)} %get-tuple-element.43), channel_id=1, source_target_pairs={{0,12},{2,14},{4,8},{6,10},{8,4},{10,6},{12,0},{14,2},{1,13},{3,15... | collective-permute-start | bytes 399368 | tf_op jit(solution)/shard_map/ppermute | solution.py:388
  37.9 9.2 %collective-permute-start.9 = (s16[520,128]{1,0:T(8,128)(2,1)S(1)}, s16[520,128]{1,0:T(8,128)(2,1)S(1)}, u32[]{:S(2)}, u32[]{:S(2)}) collective-permute-start(s16[520,128]{1,0:T(8,128)(2,1)S(1)} %get-tuple-element.44), channel_id=1, source_target_pairs={{0,4},{2,6},{4,0},{6,2},{8,12},{10,14},{12,8},{14,10},{1,5},{3,7},... | collective-permute-start | bytes 399368 | tf_op jit(solution)/shard_map/ppermute | solution.py:388
  39.6 15.2 %collective-permute-start.10 = (s16[520,128]{1,0:T(8,128)(2,1)S(1)}, s16[520,128]{1,0:T(8,128)(2,1)S(1)}, u32[]{:S(2)}, u32[]{:S(2)}) collective-permute-start(s16[520,128]{1,0:T(8,128)(2,1)S(1)} %get-tuple-element.45), channel_id=1, source_target_pairs={{0,8},{2,10},{4,12},{6,14},{8,0},{10,2},{12,4},{14,6},{1,9},{3,11}... | collective-permute-start | bytes 399368 | tf_op jit(solution)/shard_map/ppermute | solution.py:388
  39.9 20.5 %collective-permute-start.11 = (s16[520,128]{1,0:T(8,128)(2,1)S(1)}, s16[520,128]{1,0:T(8,128)(2,1)S(1)}, u32[]{:S(2)}, u32[]{:S(2)}) collective-permute-start(s16[520,128]{1,0:T(8,128)(2,1)S(1)} %get-tuple-element.46), channel_id=1, source_target_pairs={{0,10},{2,8},{4,14},{6,12},{8,2},{10,0},{12,6},{14,4},{1,11},{3,9}... | collective-permute-start | bytes 399368 | tf_op jit(solution)/shard_map/ppermute | solution.py:388
  42.5 17.9 %collective-permute-start.12 = (s16[520,128]{1,0:T(8,128)(2,1)S(1)}, s16[520,128]{1,0:T(8,128)(2,1)S(1)}, u32[]{:S(2)}, u32[]{:S(2)}) collective-permute-start(s16[520,128]{1,0:T(8,128)(2,1)S(1)} %get-tuple-element.47), channel_id=1, source_target_pairs={{0,2},{2,0},{4,6},{6,4},{8,10},{10,8},{12,14},{14,12},{1,3},{3,1},... | collective-permute-start | bytes 399368 | tf_op jit(solution)/shard_map/ppermute | solution.py:388
  44.0 16.4 %collective-permute-start.13 = (s16[520,128]{1,0:T(8,128)(2,1)S(1)}, s16[520,128]{1,0:T(8,128)(2,1)S(1)}, u32[]{:S(2)}, u32[]{:S(2)}) collective-permute-start(s16[520,128]{1,0:T(8,128)(2,1)S(1)} %get-tuple-element.48), channel_id=1, source_target_pairs={{0,6},{2,4},{4,2},{6,0},{8,14},{10,12},{12,10},{14,8},{1,7},{3,5},... | collective-permute-start | bytes 399368 | tf_op jit(solution)/shard_map/ppermute | solution.py:388
  47.1 13.3 %collective-permute-start.14 = (s16[520,128]{1,0:T(8,128)(2,1)S(1)}, s16[520,128]{1,0:T(8,128)(2,1)S(1)}, u32[]{:S(2)}, u32[]{:S(2)}) collective-permute-start(s16[520,128]{1,0:T(8,128)(2,1)S(1)} %get-tuple-element.49), channel_id=1, source_target_pairs={{0,14},{2,12},{4,10},{6,8},{8,6},{10,4},{12,2},{14,0},{1,15},{3,13... | collective-permute-start | bytes 399368 | tf_op jit(solution)/shard_map/ppermute | solution.py:388

commit v6 on v5

--- a/solution.py
+++ b/solution.py
@@ -128,8 +128,9 @@
 TILES = 8
 LINES = 2 * LINES_DEV
 SIDE = LINES_DEV // 2
-OUT_ORDER = (6, 2, 4, 5, 1, 3, 7, 0)
-BACK_ORDER = (6, 2, 4, 5, 1, 3, 7, 0)
+EARLY = (6, 2, 4, 5, 1, 0)
+LATE = (3, 7)
+EARLY_ROWS = 192
 VMEM_LIMIT = 20 * 1024 * 1024
 
 
@@ -211,8 +212,13 @@
     return [(t, t + 1) for t in range(0, tiles, 2)]
 
 
-def in_order(refs, order):
-    return [refs[order.index(i)] for i in range(NDEV)]
+def stacked3(pair):
+    return jnp.concatenate([pair[0], pair[1], pair[0]], 0)
+
+
+def late_table(rows):
+    hi, lo = (v.astype(F32) for v in split2(rows))
+    return jnp.concatenate([hi, hi, lo], 0).T.astype(BF16)
 
 
 def sign_of(me):
@@ -235,7 +241,8 @@
         store_coded(out_ref, pieces)
 
 
-def tables_kernel(me_ref, band_ref, base_ref, forward_ref, inverse_ref, image_ref, starts_ref):
+def tables_kernel(me_ref, band_ref, base_ref, *refs):
+    forward_ref, forward_late_ref, inverse_ref, image_ref, image_late_ref, starts_ref = refs
     me = me_ref[0]
     step = 2.0 * math.pi / (NDEV * LINES_DEV)
     blocks = []
@@ -252,25 +259,46 @@
     for parity in range(2):
         co, si = [w[:, parity * SIDE : (parity + 1) * SIDE] for w in whole]
         inverse = jnp.concatenate([jnp.concatenate([co, -si], 1), jnp.concatenate([si, co], 1)], 0)
-        ct, st = co.T * 2.0, si.T * 2.0
-        forward = jnp.concatenate([jnp.concatenate([ct, st], 1), jnp.concatenate([-st, ct], 1)], 0)
-        for ref, value in ((inverse_ref, inverse), (forward_ref, forward)):
-            ref[0, parity], ref[1, parity] = split2(value)
-    image_ref[0], image_ref[1] = split2(short_table(me).T)
+        inverse_ref[0, parity], inverse_ref[1, parity] = split2(inverse)
+        early = jnp.concatenate([inverse[:96], inverse[128:224]], 0).T * 2.0
+        forward_ref[0, parity], forward_ref[1, parity] = split2(early)
+        forward_late_ref[parity] = late_table(jnp.concatenate([inverse[96:128], inverse[224:]], 0) * 2.0)
+    short = short_table(me)
+    early, late = [
+        jnp.concatenate([short[i * 32 : (i + 1) * 32] for i in which], 0) for which in (EARLY, LATE)
+    ]
+    image_ref[0], image_ref[1] = split2(early.T)
+    image_late_ref[...] = late_table(late)
     starts_ref[...] = band_ref[...]
 
 
-def forward_kernel(me_ref, rg_ref, table_ref, *refs):
-    in_refs, (out_ref, edge_ref) = in_order(refs[:NDEV], OUT_ORDER), refs[NDEV:]
+def side_lines(values, pairs, sign):
+    sums = [values[i] + values[i + 4] for i in pairs]
+    gaps = [(values[i] - values[i + 4]) * sign for i in pairs]
+    for lines in (sums, gaps):
+        yield split2(jnp.concatenate([v[:MLOC] for v in lines] + [v[MLOC:] for v in lines], 0))
+
+
+def forward_early_kernel(me_ref, table_ref, *refs):
+    in_refs, sum_ref = dict(zip(EARLY, refs)), refs[len(EARLY)]
     sign = sign_of(me_ref[0])
-    scales = [load_scales(ref) for ref in in_refs]
+    scales = {i: load_scales(ref) for i, ref in in_refs.items()}
     for tiles in tile_pairs(TILES):
-        values = [load_columns(ref, scale, tiles) for ref, scale in zip(in_refs, scales)]
-        sums = [values[i] + values[i + 4] for i in range(4)]
-        gaps = [(values[i] - values[i + 4]) * sign for i in range(4)]
-        for parity, lines in enumerate((sums, gaps)):
-            lines = jnp.concatenate([v[:MLOC] for v in lines] + [v[MLOC:] for v in lines], 0)
-            result = product3((table_ref[0, parity], table_ref[1, parity]), split2(lines))
+        values = {i: load_columns(ref, scales[i], tiles) for i, ref in in_refs.items()}
+        for parity, pair in enumerate(side_lines(values, (0, 1, 2), sign)):
+            columns = slice(tiles[0] * TILE, (tiles[0] + 2) * TILE)
+            sum_ref[parity, :, columns] = product3((table_ref[0, parity], table_ref[1, parity]), pair)
+
+
+def forward_kernel(me_ref, rg_ref, table_ref, sum_ref, *refs):
+    in_refs, (out_ref, edge_ref) = dict(zip(LATE, refs)), refs[len(LATE) :]
+    sign = sign_of(me_ref[0])
+    scales = {i: load_scales(ref) for i, ref in in_refs.items()}
+    for tiles in tile_pairs(TILES):
+        values = {i: load_columns(ref, scales[i], tiles) for i, ref in in_refs.items()}
+        for parity, pair in enumerate(side_lines(values, (3,), sign)):
+            columns = slice(tiles[0] * TILE, (tiles[0] + 2) * TILE)
+            result = sum_ref[parity, :, columns] + mm(table_ref[parity], stacked3(pair))
             for at, t in enumerate(tiles):
                 for part, half in enumerate(split2(result[:, at * TILE : (at + 1) * TILE])):
                     out_ref[t, part, parity * 256 : (parity + 1) * 256, :] = half
@@ -350,20 +378,32 @@
         store_coded(out_ref, pieces)
 
 
-def image_kernel(table_ref, *refs):
-    in_refs, out_ref = in_order(refs[:NDEV], BACK_ORDER), refs[NDEV]
+def image_lines(values, h):
+    rows = [v[c * MLOC + h * HALF : c * MLOC + (h + 1) * HALF] for v in values for c in range(2)]
+    return split2(jnp.concatenate(rows, 0))
+
+
+def image_early_kernel(table_ref, *refs):
+    in_refs, sum_ref = refs[: len(EARLY)], refs[len(EARLY)]
     scales = [load_scales(ref) for ref in in_refs]
     for tiles in tile_pairs(TILES):
         values = [load_columns(ref, scale, tiles) for ref, scale in zip(in_refs, scales)]
         for h in range(2):
-            x = jnp.concatenate(
-                [v[c * MLOC + h * HALF : c * MLOC + (h + 1) * HALF] for v in values for c in range(2)], 0
-            )
-            result = product3(table_ref, split2(x)).astype(BF16)
+            columns = slice(tiles[0] * TILE, (tiles[0] + 2) * TILE)
+            sum_ref[h, :, columns] = product3(table_ref, image_lines(values, h))
+
+
+def image_kernel(table_ref, sum_ref, *refs):
+    in_refs, out_ref = refs[: len(LATE)], refs[len(LATE)]
+    scales = [load_scales(ref) for ref in in_refs]
+    for tiles in tile_pairs(TILES):
+        values = [load_columns(ref, scale, tiles) for ref, scale in zip(in_refs, scales)]
+        for h in range(2):
+            columns = slice(tiles[0] * TILE, (tiles[0] + 2) * TILE)
+            result = sum_ref[h, :, columns] + mm(table_ref[...], stacked3(image_lines(values, h)))
             for c in range(2):
                 at = c * 256 + h * 128
-                columns = slice(tiles[0] * TILE, (tiles[0] + 2) * TILE)
-                out_ref[at : at + 128, columns] = result[c * 128 : (c + 1) * 128]
+                out_ref[at : at + 128, columns] = result[c * 128 : (c + 1) * 128].astype(BF16)
 
 
 def vmem_call(kernel, name, out_shape, smem=0, vmem=0, scratch=()):
@@ -383,10 +423,13 @@
     return lax.optimization_barrier((value, *others))[0]
 
 
-def exchange(messages, order):
+def exchange(messages):
     return [
-        lax.ppermute(messages[i], "az", [(d, d ^ i) for d in range(NDEV)]) if i else messages[0]
-        for i in order
+        [
+            lax.ppermute(messages[i], "az", [(d, d ^ i) for d in range(NDEV)]) if i else messages[0]
+            for i in which
+        ]
+        for which in (EARLY, LATE)
     ]
 
 
@@ -395,32 +438,41 @@
     rg = lax.axis_index("rg").astype(jnp.int32)[None]
     bins = raw.shape[3]
     message = jax.ShapeDtypeStruct((TILES * ROWS + TAIL, TILE), jnp.int16)
-    long_shape = jax.ShapeDtypeStruct((2, 2, LINES_DEV, LINES_DEV), BF16)
+    early_shape = (2, LINES_DEV, EARLY_ROWS)
 
     sent = vmem_call(spread_kernel, "spread", [message] * NDEV, smem=1, vmem=1)(
         me, raw.reshape(LINES, bins)
     )
-    got = exchange(sent, OUT_ORDER)
-    forward_table, inverse_table, image_table, starts = vmem_call(
+    got_early, got_late = exchange(sent)
+    forward_table, forward_late, inverse_table, image_table, image_late, starts = vmem_call(
         tables_kernel,
         "tables",
         [
-            long_shape,
-            long_shape,
-            jax.ShapeDtypeStruct((2, 256, 256), BF16),
+            jax.ShapeDtypeStruct((2,) + early_shape, BF16),
+            jax.ShapeDtypeStruct(early_shape, BF16),
+            jax.ShapeDtypeStruct((2, 2, LINES_DEV, LINES_DEV), BF16),
+            jax.ShapeDtypeStruct((2, 256, EARLY_ROWS), BF16),
+            jax.ShapeDtypeStruct((256, EARLY_ROWS), BF16),
             jax.ShapeDtypeStruct(band_start.shape, band_start.dtype),
         ],
         smem=1,
         vmem=2,
     )(after(me, sent[0]), band_start, jnp.asarray(long_base()))
 
+    partial = vmem_call(
+        forward_early_kernel,
+        "forward_early",
+        jax.ShapeDtypeStruct((2, LINES_DEV, bins), F32),
+        smem=1,
+        vmem=1 + len(EARLY),
+    )(me, forward_table, *got_early)
     spectrum, edge = vmem_call(
         forward_kernel,
         "forward",
         [jax.ShapeDtypeStruct((TILES, 2, LINES, TILE), BF16), jax.ShapeDtypeStruct((2, LINES, TILE), BF16)],
         smem=2,
-        vmem=1 + NDEV,
-    )(me, rg, forward_table, *got)
+        vmem=2 + len(LATE),
+    )(me, rg, forward_late, partial, *got_late)
     halo = lax.ppermute(edge, "rg", [(0, 1), (1, 0)])
     focus = vmem_call(
         inner_kernel,
@@ -437,10 +489,13 @@
         vmem=5,
         scratch=[pltpu.VMEM((3, 2, LINES, TILE), BF16)],
     )(me, rg, starts, spectrum, halo, stolt_weights, inverse_table, focus)
-    lines = exchange(back, BACK_ORDER)
-    image = vmem_call(image_kernel, "image", jax.ShapeDtypeStruct((LINES, bins), BF16), vmem=1 + NDEV)(
-        image_table, *lines
-    )
+    early_lines, late_lines = exchange(back)
+    image_sum = vmem_call(
+        image_early_kernel, "image_early", jax.ShapeDtypeStruct((2, 256, bins), F32), vmem=1 + len(EARLY)
+    )(image_table, *early_lines)
+    image = vmem_call(
+        image_kernel, "image", jax.ShapeDtypeStruct((LINES, bins), BF16), vmem=2 + len(LATE)
+    )(image_late, image_sum, *late_lines)
     return image.reshape(2, MLOC, NDEV, bins)
 
 

time: 63.2 us -> 62.1 us (0.983)
  starting transfers between devices: 30.3 us -> 27.6 us
  waiting for transfers between devices: 19.3 us -> 20.2 us
  local copies, waits for them, and re-layouts: 3.01 us -> 3.82 us
    ppermute x14, starting transfers between devices: 30.2 us -> 27.5 us  [exchange(): lax.ppermute(messages[i], 'az', [(d, d ^ i) for d in range(NDEV)])]
    pallas_call x1 -> x3, Pallas kernels: 0.57 us -> 2.83 us  [the longest x1 1.07 us: fast_body(): vmem_call(forward_early_kernel, 'forward_early', jax.ShapeDtypeStruct((2,...]
    ppermute x14, waiting for transfers between devices: 19.3 us -> 20.2 us  [exchange(): lax.ppermute(messages[i], 'az', [(d, d ^ i) for d in range(NDEV)])]
    unnamed x8, local copies, waits for them, and re-layouts: 3.01 us -> 3.82 us
    pallas_call x1, Pallas kernels: 1.24 us -> 0.51 us  [fast_body(): vmem_call(forward_kernel, 'forward', [jax.ShapeDtypeStruct((TILES, 2, LIN...]
    pallas_call x1, Pallas kernels: 2.06 us -> 1.42 us  [fast_body(): vmem_call(image_kernel, 'image', jax.ShapeDtypeStruct((LINES, bins), BF16...]
  transfers between devices with their start and end apart: 15 -> 15, of which waited for: 4 -> 6; matrix products, arithmetic and copies ran while one was open for 0% -> 0% of each run, Pallas kernels for 4% -> 7%
where the time goes in v6:
time: 62.1 us; the launch traced here: 61.9 us
  starting transfers between devices  27.6 us (44%)
  waiting for transfers between devices  20.2 us (33%)
  Pallas kernels  10.1 us (16%)
  local copies, waits for them, and re-layouts  3.82 us (6%)
    ppermute x14, starting transfers between devices, exchange(): lax.ppermute(messages[i], 'az', [(d, d ^ i) for d in range(NDEV)])  27.5 us
    ppermute x14, waiting for transfers between devices, exchange(): lax.ppermute(messages[i], 'az', [(d, d ^ i) for d in range(NDEV)])  20.2 us
    unnamed x8, local copies, waits for them, and re-layouts  3.82 us
    pallas_call x1, Pallas kernels, fast_body(): vmem_call(outer_kernel, 'outer', [message] * NDEV, smem=3, vmem=5, scratc...  2.36 us
    pallas_call x1, Pallas kernels, fast_body(): vmem_call(inner_kernel, 'inner', jax.ShapeDtypeStruct((2, 2, TILES - 1, L...  1.67 us
    pallas_call x1, Pallas kernels, fast_body(): vmem_call(image_kernel, 'image', jax.ShapeDtypeStruct((LINES, bins), BF16...  1.42 us
    pallas_call x1, Pallas kernels, fast_body(): vmem_call(spread_kernel, 'spread', [message] * NDEV, smem=1, vmem=1)  1.32 us
  transfers between devices with their start and end apart: 15, of which 6 were waited for; matrix products, arithmetic and copies ran while one was open for 0% of the time, Pallas kernels for 7%

profile of v6, /device:TPU:0, one launch (start us, length us, event | category | flops | bytes accessed | tf_op | source)
XLA Modules:
  0.0 61.9 jit_solution(5582107309161338352)
XLA Ops:
  0.0 0.0 copy-start.1
  0.0 1.2 %copy-done.1 = bf16[2,32,8,1024]{3,2,1,0:T(8,128)(2,1)S(1)} copy-done((bf16[2,32,8,1024]{3,2,1,0:T(8,128)(2,1)S(1)}, bf16[2,32,8,1024]{3,2,1,0:T(8,128)(2,1)}, u32[]{:S(2)}) %copy-start.1) | copy-done | bytes 1048600
  1.2 1.3 %spread.1 = (s16[520,128]{1,0:T(8,128)(2,1)S(1)}, s16[520,128]{1,0:T(8,128)(2,1)S(1)}, s16[520,128]{1,0:T(8,128)(2,1)S(1)}, s16[520,128]{1,0:T(8,128)(2,1)S(1)},...) custom-call(s32[1]{0:T(128)} %bitcast.me_ref, ...), custom_call_target="tpu_custom_call" | custom-call | tf_op jit(solution)/shard_map/spread/pallas_call | solution.py:443
  2.6 5.1 %collective-permute-start = (s16[520,128]{1,0:T(8,128)(2,1)S(1)}, s16[520,128]{1,0:T(8,128)(2,1)S(1)}, u32[]{:S(2)}, u32[]{:S(2)}) collective-permute-start(s16[520,128]{1,0:T(8,128)(2,1)S(1)} %get-tuple-element.37), channel_id=1, source_target_pairs={{0,12},{2,14},{4,8},{6,10},{8,4},{10,6},{12,0},{14,2},{1,13},{3,15... | collective-permute-start | bytes 399368 | tf_op jit(solution)/shard_map/ppermute | solution.py:429
  7.7 0.0 collective-permute-start.1
  7.7 0.6 %collective-permute-start.2 = (s16[520,128]{1,0:T(8,128)(2,1)S(1)}, s16[520,128]{1,0:T(8,128)(2,1)S(1)}, u32[]{:S(2)}, u32[]{:S(2)}) collective-permute-start(s16[520,128]{1,0:T(8,128)(2,1)S(1)} %get-tuple-element.39), channel_id=1, source_target_pairs={{0,8},{2,10},{4,12},{6,14},{8,0},{10,2},{12,4},{14,6},{1,9},{3,11}... | collective-permute-start | bytes 399368 | tf_op jit(solution)/shard_map/ppermute | solution.py:429
  8.3 3.2 %collective-permute-start.3 = (s16[520,128]{1,0:T(8,128)(2,1)S(1)}, s16[520,128]{1,0:T(8,128)(2,1)S(1)}, u32[]{:S(2)}, u32[]{:S(2)}) collective-permute-start(s16[520,128]{1,0:T(8,128)(2,1)S(1)} %get-tuple-element.40), channel_id=1, source_target_pairs={{0,10},{2,8},{4,14},{6,12},{8,2},{10,0},{12,6},{14,4},{1,11},{3,9}... | collective-permute-start | bytes 399368 | tf_op jit(solution)/shard_map/ppermute | solution.py:429
  11.5 0.5 collective-permute-start.4
  12.1 0.0 collective-permute-done.refs_0_
  12.1 4.6 %collective-permute-start.5 = (s16[520,128]{1,0:T(8,128)(2,1)S(1)}, s16[520,128]{1,0:T(8,128)(2,1)S(1)}, u32[]{:S(2)}, u32[]{:S(2)}) collective-permute-start(s16[520,128]{1,0:T(8,128)(2,1)S(1)} %get-tuple-element.42), channel_id=1, source_target_pairs={{0,6},{2,4},{4,2},{6,0},{8,14},{10,12},{12,10},{14,8},{1,7},{3,5},... | collective-permute-start | bytes 399368 | tf_op jit(solution)/shard_map/ppermute | solution.py:429
  16.7 0.0 collective-permute-done.1.refs_1_
  16.7 1.6 %collective-permute-start.6 = (s16[520,128]{1,0:T(8,128)(2,1)S(1)}, s16[520,128]{1,0:T(8,128)(2,1)S(1)}, u32[]{:S(2)}, u32[]{:S(2)}) collective-permute-start(s16[520,128]{1,0:T(8,128)(2,1)S(1)} %get-tuple-element.43), channel_id=1, source_target_pairs={{0,14},{2,12},{4,10},{6,8},{8,6},{10,4},{12,2},{14,0},{1,15},{3,13... | collective-permute-start | bytes 399368 | tf_op jit(solution)/shard_map/ppermute | solution.py:429
  18.3 0.0 copy-start.2
  18.3 0.9 %copy-done.2 = f32[2,128,256]{2,1,0:T(8,128)S(1)} copy-done((f32[2,128,256]{2,1,0:T(8,128)S(1)}, f32[2,128,256]{2,1,0:T(8,128)}, u32[]{:S(2)}) %copy-start.2) | copy-done | bytes 262168
  19.2 0.0 copy-start.3
  19.2 0.7 %copy-done.3 = s32[4,16]{1,0:T(4,128)S(1)} copy-done((s32[4,16]{1,0:T(4,128)S(1)}, s32[4,16]{1,0:T(4,128)}, u32[]{:S(2)}) %copy-start.3) | copy-done | bytes 280
  19.9 0.7 %tables.1 = (bf16[2,2,256,192]{3,2,1,0:T(8,128)(2,1)S(1)}, bf16[2,256,192]{2,1,0:T(8,128)(2,1)S(1)}, bf16[2,2,256,256]{3,2,1,0:T(8,128)(2,1)S(1)}, bf16[2,256,19...) custom-call(s32[1]{0:T(128)} %bitcast.me_ref, s32[4,16]{1,0:T(4,128)S(1)} %copy-done.3, ...), custom_call_target="tpu_custom_call" | custom-call | tf_op jit(solution)/shard_map/tables/pallas_call | solution.py:447
  20.6 2.6 %collective-permute-done.2.refs_2_ = s16[520,128]{1,0:T(8,128)(2,1)S(1)} collective-permute-done((s16[520,128]{1,0:T(8,128)(2,1)S(1)}, s16[520,128]{1,0:T(8,128)(2,1)S(1)}, u32[]{:S(2)}, u32[]{:S(2)}) %collective-permute-start.2) | collective-permute-done | bytes 133152 | tf_op jit(solution)/shard_map/ppermute | solution.py:429
  23.2 6.2 %collective-permute-done.3.refs_3_ = s16[520,128]{1,0:T(8,128)(2,1)S(1)} collective-permute-done((s16[520,128]{1,0:T(8,128)(2,1)S(1)}, s16[520,128]{1,0:T(8,128)(2,1)S(1)}, u32[]{:S(2)}, u32[]{:S(2)}) %collective-permute-start.3) | collective-permute-done | bytes 133152 | tf_op jit(solution)/shard_map/ppermute | solution.py:429
  29.4 0.0 collective-permute-done.4.refs_4_
  29.4 1.1 %forward_early.1.sum_ref = f32[2,256,1024]{2,1,0:T(8,128)S(1)} custom-call(s32[1]{0:T(128)} %bitcast.me_ref, bf16[2,2,256,192]{3,2,1,0:T(8,128)(2,1)S(1)} %get-tuple-element.36.table_ref, s16[520,128]{1,0:T(8,128)(2,1)S(1)} %collective-permute-done.refs_0_, s16[520,128]{1,0:T(8,128)(2,1)S(1)} %collective-permute-done.1.refs_1_, ...), custom_call_target="tpu_custom_call" | custom-call | tf_op jit(solution)/shard_map/forward_early/pallas_call | solution.py:462
  30.4 0.0 copy-start
  30.5 0.0 collective-permute-done.5.refs_0_
  30.5 0.0 collective-permute-done.6.refs_1_
  30.5 0.5 forward.1
  31.0 0.1 collective-permute-start.7
  31.1 1.0 %copy-done = bf16[4,8,256,128]{3,2,1,0:T(8,128)(2,1)S(1)} copy-done((bf16[4,8,256,128]{3,2,1,0:T(8,128)(2,1)S(1)}, bf16[4,8,256,128]{3,2,1,0:T(8,128)(2,1)}, u32[]{:S(2)}) %copy-start) | copy-done | bytes 2097176
  32.0 1.7 %inner.1.focus_ref = bf16[2,2,7,256,128]{4,3,2,1,0:T(8,128)(2,1)S(1)} custom-call(s32[1]{0:T(128)} %bitcast.2.rg_ref, s32[4,16]{1,0:T(4,128)S(1)} %get-tuple-element.34.starts_ref, bf16[8,2,512,128]{3,2,1,0:T(8,128)(2,1)S(1)} %get-tuple-element.44.spectrum_ref, bf16[4,8,256,128]{3,2,1,0:T(8,128)(2,1)S(1)} %copy-done), custom_call_target="tpu_custom_call" | custom-call | tf_op jit(solution)/shard_map/inner/pallas_call | solution.py:477
  33.7 0.0 collective-permute-done.7.halo_ref
  33.7 2.4 %outer.1 = (s16[520,128]{1,0:T(8,128)(2,1)S(1)}, s16[520,128]{1,0:T(8,128)(2,1)S(1)}, s16[520,128]{1,0:T(8,128)(2,1)S(1)}, s16[520,128]{1,0:T(8,128)(2,1)S(1)}, ...) custom-call(s32[1]{0:T(128)} %bitcast.me_ref, ...), custom_call_target="tpu_custom_call" | custom-call | tf_op jit(solution)/shard_map/outer/pallas_call | solution.py:484
  36.1 2.4 %collective-permute-start.8 = (s16[520,128]{1,0:T(8,128)(2,1)S(1)}, s16[520,128]{1,0:T(8,128)(2,1)S(1)}, u32[]{:S(2)}, u32[]{:S(2)}) collective-permute-start(s16[520,128]{1,0:T(8,128)(2,1)S(1)} %get-tuple-element.47), channel_id=1, source_target_pairs={{0,12},{2,14},{4,8},{6,10},{8,4},{10,6},{12,0},{14,2},{1,13},{3,15... | collective-permute-start | bytes 399368 | tf_op jit(solution)/shard_map/ppermute | solution.py:429
  38.5 0.0 collective-permute-start.9
  38.5 2.0 %collective-permute-start.10 = (s16[520,128]{1,0:T(8,128)(2,1)S(1)}, s16[520,128]{1,0:T(8,128)(2,1)S(1)}, u32[]{:S(2)}, u32[]{:S(2)}) collective-permute-start(s16[520,128]{1,0:T(8,128)(2,1)S(1)} %get-tuple-element.49), channel_id=1, source_target_pairs={{0,8},{2,10},{4,12},{6,14},{8,0},{10,2},{12,4},{14,6},{1,9},{3,11}... | collective-permute-start | bytes 399368 | tf_op jit(solution)/shard_map/ppermute | solution.py:429
  40.6 0.9 %collective-permute-start.11 = (s16[520,128]{1,0:T(8,128)(2,1)S(1)}, s16[520,128]{1,0:T(8,128)(2,1)S(1)}, u32[]{:S(2)}, u32[]{:S(2)}) collective-permute-start(s16[520,128]{1,0:T(8,128)(2,1)S(1)} %get-tuple-element.50), channel_id=1, source_target_pairs={{0,10},{2,8},{4,14},{6,12},{8,2},{10,0},{12,6},{14,4},{1,11},{3,9}... | collective-permute-start | bytes 399368 | tf_op jit(solution)/shard_map/ppermute | solution.py:429
  41.4 1.5 %collective-permute-start.12 = (s16[520,128]{1,0:T(8,128)(2,1)S(1)}, s16[520,128]{1,0:T(8,128)(2,1)S(1)}, u32[]{:S(2)}, u32[]{:S(2)}) collective-permute-start(s16[520,128]{1,0:T(8,128)(2,1)S(1)} %get-tuple-element.51), channel_id=1, source_target_pairs={{0,2},{2,0},{4,6},{6,4},{8,10},{10,8},{12,14},{14,12},{1,3},{3,1},... | collective-permute-start | bytes 399368 | tf_op jit(solution)/shard_map/ppermute | solution.py:429
  42.9 1.5 %collective-permute-done.8.refs_0_ = s16[520,128]{1,0:T(8,128)(2,1)S(1)} collective-permute-done((s16[520,128]{1,0:T(8,128)(2,1)S(1)}, s16[520,128]{1,0:T(8,128)(2,1)S(1)}, u32[]{:S(2)}, u32[]{:S(2)}) %collective-permute-start.8) | collective-permute-done | bytes 133152 | tf_op jit(solution)/shard_map/ppermute | solution.py:429
  44.4 2.1 %collective-permute-start.13 = (s16[520,128]{1,0:T(8,128)(2,1)S(1)}, s16[520,128]{1,0:T(8,128)(2,1)S(1)}, u32[]{:S(2)}, u32[]{:S(2)}) collective-permute-start(s16[520,128]{1,0:T(8,128)(2,1)S(1)} %get-tuple-element.53), channel_id=1, source_target_pairs={{0,6},{2,4},{4,2},{6,0},{8,14},{10,12},{12,10},{14,8},{1,7},{3,5},... | collective-permute-start | bytes 399368 | tf_op jit(solution)/shard_map/ppermute | solution.py:429
  46.5 0.5 collective-permute-done.9.refs_1_
  47.0 3.0 %collective-permute-start.14 = (s16[520,128]{1,0:T(8,128)(2,1)S(1)}, s16[520,128]{1,0:T(8,128)(2,1)S(1)}, u32[]{:S(2)}, u32[]{:S(2)}) collective-permute-start(s16[520,128]{1,0:T(8,128)(2,1)S(1)} %get-tuple-element.54), channel_id=1, source_target_pairs={{0,14},{2,12},{4,10},{6,8},{8,6},{10,4},{12,2},{14,0},{1,15},{3,13... | collective-permute-start | bytes 399368 | tf_op jit(solution)/shard_map/ppermute | solution.py:429
  50.0 4.5 %collective-permute-done.10.refs_2_ = s16[520,128]{1,0:T(8,128)(2,1)S(1)} collective-permute-done((s16[520,128]{1,0:T(8,128)(2,1)S(1)}, s16[520,128]{1,0:T(8,128)(2,1)S(1)}, u32[]{:S(2)}, u32[]{:S(2)}) %collective-permute-start.10) | collective-permute-done | bytes 133152 | tf_op jit(solution)/shard_map/ppermute | solution.py:429
  54.5 4.9 %collective-permute-done.11.refs_3_ = s16[520,128]{1,0:T(8,128)(2,1)S(1)} collective-permute-done((s16[520,128]{1,0:T(8,128)(2,1)S(1)}, s16[520,128]{1,0:T(8,128)(2,1)S(1)}, u32[]{:S(2)}, u32[]{:S(2)}) %collective-permute-start.11) | collective-permute-done | bytes 133152 | tf_op jit(solution)/shard_map/ppermute | solution.py:429
  59.4 0.0 collective-permute-done.12.refs_4_
  59.4 1.0 %image_early.1.sum_ref = f32[2,256,1024]{2,1,0:T(8,128)S(1)} custom-call(bf16[2,256,192]{2,1,0:T(8,128)(2,1)S(1)} %get-tuple-element.33.table_ref, s16[520,128]{1,0:T(8,128)(2,1)S(1)} %collective-permute-done.8.refs_0_, s16[520,128]{1,0:T(8,128)(2,1)S(1)} %collective-permute-done.9.refs_1_, s16[520,128]{1,0:T(8,128)(2,1)S(1)} %collective-permute-done.10.refs_2_, ...), custom_call_target="tpu_custom_call" | custom-call | tf_op jit(solution)/shard_map/image_early/pallas_call | solution.py:493
  60.5 0.0 collective-permute-done.13.refs_0_
  60.5 0.0 collective-permute-done.14.refs_1_
  60.5 1.4 %image.1 = bf16[512,1024]{1,0:T(8,128)(2,1)} custom-call(bf16[256,192]{1,0:T(8,128)(2,1)S(1)} %get-tuple-element.32.table_ref, f32[2,256,1024]{2,1,0:T(8,128)S(1)} %image_early.1.sum_ref, s16[520,128]{1,0:T(8,128)(2,1)S(1)} %collective-permute-done.13.refs_0_, s16[520,128]{1,0:T(8,128)(2,1)S(1)} %collective-permute-done.14.refs_1_), custom_call_target="tpu_custom_call" | custom-call | tf_op jit(solution)/shard_map/image/pallas_call | solution.py:496
Async XLA Ops:
  0.0 1.2 %copy-start.1 = (bf16[2,32,8,1024]{3,2,1,0:T(8,128)(2,1)S(1)}, bf16[2,32,8,1024]{3,2,1,0:T(8,128)(2,1)}, u32[]{:S(2)}) copy-start(bf16[2,32,8,1024]{3,2,1,0:T(8,128)(2,1)} %param.4) | copy-start | bytes 3145732
  2.6 9.5 %collective-permute-start = (s16[520,128]{1,0:T(8,128)(2,1)S(1)}, s16[520,128]{1,0:T(8,128)(2,1)S(1)}, u32[]{:S(2)}, u32[]{:S(2)}) collective-permute-start(s16[520,128]{1,0:T(8,128)(2,1)S(1)} %get-tuple-element.37), channel_id=1, source_target_pairs={{0,12},{2,14},{4,8},{6,10},{8,4},{10,6},{12,0},{14,2},{1,13},{3,15... | collective-permute-start | bytes 399368 | tf_op jit(solution)/shard_map/ppermute | solution.py:429
  7.7 9.0 %collective-permute-start.1 = (s16[520,128]{1,0:T(8,128)(2,1)S(1)}, s16[520,128]{1,0:T(8,128)(2,1)S(1)}, u32[]{:S(2)}, u32[]{:S(2)}) collective-permute-start(s16[520,128]{1,0:T(8,128)(2,1)S(1)} %get-tuple-element.38), channel_id=1, source_target_pairs={{0,4},{2,6},{4,0},{6,2},{8,12},{10,14},{12,8},{14,10},{1,5},{3,7},... | collective-permute-start | bytes 399368 | tf_op jit(solution)/shard_map/ppermute | solution.py:429
  7.7 15.5 %collective-permute-start.2 = (s16[520,128]{1,0:T(8,128)(2,1)S(1)}, s16[520,128]{1,0:T(8,128)(2,1)S(1)}, u32[]{:S(2)}, u32[]{:S(2)}) collective-permute-start(s16[520,128]{1,0:T(8,128)(2,1)S(1)} %get-tuple-element.39), channel_id=1, source_target_pairs={{0,8},{2,10},{4,12},{6,14},{8,0},{10,2},{12,4},{14,6},{1,9},{3,11}... | collective-permute-start | bytes 399368 | tf_op jit(solution)/shard_map/ppermute | solution.py:429
  8.3 21.1 %collective-permute-start.3 = (s16[520,128]{1,0:T(8,128)(2,1)S(1)}, s16[520,128]{1,0:T(8,128)(2,1)S(1)}, u32[]{:S(2)}, u32[]{:S(2)}) collective-permute-start(s16[520,128]{1,0:T(8,128)(2,1)S(1)} %get-tuple-element.40), channel_id=1, source_target_pairs={{0,10},{2,8},{4,14},{6,12},{8,2},{10,0},{12,6},{14,4},{1,11},{3,9}... | collective-permute-start | bytes 399368 | tf_op jit(solution)/shard_map/ppermute | solution.py:429
  11.5 17.8 %collective-permute-start.4 = (s16[520,128]{1,0:T(8,128)(2,1)S(1)}, s16[520,128]{1,0:T(8,128)(2,1)S(1)}, u32[]{:S(2)}, u32[]{:S(2)}) collective-permute-start(s16[520,128]{1,0:T(8,128)(2,1)S(1)} %get-tuple-element.41), channel_id=1, source_target_pairs={{0,2},{2,0},{4,6},{6,4},{8,10},{10,8},{12,14},{14,12},{1,3},{3,1},... | collective-permute-start | bytes 399368 | tf_op jit(solution)/shard_map/ppermute | solution.py:429
  12.1 18.4 %collective-permute-start.5 = (s16[520,128]{1,0:T(8,128)(2,1)S(1)}, s16[520,128]{1,0:T(8,128)(2,1)S(1)}, u32[]{:S(2)}, u32[]{:S(2)}) collective-permute-start(s16[520,128]{1,0:T(8,128)(2,1)S(1)} %get-tuple-element.42), channel_id=1, source_target_pairs={{0,6},{2,4},{4,2},{6,0},{8,14},{10,12},{12,10},{14,8},{1,7},{3,5},... | collective-permute-start | bytes 399368 | tf_op jit(solution)/shard_map/ppermute | solution.py:429
  16.7 13.8 %collective-permute-start.6 = (s16[520,128]{1,0:T(8,128)(2,1)S(1)}, s16[520,128]{1,0:T(8,128)(2,1)S(1)}, u32[]{:S(2)}, u32[]{:S(2)}) collective-permute-start(s16[520,128]{1,0:T(8,128)(2,1)S(1)} %get-tuple-element.43), channel_id=1, source_target_pairs={{0,14},{2,12},{4,10},{6,8},{8,6},{10,4},{12,2},{14,0},{1,15},{3,13... | collective-permute-start | bytes 399368 | tf_op jit(solution)/shard_map/ppermute | solution.py:429
  18.3 0.9 %copy-start.2 = (f32[2,128,256]{2,1,0:T(8,128)S(1)}, f32[2,128,256]{2,1,0:T(8,128)}, u32[]{:S(2)}) copy-start(f32[2,128,256]{2,1,0:T(8,128)} %constant.10.clone.base_ref) | copy-start | bytes 786436
  19.2 0.7 %copy-start.3 = (s32[4,16]{1,0:T(4,128)S(1)}, s32[4,16]{1,0:T(4,128)}, u32[]{:S(2)}) copy-start(s32[4,16]{1,0:T(4,128)} %band_ref.1) | copy-start | bytes 772
  30.4 1.6 %copy-start = (bf16[4,8,256,128]{3,2,1,0:T(8,128)(2,1)S(1)}, bf16[4,8,256,128]{3,2,1,0:T(8,128)(2,1)}, u32[]{:S(2)}) copy-start(bf16[4,8,256,128]{3,2,1,0:T(8,128)(2,1)} %weights_ref.3) | copy-start | bytes 6291460
  31.0 2.7 %collective-permute-start.7 = (bf16[2,512,128]{2,1,0:T(8,128)(2,1)S(1)}, bf16[2,512,128]{2,1,0:T(8,128)(2,1)S(1)}, u32[]{:S(2)}, u32[]{:S(2)}) collective-permute-start(bf16[2,512,128]{2,1,0:T(8,128)(2,1)S(1)} %get-tuple-element.45), channel_id=1, source_target_pairs={{0,1},{1,0},{2,3},{3,2},{4,5},{5,4},{6,7},{7,6},{8,9},{9,8},{10,11... | collective-permute-start | bytes 786440 | tf_op jit(solution)/shard_map/ppermute | solution.py:476
  36.1 8.3 %collective-permute-start.8 = (s16[520,128]{1,0:T(8,128)(2,1)S(1)}, s16[520,128]{1,0:T(8,128)(2,1)S(1)}, u32[]{:S(2)}, u32[]{:S(2)}) collective-permute-start(s16[520,128]{1,0:T(8,128)(2,1)S(1)} %get-tuple-element.47), channel_id=1, source_target_pairs={{0,12},{2,14},{4,8},{6,10},{8,4},{10,6},{12,0},{14,2},{1,13},{3,15... | collective-permute-start | bytes 399368 | tf_op jit(solution)/shard_map/ppermute | solution.py:429
  38.5 8.5 %collective-permute-start.9 = (s16[520,128]{1,0:T(8,128)(2,1)S(1)}, s16[520,128]{1,0:T(8,128)(2,1)S(1)}, u32[]{:S(2)}, u32[]{:S(2)}) collective-permute-start(s16[520,128]{1,0:T(8,128)(2,1)S(1)} %get-tuple-element.48), channel_id=1, source_target_pairs={{0,4},{2,6},{4,0},{6,2},{8,12},{10,14},{12,8},{14,10},{1,5},{3,7},... | collective-permute-start | bytes 399368 | tf_op jit(solution)/shard_map/ppermute | solution.py:429
  38.5 16.0 %collective-permute-start.10 = (s16[520,128]{1,0:T(8,128)(2,1)S(1)}, s16[520,128]{1,0:T(8,128)(2,1)S(1)}, u32[]{:S(2)}, u32[]{:S(2)}) collective-permute-start(s16[520,128]{1,0:T(8,128)(2,1)S(1)} %get-tuple-element.49), channel_id=1, source_target_pairs={{0,8},{2,10},{4,12},{6,14},{8,0},{10,2},{12,4},{14,6},{1,9},{3,11}... | collective-permute-start | bytes 399368 | tf_op jit(solution)/shard_map/ppermute | solution.py:429
  40.6 18.9 %collective-permute-start.11 = (s16[520,128]{1,0:T(8,128)(2,1)S(1)}, s16[520,128]{1,0:T(8,128)(2,1)S(1)}, u32[]{:S(2)}, u32[]{:S(2)}) collective-permute-start(s16[520,128]{1,0:T(8,128)(2,1)S(1)} %get-tuple-element.50), channel_id=1, source_target_pairs={{0,10},{2,8},{4,14},{6,12},{8,2},{10,0},{12,6},{14,4},{1,11},{3,9}... | collective-permute-start | bytes 399368 | tf_op jit(solution)/shard_map/ppermute | solution.py:429
  41.4 18.0 %collective-permute-start.12 = (s16[520,128]{1,0:T(8,128)(2,1)S(1)}, s16[520,128]{1,0:T(8,128)(2,1)S(1)}, u32[]{:S(2)}, u32[]{:S(2)}) collective-permute-start(s16[520,128]{1,0:T(8,128)(2,1)S(1)} %get-tuple-element.51), channel_id=1, source_target_pairs={{0,2},{2,0},{4,6},{6,4},{8,10},{10,8},{12,14},{14,12},{1,3},{3,1},... | collective-permute-start | bytes 399368 | tf_op jit(solution)/shard_map/ppermute | solution.py:429
  44.4 16.0 %collective-permute-start.13 = (s16[520,128]{1,0:T(8,128)(2,1)S(1)}, s16[520,128]{1,0:T(8,128)(2,1)S(1)}, u32[]{:S(2)}, u32[]{:S(2)}) collective-permute-start(s16[520,128]{1,0:T(8,128)(2,1)S(1)} %get-tuple-element.53), channel_id=1, source_target_pairs={{0,6},{2,4},{4,2},{6,0},{8,14},{10,12},{12,10},{14,8},{1,7},{3,5},... | collective-permute-start | bytes 399368 | tf_op jit(solution)/shard_map/ppermute | solution.py:429
  47.0 13.4 %collective-permute-start.14 = (s16[520,128]{1,0:T(8,128)(2,1)S(1)}, s16[520,128]{1,0:T(8,128)(2,1)S(1)}, u32[]{:S(2)}, u32[]{:S(2)}) collective-permute-start(s16[520,128]{1,0:T(8,128)(2,1)S(1)} %get-tuple-element.54), channel_id=1, source_target_pairs={{0,14},{2,12},{4,10},{6,8},{8,6},{10,4},{12,2},{14,0},{1,15},{3,13... | collective-permute-start | bytes 399368 | tf_op jit(solution)/shard_map/ppermute | solution.py:429

commit v7 on v6

--- a/solution.py
+++ b/solution.py
@@ -131,6 +131,8 @@
 EARLY = (6, 2, 4, 5, 1, 0)
 LATE = (3, 7)
 EARLY_ROWS = 192
+LEAD = (2,)
+REST = (0, 1, 3)
 VMEM_LIMIT = 20 * 1024 * 1024
 
 
@@ -332,17 +334,44 @@
         ):
             for part, half in enumerate(pair):
                 for at, (parity, row) in enumerate(focus_rows(g)):
-                    focus_ref[part, parity, n, row : row + 32, :] = half[at * 32 : (at + 1) * 32]
+                    focus_ref[part, parity, j, row : row + 32, :] = half[at * 32 : (at + 1) * 32]
+
+
+def back_messages(me, rg, slots, table_ref, focus_ref, face_ref, out_refs):
+    results = []
+    for parity in range(2):
+        table = [
+            jnp.concatenate(
+                [
+                    table_ref[part, parity, c * SIDE + i * MLOC : c * SIDE + (i + 1) * MLOC, :]
+                    for i in slots
+                    for c in range(2)
+                ],
+                0,
+            )
+            for part in range(2)
+        ]
+        pair = []
+        for part in range(2):
+            block = face_ref[part, parity]
+            inner = [focus_ref[part, parity, n] for n in range(TILES)]
+            inner[0] = jnp.where(rg == 1, block, inner[0])
+            inner[-1] = jnp.where(rg == 1, inner[-1], block)
+            pair.append(jnp.concatenate(inner, 1))
+        results.append(product3(table, pair))
+    even, odd = results[0], results[1] * sign_of(me)
+    for upper, lines in enumerate((even + odd, even - odd)):
+        for n in range(len(slots)):
+            store_coded(out_refs[2 * n + upper], [(0, lines[n * ROWS : (n + 1) * ROWS, :])])
 
 
 def outer_kernel(me_ref, rg_ref, starts_ref, spectrum_ref, halo_ref, weights_ref, table_ref, focus_ref, *refs):
-    out_refs, window_ref = refs[:NDEV], refs[NDEV]
-    me, rg = me_ref[0], rg_ref[0]
+    out_refs, face_ref, window_ref = refs[:2], refs[2], refs[3]
+    rg = rg_ref[0]
     first = 6 - 7 * rg
     window_ref[2 - 2 * rg] = halo_ref[...]
     for n in range(2):
         window_ref[rg + n] = spectrum_ref[(1 - rg) * 6 + n]
-    face = [[[None] * 8 for _ in range(2)] for _ in range(2)]
     for g, pair in remap_block(
         starts_ref,
         weights_ref,
@@ -352,30 +381,12 @@
     ):
         for part, half in enumerate(pair):
             for at, (parity, row) in enumerate(focus_rows(g)):
-                face[part][parity][row // 32] = half[at * 32 : (at + 1) * 32]
-    results = []
-    for parity in range(2):
-        pair = []
-        for part in range(2):
-            block = jnp.concatenate(face[part][parity], 0)
-            inner = [focus_ref[part, parity, n] for n in range(TILES - 1)]
-            pair.append(
-                jnp.concatenate(
-                    [jnp.where(rg == 1, block, inner[0])]
-                    + [jnp.where(rg == 1, inner[n - 1], inner[n]) for n in range(1, TILES - 1)]
-                    + [jnp.where(rg == 1, inner[-1], block)],
-                    1,
-                )
-            )
-        results.append(product3((table_ref[0, parity], table_ref[1, parity]), pair))
-    even, odd = results[0], results[1] * sign_of(me)
-    for i, out_ref in enumerate(out_refs):
-        lines = even + odd if i < 4 else even - odd
-        pieces = []
-        for c in range(2):
-            at = c * SIDE + (i % 4) * MLOC
-            pieces.append((c * MLOC, lines[at : at + MLOC, :]))
-        store_coded(out_ref, pieces)
+                face_ref[part, parity, row : row + 32, :] = half[at * 32 : (at + 1) * 32]
+    back_messages(me_ref[0], rg, LEAD, table_ref, focus_ref, face_ref, out_refs)
+
+
+def rest_kernel(me_ref, rg_ref, table_ref, focus_ref, face_ref, *out_refs):
+    back_messages(me_ref[0], rg_ref[0], REST, table_ref, focus_ref, face_ref, out_refs)
 
 
 def image_lines(values, h):
@@ -394,7 +405,8 @@
 
 
 def image_kernel(table_ref, sum_ref, *refs):
-    in_refs, out_ref = refs[: len(LATE)], refs[len(LATE)]
+    in_refs, (out_hbm, out_ref, sems) = refs[: len(LATE)], refs[len(LATE) :]
+    stores = []
     scales = [load_scales(ref) for ref in in_refs]
     for tiles in tile_pairs(TILES):
         values = [load_columns(ref, scale, tiles) for ref, scale in zip(in_refs, scales)]
@@ -404,16 +416,22 @@
             for c in range(2):
                 at = c * 256 + h * 128
                 out_ref[at : at + 128, columns] = result[c * 128 : (c + 1) * 128].astype(BF16)
-
-
-def vmem_call(kernel, name, out_shape, smem=0, vmem=0, scratch=()):
+        stores.append(
+            pltpu.make_async_copy(out_ref.at[:, columns], out_hbm.at[:, columns], sems.at[tiles[0] // 2])
+        )
+        stores[-1].start()
+    for store in stores:
+        store.wait()
+
+
+def vmem_call(kernel, name, out_shape, smem=0, vmem=0, scratch=(), out_space=pltpu.VMEM):
     return pl.pallas_call(
         kernel,
         name=name,
         out_shape=out_shape,
         in_specs=[pl.BlockSpec(memory_space=pltpu.SMEM)] * smem
         + [pl.BlockSpec(memory_space=pltpu.VMEM)] * vmem,
-        out_specs=jax.tree.map(lambda _: pl.BlockSpec(memory_space=pltpu.VMEM), out_shape),
+        out_specs=jax.tree.map(lambda _: pl.BlockSpec(memory_space=out_space), out_shape),
         scratch_shapes=scratch,
         compiler_params=pltpu.CompilerParams(vmem_limit_bytes=VMEM_LIMIT),
     )
@@ -477,24 +495,33 @@
     focus = vmem_call(
         inner_kernel,
         "inner",
-        jax.ShapeDtypeStruct((2, 2, TILES - 1, LINES_DEV, TILE), BF16),
+        jax.ShapeDtypeStruct((2, 2, TILES, LINES_DEV, TILE), BF16),
         smem=2,
         vmem=2,
     )(rg, starts, spectrum, stolt_weights)
-    back = vmem_call(
+    back = [None] * NDEV
+    back[2], back[6], face = vmem_call(
         outer_kernel,
         "outer",
-        [message] * NDEV,
+        [message, message, jax.ShapeDtypeStruct((2, 2, LINES_DEV, TILE), BF16)],
         smem=3,
         vmem=5,
         scratch=[pltpu.VMEM((3, 2, LINES, TILE), BF16)],
     )(me, rg, starts, spectrum, halo, stolt_weights, inverse_table, focus)
+    rest = vmem_call(rest_kernel, "rest", [message] * 6, smem=2, vmem=3)(me, rg, inverse_table, focus, face)
+    for n, i in enumerate(REST):
+        back[i], back[i + 4] = rest[2 * n], rest[2 * n + 1]
     early_lines, late_lines = exchange(back)
     image_sum = vmem_call(
         image_early_kernel, "image_early", jax.ShapeDtypeStruct((2, 256, bins), F32), vmem=1 + len(EARLY)
     )(image_table, *early_lines)
     image = vmem_call(
-        image_kernel, "image", jax.ShapeDtypeStruct((LINES, bins), BF16), vmem=2 + len(LATE)
+        image_kernel,
+        "image",
+        jax.ShapeDtypeStruct((LINES, bins), BF16),
+        vmem=2 + len(LATE),
+        scratch=[pltpu.VMEM((LINES, bins), BF16), pltpu.SemaphoreType.DMA((TILES // 2,))],
+        out_space=pltpu.HBM,
     )(image_late, image_sum, *late_lines)
     return image.reshape(2, MLOC, NDEV, bins)
 

time: 62.1 us -> 61.2 us (0.986)
  waiting for transfers between devices: 20.2 us -> 19.1 us
    ppermute x14, waiting for transfers between devices: 20.2 us -> 19.1 us  [exchange(): lax.ppermute(messages[i], 'az', [(d, d ^ i) for d in range(NDEV)])]
    pallas_call x2 -> x3, Pallas kernels: 4.03 us -> 4.38 us  [the longest x1 1.67 us: fast_body(): vmem_call(inner_kernel, 'inner', jax.ShapeDtypeStruct((2, 2, TILES, LINES...]
  transfers between devices with their start and end apart: 15 -> 15, of which waited for: 6 -> 6; matrix products, arithmetic and copies ran while one was open for 0% -> 0% of each run, Pallas kernels for 7% -> 9%
where the time goes in v7:
time: 61.2 us; the launch traced here: 61 us
  starting transfers between devices  27.7 us (45%)
  waiting for transfers between devices  19.1 us (31%)
  Pallas kernels  10.3 us (17%)
  local copies, waits for them, and re-layouts  3.82 us (6%)
    ppermute x14, starting transfers between devices, exchange(): lax.ppermute(messages[i], 'az', [(d, d ^ i) for d in range(NDEV)])  27.6 us
    ppermute x14, waiting for transfers between devices, exchange(): lax.ppermute(messages[i], 'az', [(d, d ^ i) for d in range(NDEV)])  19.1 us
    unnamed x8, local copies, waits for them, and re-layouts  3.82 us
    pallas_call x1, Pallas kernels, fast_body(): vmem_call(inner_kernel, 'inner', jax.ShapeDtypeStruct((2, 2, TILES, LINES...  1.67 us
    pallas_call x1, Pallas kernels, fast_body(): vmem_call(outer_kernel, 'outer', [message, message, jax.ShapeDtypeStruct(...  1.62 us
    pallas_call x1, Pallas kernels, fast_body(): vmem_call(spread_kernel, 'spread', [message] * NDEV, smem=1, vmem=1)  1.32 us
    pallas_call x1, Pallas kernels, fast_body(): vmem_call(image_kernel, 'image', jax.ShapeDtypeStruct((LINES, bins), BF16...  1.25 us
  transfers between devices with their start and end apart: 15, of which 6 were waited for; matrix products, arithmetic and copies ran while one was open for 0% of the time, Pallas kernels for 9%

profile of v7, /device:TPU:0, one launch (start us, length us, event | category | flops | bytes accessed | tf_op | source)
XLA Modules:
  0.0 61.0 jit_solution(7082818897093769753)
XLA Ops:
  0.0 0.0 copy-start.1
  0.0 1.2 %copy-done.1 = bf16[2,32,8,1024]{3,2,1,0:T(8,128)(2,1)S(1)} copy-done((bf16[2,32,8,1024]{3,2,1,0:T(8,128)(2,1)S(1)}, bf16[2,32,8,1024]{3,2,1,0:T(8,128)(2,1)}, u32[]{:S(2)}) %copy-start.1) | copy-done | bytes 1048600
  1.2 1.3 %spread.1 = (s16[520,128]{1,0:T(8,128)(2,1)S(1)}, s16[520,128]{1,0:T(8,128)(2,1)S(1)}, s16[520,128]{1,0:T(8,128)(2,1)S(1)}, s16[520,128]{1,0:T(8,128)(2,1)S(1)},...) custom-call(s32[1]{0:T(128)} %bitcast.me_ref, ...), custom_call_target="tpu_custom_call" | custom-call | tf_op jit(solution)/shard_map/spread/pallas_call | solution.py:461
  2.6 5.1 %collective-permute-start = (s16[520,128]{1,0:T(8,128)(2,1)S(1)}, s16[520,128]{1,0:T(8,128)(2,1)S(1)}, u32[]{:S(2)}, u32[]{:S(2)}) collective-permute-start(s16[520,128]{1,0:T(8,128)(2,1)S(1)} %get-tuple-element.38), channel_id=1, source_target_pairs={{0,12},{2,14},{4,8},{6,10},{8,4},{10,6},{12,0},{14,2},{1,13},{3,15... | collective-permute-start | bytes 399368 | tf_op jit(solution)/shard_map/ppermute | solution.py:447
  7.7 0.0 collective-permute-start.1
  7.7 0.6 %collective-permute-start.2 = (s16[520,128]{1,0:T(8,128)(2,1)S(1)}, s16[520,128]{1,0:T(8,128)(2,1)S(1)}, u32[]{:S(2)}, u32[]{:S(2)}) collective-permute-start(s16[520,128]{1,0:T(8,128)(2,1)S(1)} %get-tuple-element.40), channel_id=1, source_target_pairs={{0,8},{2,10},{4,12},{6,14},{8,0},{10,2},{12,4},{14,6},{1,9},{3,11}... | collective-permute-start | bytes 399368 | tf_op jit(solution)/shard_map/ppermute | solution.py:447
  8.3 3.2 %collective-permute-start.3 = (s16[520,128]{1,0:T(8,128)(2,1)S(1)}, s16[520,128]{1,0:T(8,128)(2,1)S(1)}, u32[]{:S(2)}, u32[]{:S(2)}) collective-permute-start(s16[520,128]{1,0:T(8,128)(2,1)S(1)} %get-tuple-element.41), channel_id=1, source_target_pairs={{0,10},{2,8},{4,14},{6,12},{8,2},{10,0},{12,6},{14,4},{1,11},{3,9}... | collective-permute-start | bytes 399368 | tf_op jit(solution)/shard_map/ppermute | solution.py:447
  11.5 0.5 collective-permute-start.4
  12.1 0.0 collective-permute-done.refs_0_
  12.1 4.6 %collective-permute-start.5 = (s16[520,128]{1,0:T(8,128)(2,1)S(1)}, s16[520,128]{1,0:T(8,128)(2,1)S(1)}, u32[]{:S(2)}, u32[]{:S(2)}) collective-permute-start(s16[520,128]{1,0:T(8,128)(2,1)S(1)} %get-tuple-element.43), channel_id=1, source_target_pairs={{0,6},{2,4},{4,2},{6,0},{8,14},{10,12},{12,10},{14,8},{1,7},{3,5},... | collective-permute-start | bytes 399368 | tf_op jit(solution)/shard_map/ppermute | solution.py:447
  16.7 0.0 collective-permute-done.1.refs_1_
  16.7 1.6 %collective-permute-start.6 = (s16[520,128]{1,0:T(8,128)(2,1)S(1)}, s16[520,128]{1,0:T(8,128)(2,1)S(1)}, u32[]{:S(2)}, u32[]{:S(2)}) collective-permute-start(s16[520,128]{1,0:T(8,128)(2,1)S(1)} %get-tuple-element.44), channel_id=1, source_target_pairs={{0,14},{2,12},{4,10},{6,8},{8,6},{10,4},{12,2},{14,0},{1,15},{3,13... | collective-permute-start | bytes 399368 | tf_op jit(solution)/shard_map/ppermute | solution.py:447
  18.3 0.0 copy-start.2
  18.3 0.9 %copy-done.2 = f32[2,128,256]{2,1,0:T(8,128)S(1)} copy-done((f32[2,128,256]{2,1,0:T(8,128)S(1)}, f32[2,128,256]{2,1,0:T(8,128)}, u32[]{:S(2)}) %copy-start.2) | copy-done | bytes 262168
  19.2 0.0 copy-start.3
  19.2 0.7 %copy-done.3 = s32[4,16]{1,0:T(4,128)S(1)} copy-done((s32[4,16]{1,0:T(4,128)S(1)}, s32[4,16]{1,0:T(4,128)}, u32[]{:S(2)}) %copy-start.3) | copy-done | bytes 280
  19.9 0.7 %tables.1 = (bf16[2,2,256,192]{3,2,1,0:T(8,128)(2,1)S(1)}, bf16[2,256,192]{2,1,0:T(8,128)(2,1)S(1)}, bf16[2,2,256,256]{3,2,1,0:T(8,128)(2,1)S(1)}, bf16[2,256,19...) custom-call(s32[1]{0:T(128)} %bitcast.me_ref, s32[4,16]{1,0:T(4,128)S(1)} %copy-done.3, ...), custom_call_target="tpu_custom_call" | custom-call | tf_op jit(solution)/shard_map/tables/pallas_call | solution.py:465
  20.6 2.6 %collective-permute-done.2.refs_2_ = s16[520,128]{1,0:T(8,128)(2,1)S(1)} collective-permute-done((s16[520,128]{1,0:T(8,128)(2,1)S(1)}, s16[520,128]{1,0:T(8,128)(2,1)S(1)}, u32[]{:S(2)}, u32[]{:S(2)}) %collective-permute-start.2) | collective-permute-done | bytes 133152 | tf_op jit(solution)/shard_map/ppermute | solution.py:447
  23.2 6.2 %collective-permute-done.3.refs_3_ = s16[520,128]{1,0:T(8,128)(2,1)S(1)} collective-permute-done((s16[520,128]{1,0:T(8,128)(2,1)S(1)}, s16[520,128]{1,0:T(8,128)(2,1)S(1)}, u32[]{:S(2)}, u32[]{:S(2)}) %collective-permute-start.3) | collective-permute-done | bytes 133152 | tf_op jit(solution)/shard_map/ppermute | solution.py:447
  29.4 0.0 collective-permute-done.4.refs_4_
  29.4 1.1 %forward_early.1.sum_ref = f32[2,256,1024]{2,1,0:T(8,128)S(1)} custom-call(s32[1]{0:T(128)} %bitcast.me_ref, bf16[2,2,256,192]{3,2,1,0:T(8,128)(2,1)S(1)} %get-tuple-element.37.table_ref, s16[520,128]{1,0:T(8,128)(2,1)S(1)} %collective-permute-done.refs_0_, s16[520,128]{1,0:T(8,128)(2,1)S(1)} %collective-permute-done.1.refs_1_, ...), custom_call_target="tpu_custom_call" | custom-call | tf_op jit(solution)/shard_map/forward_early/pallas_call | solution.py:480
  30.4 0.0 copy-start
  30.5 0.0 collective-permute-done.5.refs_0_
  30.5 0.0 collective-permute-done.6.refs_1_
  30.5 0.5 forward.1
  31.0 0.1 collective-permute-start.7
  31.1 1.0 %copy-done = bf16[4,8,256,128]{3,2,1,0:T(8,128)(2,1)S(1)} copy-done((bf16[4,8,256,128]{3,2,1,0:T(8,128)(2,1)S(1)}, bf16[4,8,256,128]{3,2,1,0:T(8,128)(2,1)}, u32[]{:S(2)}) %copy-start) | copy-done | bytes 2097176
  32.0 1.7 %inner.1.focus_ref = bf16[2,2,8,256,128]{4,3,2,1,0:T(8,128)(2,1)S(1)} custom-call(s32[1]{0:T(128)} %bitcast.2.rg_ref, s32[4,16]{1,0:T(4,128)S(1)} %get-tuple-element.35.starts_ref, bf16[8,2,512,128]{3,2,1,0:T(8,128)(2,1)S(1)} %get-tuple-element.45.spectrum_ref, bf16[4,8,256,128]{3,2,1,0:T(8,128)(2,1)S(1)} %copy-done), custom_call_target="tpu_custom_call" | custom-call | tf_op jit(solution)/shard_map/inner/pallas_call | solution.py:495
  33.7 0.0 collective-permute-done.7.halo_ref
  33.7 1.6 %outer.1 = (s16[520,128]{1,0:T(8,128)(2,1)S(1)}, s16[520,128]{1,0:T(8,128)(2,1)S(1)}, bf16[2,2,256,128]{3,2,1,0:T(8,128)(2,1)S(1)}) custom-call(s32[1]{0:T(128)} %bitcast.me_ref, s32[1]{0:T(128)} %bitcast.2.rg_ref, s32[4,16]{1,0:T(4,128)S(1)} %get-tuple-element.35.starts_ref, bf16[8,2,512,128]{3,2,1,0:T(8,128)(2,1)S(1)} %get-tuple-element.45.spectrum_ref, ...), custom_call_target="tpu_custom_call" | custom-call | tf_op jit(solution)/shard_map/outer/pallas_call | solution.py:503
  35.4 2.4 %collective-permute-start.8 = (s16[520,128]{1,0:T(8,128)(2,1)S(1)}, s16[520,128]{1,0:T(8,128)(2,1)S(1)}, u32[]{:S(2)}, u32[]{:S(2)}) collective-permute-start(s16[520,128]{1,0:T(8,128)(2,1)S(1)} %get-tuple-element.48), channel_id=1, source_target_pairs={{0,12},{2,14},{4,8},{6,10},{8,4},{10,6},{12,0},{14,2},{1,13},{3,15... | collective-permute-start | bytes 399368 | tf_op jit(solution)/shard_map/ppermute | solution.py:447
  37.8 0.0 collective-permute-start.9
  37.8 1.1 %rest.1 = (s16[520,128]{1,0:T(8,128)(2,1)S(1)}, s16[520,128]{1,0:T(8,128)(2,1)S(1)}, s16[520,128]{1,0:T(8,128)(2,1)S(1)}, s16[520,128]{1,0:T(8,128)(2,1)S(1)}, s...) custom-call(s32[1]{0:T(128)} %bitcast.me_ref, s32[1]{0:T(128)} %bitcast.2.rg_ref, ...), custom_call_target="tpu_custom_call" | custom-call | tf_op jit(solution)/shard_map/rest/pallas_call | solution.py:511
  38.9 2.1 %collective-permute-start.10 = (s16[520,128]{1,0:T(8,128)(2,1)S(1)}, s16[520,128]{1,0:T(8,128)(2,1)S(1)}, u32[]{:S(2)}, u32[]{:S(2)}) collective-permute-start(s16[520,128]{1,0:T(8,128)(2,1)S(1)} %get-tuple-element.51), channel_id=1, source_target_pairs={{0,8},{2,10},{4,12},{6,14},{8,0},{10,2},{12,4},{14,6},{1,9},{3,11}... | collective-permute-start | bytes 399368 | tf_op jit(solution)/shard_map/ppermute | solution.py:447
  41.0 0.9 %collective-permute-start.11 = (s16[520,128]{1,0:T(8,128)(2,1)S(1)}, s16[520,128]{1,0:T(8,128)(2,1)S(1)}, u32[]{:S(2)}, u32[]{:S(2)}) collective-permute-start(s16[520,128]{1,0:T(8,128)(2,1)S(1)} %get-tuple-element.52), channel_id=1, source_target_pairs={{0,10},{2,8},{4,14},{6,12},{8,2},{10,0},{12,6},{14,4},{1,11},{3,9}... | collective-permute-start | bytes 399368 | tf_op jit(solution)/shard_map/ppermute | solution.py:447
  41.8 1.5 %collective-permute-start.12 = (s16[520,128]{1,0:T(8,128)(2,1)S(1)}, s16[520,128]{1,0:T(8,128)(2,1)S(1)}, u32[]{:S(2)}, u32[]{:S(2)}) collective-permute-start(s16[520,128]{1,0:T(8,128)(2,1)S(1)} %get-tuple-element.53), channel_id=1, source_target_pairs={{0,2},{2,0},{4,6},{6,4},{8,10},{10,8},{12,14},{14,12},{1,3},{3,1},... | collective-permute-start | bytes 399368 | tf_op jit(solution)/shard_map/ppermute | solution.py:447
  43.3 0.4 collective-permute-done.8.refs_0_
  43.7 2.1 %collective-permute-start.13 = (s16[520,128]{1,0:T(8,128)(2,1)S(1)}, s16[520,128]{1,0:T(8,128)(2,1)S(1)}, u32[]{:S(2)}, u32[]{:S(2)}) collective-permute-start(s16[520,128]{1,0:T(8,128)(2,1)S(1)} %get-tuple-element.55), channel_id=1, source_target_pairs={{0,6},{2,4},{4,2},{6,0},{8,14},{10,12},{12,10},{14,8},{1,7},{3,5},... | collective-permute-start | bytes 399368 | tf_op jit(solution)/shard_map/ppermute | solution.py:447
  45.8 0.5 collective-permute-done.9.refs_1_
  46.3 3.0 %collective-permute-start.14 = (s16[520,128]{1,0:T(8,128)(2,1)S(1)}, s16[520,128]{1,0:T(8,128)(2,1)S(1)}, u32[]{:S(2)}, u32[]{:S(2)}) collective-permute-start(s16[520,128]{1,0:T(8,128)(2,1)S(1)} %get-tuple-element.56), channel_id=1, source_target_pairs={{0,14},{2,12},{4,10},{6,8},{8,6},{10,4},{12,2},{14,0},{1,15},{3,13... | collective-permute-start | bytes 399368 | tf_op jit(solution)/shard_map/ppermute | solution.py:447
  49.3 4.5 %collective-permute-done.10.refs_2_ = s16[520,128]{1,0:T(8,128)(2,1)S(1)} collective-permute-done((s16[520,128]{1,0:T(8,128)(2,1)S(1)}, s16[520,128]{1,0:T(8,128)(2,1)S(1)}, u32[]{:S(2)}, u32[]{:S(2)}) %collective-permute-start.10) | collective-permute-done | bytes 133152 | tf_op jit(solution)/shard_map/ppermute | solution.py:447
  53.8 4.9 %collective-permute-done.11.refs_3_ = s16[520,128]{1,0:T(8,128)(2,1)S(1)} collective-permute-done((s16[520,128]{1,0:T(8,128)(2,1)S(1)}, s16[520,128]{1,0:T(8,128)(2,1)S(1)}, u32[]{:S(2)}, u32[]{:S(2)}) %collective-permute-start.11) | collective-permute-done | bytes 133152 | tf_op jit(solution)/shard_map/ppermute | solution.py:447
  58.7 0.0 collective-permute-done.12.refs_4_
  58.7 1.0 %image_early.1.sum_ref = f32[2,256,1024]{2,1,0:T(8,128)S(1)} custom-call(bf16[2,256,192]{2,1,0:T(8,128)(2,1)S(1)} %get-tuple-element.34.table_ref, s16[520,128]{1,0:T(8,128)(2,1)S(1)} %collective-permute-done.8.refs_0_, s16[520,128]{1,0:T(8,128)(2,1)S(1)} %collective-permute-done.9.refs_1_, s16[520,128]{1,0:T(8,128)(2,1)S(1)} %collective-permute-done.10.refs_2_, ...), custom_call_target="tpu_custom_call" | custom-call | tf_op jit(solution)/shard_map/image_early/pallas_call | solution.py:515
  59.7 0.0 collective-permute-done.13.refs_0_
  59.7 0.0 collective-permute-done.14.refs_1_
  59.8 1.2 %image.1 = bf16[512,1024]{1,0:T(8,128)(2,1)} custom-call(bf16[256,192]{1,0:T(8,128)(2,1)S(1)} %get-tuple-element.33.table_ref, f32[2,256,1024]{2,1,0:T(8,128)S(1)} %image_early.1.sum_ref, s16[520,128]{1,0:T(8,128)(2,1)S(1)} %collective-permute-done.13.refs_0_, s16[520,128]{1,0:T(8,128)(2,1)S(1)} %collective-permute-done.14.refs_1_), custom_call_target="tpu_custom_call" | custom-call | tf_op jit(solution)/shard_map/image/pallas_call | solution.py:518
Async XLA Ops:
  0.0 1.2 %copy-start.1 = (bf16[2,32,8,1024]{3,2,1,0:T(8,128)(2,1)S(1)}, bf16[2,32,8,1024]{3,2,1,0:T(8,128)(2,1)}, u32[]{:S(2)}) copy-start(bf16[2,32,8,1024]{3,2,1,0:T(8,128)(2,1)} %param.4) | copy-start | bytes 3145732
  2.6 9.5 %collective-permute-start = (s16[520,128]{1,0:T(8,128)(2,1)S(1)}, s16[520,128]{1,0:T(8,128)(2,1)S(1)}, u32[]{:S(2)}, u32[]{:S(2)}) collective-permute-start(s16[520,128]{1,0:T(8,128)(2,1)S(1)} %get-tuple-element.38), channel_id=1, source_target_pairs={{0,12},{2,14},{4,8},{6,10},{8,4},{10,6},{12,0},{14,2},{1,13},{3,15... | collective-permute-start | bytes 399368 | tf_op jit(solution)/shard_map/ppermute | solution.py:447
  7.7 9.0 %collective-permute-start.1 = (s16[520,128]{1,0:T(8,128)(2,1)S(1)}, s16[520,128]{1,0:T(8,128)(2,1)S(1)}, u32[]{:S(2)}, u32[]{:S(2)}) collective-permute-start(s16[520,128]{1,0:T(8,128)(2,1)S(1)} %get-tuple-element.39), channel_id=1, source_target_pairs={{0,4},{2,6},{4,0},{6,2},{8,12},{10,14},{12,8},{14,10},{1,5},{3,7},... | collective-permute-start | bytes 399368 | tf_op jit(solution)/shard_map/ppermute | solution.py:447
  7.7 15.5 %collective-permute-start.2 = (s16[520,128]{1,0:T(8,128)(2,1)S(1)}, s16[520,128]{1,0:T(8,128)(2,1)S(1)}, u32[]{:S(2)}, u32[]{:S(2)}) collective-permute-start(s16[520,128]{1,0:T(8,128)(2,1)S(1)} %get-tuple-element.40), channel_id=1, source_target_pairs={{0,8},{2,10},{4,12},{6,14},{8,0},{10,2},{12,4},{14,6},{1,9},{3,11}... | collective-permute-start | bytes 399368 | tf_op jit(solution)/shard_map/ppermute | solution.py:447
  8.3 21.1 %collective-permute-start.3 = (s16[520,128]{1,0:T(8,128)(2,1)S(1)}, s16[520,128]{1,0:T(8,128)(2,1)S(1)}, u32[]{:S(2)}, u32[]{:S(2)}) collective-permute-start(s16[520,128]{1,0:T(8,128)(2,1)S(1)} %get-tuple-element.41), channel_id=1, source_target_pairs={{0,10},{2,8},{4,14},{6,12},{8,2},{10,0},{12,6},{14,4},{1,11},{3,9}... | collective-permute-start | bytes 399368 | tf_op jit(solution)/shard_map/ppermute | solution.py:447
  11.5 17.8 %collective-permute-start.4 = (s16[520,128]{1,0:T(8,128)(2,1)S(1)}, s16[520,128]{1,0:T(8,128)(2,1)S(1)}, u32[]{:S(2)}, u32[]{:S(2)}) collective-permute-start(s16[520,128]{1,0:T(8,128)(2,1)S(1)} %get-tuple-element.42), channel_id=1, source_target_pairs={{0,2},{2,0},{4,6},{6,4},{8,10},{10,8},{12,14},{14,12},{1,3},{3,1},... | collective-permute-start | bytes 399368 | tf_op jit(solution)/shard_map/ppermute | solution.py:447
  12.1 18.4 %collective-permute-start.5 = (s16[520,128]{1,0:T(8,128)(2,1)S(1)}, s16[520,128]{1,0:T(8,128)(2,1)S(1)}, u32[]{:S(2)}, u32[]{:S(2)}) collective-permute-start(s16[520,128]{1,0:T(8,128)(2,1)S(1)} %get-tuple-element.43), channel_id=1, source_target_pairs={{0,6},{2,4},{4,2},{6,0},{8,14},{10,12},{12,10},{14,8},{1,7},{3,5},... | collective-permute-start | bytes 399368 | tf_op jit(solution)/shard_map/ppermute | solution.py:447
  16.7 13.8 %collective-permute-start.6 = (s16[520,128]{1,0:T(8,128)(2,1)S(1)}, s16[520,128]{1,0:T(8,128)(2,1)S(1)}, u32[]{:S(2)}, u32[]{:S(2)}) collective-permute-start(s16[520,128]{1,0:T(8,128)(2,1)S(1)} %get-tuple-element.44), channel_id=1, source_target_pairs={{0,14},{2,12},{4,10},{6,8},{8,6},{10,4},{12,2},{14,0},{1,15},{3,13... | collective-permute-start | bytes 399368 | tf_op jit(solution)/shard_map/ppermute | solution.py:447
  18.3 0.9 %copy-start.2 = (f32[2,128,256]{2,1,0:T(8,128)S(1)}, f32[2,128,256]{2,1,0:T(8,128)}, u32[]{:S(2)}) copy-start(f32[2,128,256]{2,1,0:T(8,128)} %constant.10.clone.base_ref) | copy-start | bytes 786436
  19.2 0.7 %copy-start.3 = (s32[4,16]{1,0:T(4,128)S(1)}, s32[4,16]{1,0:T(4,128)}, u32[]{:S(2)}) copy-start(s32[4,16]{1,0:T(4,128)} %band_ref.1) | copy-start | bytes 772
  30.4 1.6 %copy-start = (bf16[4,8,256,128]{3,2,1,0:T(8,128)(2,1)S(1)}, bf16[4,8,256,128]{3,2,1,0:T(8,128)(2,1)}, u32[]{:S(2)}) copy-start(bf16[4,8,256,128]{3,2,1,0:T(8,128)(2,1)} %weights_ref.3) | copy-start | bytes 6291460
  31.0 2.7 %collective-permute-start.7 = (bf16[2,512,128]{2,1,0:T(8,128)(2,1)S(1)}, bf16[2,512,128]{2,1,0:T(8,128)(2,1)S(1)}, u32[]{:S(2)}, u32[]{:S(2)}) collective-permute-start(bf16[2,512,128]{2,1,0:T(8,128)(2,1)S(1)} %get-tuple-element.46), channel_id=1, source_target_pairs={{0,1},{1,0},{2,3},{3,2},{4,5},{5,4},{6,7},{7,6},{8,9},{9,8},{10,11... | collective-permute-start | bytes 786440 | tf_op jit(solution)/shard_map/ppermute | solution.py:494
  35.4 8.3 %collective-permute-start.8 = (s16[520,128]{1,0:T(8,128)(2,1)S(1)}, s16[520,128]{1,0:T(8,128)(2,1)S(1)}, u32[]{:S(2)}, u32[]{:S(2)}) collective-permute-start(s16[520,128]{1,0:T(8,128)(2,1)S(1)} %get-tuple-element.48), channel_id=1, source_target_pairs={{0,12},{2,14},{4,8},{6,10},{8,4},{10,6},{12,0},{14,2},{1,13},{3,15... | collective-permute-start | bytes 399368 | tf_op jit(solution)/shard_map/ppermute | solution.py:447
  37.8 8.5 %collective-permute-start.9 = (s16[520,128]{1,0:T(8,128)(2,1)S(1)}, s16[520,128]{1,0:T(8,128)(2,1)S(1)}, u32[]{:S(2)}, u32[]{:S(2)}) collective-permute-start(s16[520,128]{1,0:T(8,128)(2,1)S(1)} %get-tuple-element.49), channel_id=1, source_target_pairs={{0,4},{2,6},{4,0},{6,2},{8,12},{10,14},{12,8},{14,10},{1,5},{3,7},... | collective-permute-start | bytes 399368 | tf_op jit(solution)/shard_map/ppermute | solution.py:447
  38.9 14.9 %collective-permute-start.10 = (s16[520,128]{1,0:T(8,128)(2,1)S(1)}, s16[520,128]{1,0:T(8,128)(2,1)S(1)}, u32[]{:S(2)}, u32[]{:S(2)}) collective-permute-start(s16[520,128]{1,0:T(8,128)(2,1)S(1)} %get-tuple-element.51), channel_id=1, source_target_pairs={{0,8},{2,10},{4,12},{6,14},{8,0},{10,2},{12,4},{14,6},{1,9},{3,11}... | collective-permute-start | bytes 399368 | tf_op jit(solution)/shard_map/ppermute | solution.py:447
  41.0 17.7 %collective-permute-start.11 = (s16[520,128]{1,0:T(8,128)(2,1)S(1)}, s16[520,128]{1,0:T(8,128)(2,1)S(1)}, u32[]{:S(2)}, u32[]{:S(2)}) collective-permute-start(s16[520,128]{1,0:T(8,128)(2,1)S(1)} %get-tuple-element.52), channel_id=1, source_target_pairs={{0,10},{2,8},{4,14},{6,12},{8,2},{10,0},{12,6},{14,4},{1,11},{3,9}... | collective-permute-start | bytes 399368 | tf_op jit(solution)/shard_map/ppermute | solution.py:447
  41.8 16.8 %collective-permute-start.12 = (s16[520,128]{1,0:T(8,128)(2,1)S(1)}, s16[520,128]{1,0:T(8,128)(2,1)S(1)}, u32[]{:S(2)}, u32[]{:S(2)}) collective-permute-start(s16[520,128]{1,0:T(8,128)(2,1)S(1)} %get-tuple-element.53), channel_id=1, source_target_pairs={{0,2},{2,0},{4,6},{6,4},{8,10},{10,8},{12,14},{14,12},{1,3},{3,1},... | collective-permute-start | bytes 399368 | tf_op jit(solution)/shard_map/ppermute | solution.py:447
  43.7 16.0 %collective-permute-start.13 = (s16[520,128]{1,0:T(8,128)(2,1)S(1)}, s16[520,128]{1,0:T(8,128)(2,1)S(1)}, u32[]{:S(2)}, u32[]{:S(2)}) collective-permute-start(s16[520,128]{1,0:T(8,128)(2,1)S(1)} %get-tuple-element.55), channel_id=1, source_target_pairs={{0,6},{2,4},{4,2},{6,0},{8,14},{10,12},{12,10},{14,8},{1,7},{3,5},... | collective-permute-start | bytes 399368 | tf_op jit(solution)/shard_map/ppermute | solution.py:447
  46.3 13.4 %collective-permute-start.14 = (s16[520,128]{1,0:T(8,128)(2,1)S(1)}, s16[520,128]{1,0:T(8,128)(2,1)S(1)}, u32[]{:S(2)}, u32[]{:S(2)}) collective-permute-start(s16[520,128]{1,0:T(8,128)(2,1)S(1)} %get-tuple-element.56), channel_id=1, source_target_pairs={{0,14},{2,12},{4,10},{6,8},{8,6},{10,4},{12,2},{14,0},{1,15},{3,13... | collective-permute-start | bytes 399368 | tf_op jit(solution)/shard_map/ppermute | solution.py:447

commit v8 on v7

--- a/solution.py
+++ b/solution.py
@@ -132,6 +132,8 @@
 LATE = (3, 7)
 EARLY_ROWS = 192
 LEAD = (2,)
+SPREAD_LEAD = (6, )
+SPREAD_REST = (2, 4, 5, 1, 3, 7, 0, )
 REST = (0, 1, 3)
 VMEM_LIMIT = 20 * 1024 * 1024
 
@@ -227,8 +229,9 @@
     return (1 - 2 * (me // 4)).astype(F32)
 
 
-def spread_kernel(me_ref, x_ref, *out_refs):
-    hi, lo = split2(short_table(me_ref[0]))
+def spread_kernel(which, me_ref, x_ref, *out_refs):
+    table = short_table(me_ref[0])
+    hi, lo = split2(jnp.concatenate([table[i * 32 : (i + 1) * 32] for i in which], 0))
     halves = []
     for h in range(2):
         at = h * 128
@@ -458,9 +461,15 @@
     message = jax.ShapeDtypeStruct((TILES * ROWS + TAIL, TILE), jnp.int16)
     early_shape = (2, LINES_DEV, EARLY_ROWS)
 
-    sent = vmem_call(spread_kernel, "spread", [message] * NDEV, smem=1, vmem=1)(
-        me, raw.reshape(LINES, bins)
-    )
+    rows = raw.reshape(LINES, bins)
+    sent = [None] * NDEV
+    for name, which in (("spread", SPREAD_LEAD), ("spread_rest", SPREAD_REST)):
+        own = me if name == "spread" else after(me, sent[SPREAD_LEAD[0]])
+        made = vmem_call(functools.partial(spread_kernel, which), name, [message] * len(which), smem=1, vmem=1)(
+            own, rows
+        )
+        for n, i in enumerate(which):
+            sent[i] = made[n]
     got_early, got_late = exchange(sent)
     forward_table, forward_late, inverse_table, image_table, image_late, starts = vmem_call(
         tables_kernel,
@@ -475,7 +484,7 @@
         ],
         smem=1,
         vmem=2,
-    )(after(me, sent[0]), band_start, jnp.asarray(long_base()))
+    )(after(me, sent[SPREAD_REST[0]]), band_start, jnp.asarray(long_base()))
 
     partial = vmem_call(
         forward_early_kernel,

time: 61.2 us -> 59.5 us (0.972)
  starting transfers between devices: 27.7 us -> 33.3 us
  waiting for transfers between devices: 19.1 us -> 13.7 us
  local copies, waits for them, and re-layouts: 3.82 us -> 1.25 us
    ppermute x14, starting transfers between devices: 27.6 us -> 33.2 us  [exchange(): lax.ppermute(messages[i], 'az', [(d, d ^ i) for d in range(NDEV)])]
    ppermute x14, waiting for transfers between devices: 19.1 us -> 13.7 us  [exchange(): lax.ppermute(messages[i], 'az', [(d, d ^ i) for d in range(NDEV)])]
    unnamed x8, local copies, waits for them, and re-layouts: 3.82 us -> 1.25 us
    pallas_call x1 -> x2, Pallas kernels: 1.32 us -> 1.75 us  [fast_body(): vmem_call(functools.partial(spread_kernel, which), name, [message] * len(...]
  transfers between devices with their start and end apart: 15 -> 15, of which waited for: 6 -> 8; matrix products, arithmetic and copies ran while one was open for 0% -> 0% of each run, Pallas kernels for 9% -> 11%
where the time goes in v8:
time: 59.5 us; the launch traced here: 59.1 us
  starting transfers between devices  33.3 us (56%)
  waiting for transfers between devices  13.7 us (23%)
  Pallas kernels  10.7 us (18%)
  local copies, waits for them, and re-layouts  1.25 us (2%)
    ppermute x14, starting transfers between devices, exchange(): lax.ppermute(messages[i], 'az', [(d, d ^ i) for d in range(NDEV)])  33.2 us
    ppermute x14, waiting for transfers between devices, exchange(): lax.ppermute(messages[i], 'az', [(d, d ^ i) for d in range(NDEV)])  13.7 us
    pallas_call x2, Pallas kernels, fast_body(): vmem_call(functools.partial(spread_kernel, which), name, [message] * len(...  1.75 us
    pallas_call x1, Pallas kernels, fast_body(): vmem_call(inner_kernel, 'inner', jax.ShapeDtypeStruct((2, 2, TILES, LINES...  1.67 us
    pallas_call x1, Pallas kernels, fast_body(): vmem_call(outer_kernel, 'outer', [message, message, jax.ShapeDtypeStruct(...  1.62 us
    unnamed x8, local copies, waits for them, and re-layouts  1.25 us
    pallas_call x1, Pallas kernels, fast_body(): vmem_call(image_kernel, 'image', jax.ShapeDtypeStruct((LINES, bins), BF16...  1.24 us
  transfers between devices with their start and end apart: 15, of which 8 were waited for; matrix products, arithmetic and copies ran while one was open for 0% of the time, Pallas kernels for 11%

profile of v8, /device:TPU:0, one launch (start us, length us, event | category | flops | bytes accessed | tf_op | source)
XLA Modules:
  0.0 59.1 jit_solution(11951671627517274845)
XLA Ops:
  0.0 0.0 copy-start.3
  0.0 0.0 copy-start.1
  0.0 1.2 %copy-done.1 = bf16[2,32,8,1024]{3,2,1,0:T(8,128)(2,1)S(1)} copy-done((bf16[2,32,8,1024]{3,2,1,0:T(8,128)(2,1)S(1)}, bf16[2,32,8,1024]{3,2,1,0:T(8,128)(2,1)}, u32[]{:S(2)}) %copy-start.1) | copy-done | bytes 1048600
  1.2 0.0 copy-start.2
  1.2 0.6 spread.1
  1.8 5.1 %collective-permute-start = (s16[520,128]{1,0:T(8,128)(2,1)S(1)}, s16[520,128]{1,0:T(8,128)(2,1)S(1)}, u32[]{:S(2)}, u32[]{:S(2)}) collective-permute-start(s16[520,128]{1,0:T(8,128)(2,1)S(1)} %spread.1), channel_id=1, source_target_pairs={{0,12},{2,14},{4,8},{6,10},{8,4},{10,6},{12,0},{14,2},{1,13},{3,15... | collective-permute-start | bytes 399368 | tf_op jit(solution)/shard_map/ppermute | solution.py:450
  6.9 1.2 %spread_rest.1 = (s16[520,128]{1,0:T(8,128)(2,1)S(1)}, s16[520,128]{1,0:T(8,128)(2,1)S(1)}, s16[520,128]{1,0:T(8,128)(2,1)S(1)}, s16[520,128]{1,0:T(8,128)(2,1)S...) custom-call(s32[1]{0:T(128)} %bitcast.me_ref, ...), custom_call_target="tpu_custom_call" | custom-call | tf_op jit(solution)/shard_map/spread_rest/pallas_call | solution.py:468
  8.1 0.1 collective-permute-start.2
  8.2 3.8 %collective-permute-start.3 = (s16[520,128]{1,0:T(8,128)(2,1)S(1)}, s16[520,128]{1,0:T(8,128)(2,1)S(1)}, u32[]{:S(2)}, u32[]{:S(2)}) collective-permute-start(s16[520,128]{1,0:T(8,128)(2,1)S(1)} %get-tuple-element.40), channel_id=1, source_target_pairs={{0,10},{2,8},{4,14},{6,12},{8,2},{10,0},{12,6},{14,4},{1,11},{3,9}... | collective-permute-start | bytes 399368 | tf_op jit(solution)/shard_map/ppermute | solution.py:450
  12.1 0.5 collective-permute-start.4
  12.6 0.0 collective-permute-start.1
  12.6 0.0 collective-permute-done.refs_0_
  12.6 8.1 %collective-permute-start.5 = (s16[520,128]{1,0:T(8,128)(2,1)S(1)}, s16[520,128]{1,0:T(8,128)(2,1)S(1)}, u32[]{:S(2)}, u32[]{:S(2)}) collective-permute-start(s16[520,128]{1,0:T(8,128)(2,1)S(1)} %get-tuple-element.43), channel_id=1, source_target_pairs={{0,6},{2,4},{4,2},{6,0},{8,14},{10,12},{12,10},{14,8},{1,7},{3,5},... | collective-permute-start | bytes 399368 | tf_op jit(solution)/shard_map/ppermute | solution.py:450
  20.6 1.5 %collective-permute-done.2.refs_2_ = s16[520,128]{1,0:T(8,128)(2,1)S(1)} collective-permute-done((s16[520,128]{1,0:T(8,128)(2,1)S(1)}, s16[520,128]{1,0:T(8,128)(2,1)S(1)}, u32[]{:S(2)}, u32[]{:S(2)}) %collective-permute-start.2) | collective-permute-done | bytes 133152 | tf_op jit(solution)/shard_map/ppermute | solution.py:450
  22.1 3.2 %collective-permute-start.6 = (s16[520,128]{1,0:T(8,128)(2,1)S(1)}, s16[520,128]{1,0:T(8,128)(2,1)S(1)}, u32[]{:S(2)}, u32[]{:S(2)}) collective-permute-start(s16[520,128]{1,0:T(8,128)(2,1)S(1)} %get-tuple-element.44), channel_id=1, source_target_pairs={{0,14},{2,12},{4,10},{6,8},{8,6},{10,4},{12,2},{14,0},{1,15},{3,13... | collective-permute-start | bytes 399368 | tf_op jit(solution)/shard_map/ppermute | solution.py:450
  25.4 0.0 copy-done.3
  25.4 0.0 copy-done.2
  25.4 0.7 %tables.1 = (bf16[2,2,256,192]{3,2,1,0:T(8,128)(2,1)S(1)}, bf16[2,256,192]{2,1,0:T(8,128)(2,1)S(1)}, bf16[2,2,256,256]{3,2,1,0:T(8,128)(2,1)S(1)}, bf16[2,256,19...) custom-call(s32[1]{0:T(128)} %bitcast.me_ref, s32[4,16]{1,0:T(4,128)S(1)} %copy-done.3, ...), custom_call_target="tpu_custom_call" | custom-call | tf_op jit(solution)/shard_map/tables/pallas_call | solution.py:474
  26.1 0.1 collective-permute-done.3.refs_3_
  26.2 0.0 collective-permute-done.4.refs_4_
  26.2 0.0 collective-permute-done.1.refs_1_
  26.2 1.1 %forward_early.1.sum_ref = f32[2,256,1024]{2,1,0:T(8,128)S(1)} custom-call(s32[1]{0:T(128)} %bitcast.me_ref, bf16[2,2,256,192]{3,2,1,0:T(8,128)(2,1)S(1)} %get-tuple-element.38.table_ref, s16[520,128]{1,0:T(8,128)(2,1)S(1)} %collective-permute-done.refs_0_, s16[520,128]{1,0:T(8,128)(2,1)S(1)} %collective-permute-done.1.refs_1_, ...), custom_call_target="tpu_custom_call" | custom-call | tf_op jit(solution)/shard_map/forward_early/pallas_call | solution.py:489
  27.3 0.0 copy-start
  27.3 3.0 %collective-permute-done.5.refs_0_ = s16[520,128]{1,0:T(8,128)(2,1)S(1)} collective-permute-done((s16[520,128]{1,0:T(8,128)(2,1)S(1)}, s16[520,128]{1,0:T(8,128)(2,1)S(1)}, u32[]{:S(2)}, u32[]{:S(2)}) %collective-permute-start.5) | collective-permute-done | bytes 133152 | tf_op jit(solution)/shard_map/ppermute | solution.py:450
  30.2 0.0 collective-permute-done.6.refs_1_
  30.3 0.5 forward.1
  30.8 0.1 collective-permute-start.7
  30.8 0.0 copy-done
  30.9 1.7 %inner.1.focus_ref = bf16[2,2,8,256,128]{4,3,2,1,0:T(8,128)(2,1)S(1)} custom-call(s32[1]{0:T(128)} %bitcast.2.rg_ref, s32[4,16]{1,0:T(4,128)S(1)} %get-tuple-element.36.starts_ref, bf16[8,2,512,128]{3,2,1,0:T(8,128)(2,1)S(1)} %get-tuple-element.45.spectrum_ref, bf16[4,8,256,128]{3,2,1,0:T(8,128)(2,1)S(1)} %copy-done), custom_call_target="tpu_custom_call" | custom-call | tf_op jit(solution)/shard_map/inner/pallas_call | solution.py:504
  32.5 0.0 collective-permute-done.7.halo_ref
  32.5 1.6 %outer.1 = (s16[520,128]{1,0:T(8,128)(2,1)S(1)}, s16[520,128]{1,0:T(8,128)(2,1)S(1)}, bf16[2,2,256,128]{3,2,1,0:T(8,128)(2,1)S(1)}) custom-call(s32[1]{0:T(128)} %bitcast.me_ref, s32[1]{0:T(128)} %bitcast.2.rg_ref, s32[4,16]{1,0:T(4,128)S(1)} %get-tuple-element.36.starts_ref, bf16[8,2,512,128]{3,2,1,0:T(8,128)(2,1)S(1)} %get-tuple-element.45.spectrum_ref, ...), custom_call_target="tpu_custom_call" | custom-call | tf_op jit(solution)/shard_map/outer/pallas_call | solution.py:512
  34.2 2.0 %collective-permute-start.8 = (s16[520,128]{1,0:T(8,128)(2,1)S(1)}, s16[520,128]{1,0:T(8,128)(2,1)S(1)}, u32[]{:S(2)}, u32[]{:S(2)}) collective-permute-start(s16[520,128]{1,0:T(8,128)(2,1)S(1)} %get-tuple-element.48), channel_id=1, source_target_pairs={{0,12},{2,14},{4,8},{6,10},{8,4},{10,6},{12,0},{14,2},{1,13},{3,15... | collective-permute-start | bytes 399368 | tf_op jit(solution)/shard_map/ppermute | solution.py:450
  36.2 0.5 collective-permute-start.9
  36.7 1.1 %rest.1 = (s16[520,128]{1,0:T(8,128)(2,1)S(1)}, s16[520,128]{1,0:T(8,128)(2,1)S(1)}, s16[520,128]{1,0:T(8,128)(2,1)S(1)}, s16[520,128]{1,0:T(8,128)(2,1)S(1)}, s...) custom-call(s32[1]{0:T(128)} %bitcast.me_ref, s32[1]{0:T(128)} %bitcast.2.rg_ref, ...), custom_call_target="tpu_custom_call" | custom-call | tf_op jit(solution)/shard_map/rest/pallas_call | solution.py:520
  37.8 2.0 %collective-permute-start.10 = (s16[520,128]{1,0:T(8,128)(2,1)S(1)}, s16[520,128]{1,0:T(8,128)(2,1)S(1)}, u32[]{:S(2)}, u32[]{:S(2)}) collective-permute-start(s16[520,128]{1,0:T(8,128)(2,1)S(1)} %get-tuple-element.51), channel_id=1, source_target_pairs={{0,8},{2,10},{4,12},{6,14},{8,0},{10,2},{12,4},{14,6},{1,9},{3,11}... | collective-permute-start | bytes 399368 | tf_op jit(solution)/shard_map/ppermute | solution.py:450
  39.8 1.4 %collective-permute-start.11 = (s16[520,128]{1,0:T(8,128)(2,1)S(1)}, s16[520,128]{1,0:T(8,128)(2,1)S(1)}, u32[]{:S(2)}, u32[]{:S(2)}) collective-permute-start(s16[520,128]{1,0:T(8,128)(2,1)S(1)} %get-tuple-element.52), channel_id=1, source_target_pairs={{0,10},{2,8},{4,14},{6,12},{8,2},{10,0},{12,6},{14,4},{1,11},{3,9}... | collective-permute-start | bytes 399368 | tf_op jit(solution)/shard_map/ppermute | solution.py:450
  41.2 1.0 %collective-permute-start.12 = (s16[520,128]{1,0:T(8,128)(2,1)S(1)}, s16[520,128]{1,0:T(8,128)(2,1)S(1)}, u32[]{:S(2)}, u32[]{:S(2)}) collective-permute-start(s16[520,128]{1,0:T(8,128)(2,1)S(1)} %get-tuple-element.53), channel_id=1, source_target_pairs={{0,2},{2,0},{4,6},{6,4},{8,10},{10,8},{12,14},{14,12},{1,3},{3,1},... | collective-permute-start | bytes 399368 | tf_op jit(solution)/shard_map/ppermute | solution.py:450
  42.3 0.2 collective-permute-done.8.refs_0_
  42.4 2.3 %collective-permute-start.13 = (s16[520,128]{1,0:T(8,128)(2,1)S(1)}, s16[520,128]{1,0:T(8,128)(2,1)S(1)}, u32[]{:S(2)}, u32[]{:S(2)}) collective-permute-start(s16[520,128]{1,0:T(8,128)(2,1)S(1)} %get-tuple-element.55), channel_id=1, source_target_pairs={{0,6},{2,4},{4,2},{6,0},{8,14},{10,12},{12,10},{14,8},{1,7},{3,5},... | collective-permute-start | bytes 399368 | tf_op jit(solution)/shard_map/ppermute | solution.py:450
  44.7 1.9 %collective-permute-done.9.refs_1_ = s16[520,128]{1,0:T(8,128)(2,1)S(1)} collective-permute-done((s16[520,128]{1,0:T(8,128)(2,1)S(1)}, s16[520,128]{1,0:T(8,128)(2,1)S(1)}, u32[]{:S(2)}, u32[]{:S(2)}) %collective-permute-start.9) | collective-permute-done | bytes 133152 | tf_op jit(solution)/shard_map/ppermute | solution.py:450
  46.6 3.1 %collective-permute-start.14 = (s16[520,128]{1,0:T(8,128)(2,1)S(1)}, s16[520,128]{1,0:T(8,128)(2,1)S(1)}, u32[]{:S(2)}, u32[]{:S(2)}) collective-permute-start(s16[520,128]{1,0:T(8,128)(2,1)S(1)} %get-tuple-element.56), channel_id=1, source_target_pairs={{0,14},{2,12},{4,10},{6,8},{8,6},{10,4},{12,2},{14,0},{1,15},{3,13... | collective-permute-start | bytes 399368 | tf_op jit(solution)/shard_map/ppermute | solution.py:450
  49.7 2.6 %collective-permute-done.10.refs_2_ = s16[520,128]{1,0:T(8,128)(2,1)S(1)} collective-permute-done((s16[520,128]{1,0:T(8,128)(2,1)S(1)}, s16[520,128]{1,0:T(8,128)(2,1)S(1)}, u32[]{:S(2)}, u32[]{:S(2)}) %collective-permute-start.10) | collective-permute-done | bytes 133152 | tf_op jit(solution)/shard_map/ppermute | solution.py:450
  52.3 3.0 %collective-permute-done.11.refs_3_ = s16[520,128]{1,0:T(8,128)(2,1)S(1)} collective-permute-done((s16[520,128]{1,0:T(8,128)(2,1)S(1)}, s16[520,128]{1,0:T(8,128)(2,1)S(1)}, u32[]{:S(2)}, u32[]{:S(2)}) %collective-permute-start.11) | collective-permute-done | bytes 133152 | tf_op jit(solution)/shard_map/ppermute | solution.py:450
  55.3 0.0 collective-permute-done.12.refs_4_
  55.3 1.0 %image_early.1.sum_ref = f32[2,256,1024]{2,1,0:T(8,128)S(1)} custom-call(bf16[2,256,192]{2,1,0:T(8,128)(2,1)S(1)} %get-tuple-element.35.table_ref, s16[520,128]{1,0:T(8,128)(2,1)S(1)} %collective-permute-done.8.refs_0_, s16[520,128]{1,0:T(8,128)(2,1)S(1)} %collective-permute-done.9.refs_1_, s16[520,128]{1,0:T(8,128)(2,1)S(1)} %collective-permute-done.10.refs_2_, ...), custom_call_target="tpu_custom_call" | custom-call | tf_op jit(solution)/shard_map/image_early/pallas_call | solution.py:524
  56.4 0.0 collective-permute-done.13.refs_0_
  56.4 1.4 %collective-permute-done.14.refs_1_ = s16[520,128]{1,0:T(8,128)(2,1)S(1)} collective-permute-done((s16[520,128]{1,0:T(8,128)(2,1)S(1)}, s16[520,128]{1,0:T(8,128)(2,1)S(1)}, u32[]{:S(2)}, u32[]{:S(2)}) %collective-permute-start.14) | collective-permute-done | bytes 133152 | tf_op jit(solution)/shard_map/ppermute | solution.py:450
  57.9 1.2 %image.1 = bf16[512,1024]{1,0:T(8,128)(2,1)} custom-call(bf16[256,192]{1,0:T(8,128)(2,1)S(1)} %get-tuple-element.34.table_ref, f32[2,256,1024]{2,1,0:T(8,128)S(1)} %image_early.1.sum_ref, s16[520,128]{1,0:T(8,128)(2,1)S(1)} %collective-permute-done.13.refs_0_, s16[520,128]{1,0:T(8,128)(2,1)S(1)} %collective-permute-done.14.refs_1_), custom_call_target="tpu_custom_call" | custom-call | tf_op jit(solution)/shard_map/image/pallas_call | solution.py:527
Async XLA Ops:
  0.0 25.4 %copy-start.3 = (s32[4,16]{1,0:T(4,128)S(1)}, s32[4,16]{1,0:T(4,128)}, u32[]{:S(2)}) copy-start(s32[4,16]{1,0:T(4,128)} %band_ref.1) | copy-start | bytes 772
  0.0 1.2 %copy-start.1 = (bf16[2,32,8,1024]{3,2,1,0:T(8,128)(2,1)S(1)}, bf16[2,32,8,1024]{3,2,1,0:T(8,128)(2,1)}, u32[]{:S(2)}) copy-start(bf16[2,32,8,1024]{3,2,1,0:T(8,128)(2,1)} %param.4) | copy-start | bytes 3145732
  1.2 24.1 %copy-start.2 = (f32[2,128,256]{2,1,0:T(8,128)S(1)}, f32[2,128,256]{2,1,0:T(8,128)}, u32[]{:S(2)}) copy-start(f32[2,128,256]{2,1,0:T(8,128)} %constant.10.clone.base_ref) | copy-start | bytes 786436
  1.8 10.8 %collective-permute-start = (s16[520,128]{1,0:T(8,128)(2,1)S(1)}, s16[520,128]{1,0:T(8,128)(2,1)S(1)}, u32[]{:S(2)}, u32[]{:S(2)}) collective-permute-start(s16[520,128]{1,0:T(8,128)(2,1)S(1)} %spread.1), channel_id=1, source_target_pairs={{0,12},{2,14},{4,8},{6,10},{8,4},{10,6},{12,0},{14,2},{1,13},{3,15... | collective-permute-start | bytes 399368 | tf_op jit(solution)/shard_map/ppermute | solution.py:450
  8.1 14.0 %collective-permute-start.2 = (s16[520,128]{1,0:T(8,128)(2,1)S(1)}, s16[520,128]{1,0:T(8,128)(2,1)S(1)}, u32[]{:S(2)}, u32[]{:S(2)}) collective-permute-start(s16[520,128]{1,0:T(8,128)(2,1)S(1)} %get-tuple-element.39), channel_id=1, source_target_pairs={{0,8},{2,10},{4,12},{6,14},{8,0},{10,2},{12,4},{14,6},{1,9},{3,11}... | collective-permute-start | bytes 399368 | tf_op jit(solution)/shard_map/ppermute | solution.py:450
  8.2 18.0 %collective-permute-start.3 = (s16[520,128]{1,0:T(8,128)(2,1)S(1)}, s16[520,128]{1,0:T(8,128)(2,1)S(1)}, u32[]{:S(2)}, u32[]{:S(2)}) collective-permute-start(s16[520,128]{1,0:T(8,128)(2,1)S(1)} %get-tuple-element.40), channel_id=1, source_target_pairs={{0,10},{2,8},{4,14},{6,12},{8,2},{10,0},{12,6},{14,4},{1,11},{3,9}... | collective-permute-start | bytes 399368 | tf_op jit(solution)/shard_map/ppermute | solution.py:450
  12.1 14.1 %collective-permute-start.4 = (s16[520,128]{1,0:T(8,128)(2,1)S(1)}, s16[520,128]{1,0:T(8,128)(2,1)S(1)}, u32[]{:S(2)}, u32[]{:S(2)}) collective-permute-start(s16[520,128]{1,0:T(8,128)(2,1)S(1)} %get-tuple-element.41), channel_id=1, source_target_pairs={{0,2},{2,0},{4,6},{6,4},{8,10},{10,8},{12,14},{14,12},{1,3},{3,1},... | collective-permute-start | bytes 399368 | tf_op jit(solution)/shard_map/ppermute | solution.py:450
  12.6 13.6 %collective-permute-start.1 = (s16[520,128]{1,0:T(8,128)(2,1)S(1)}, s16[520,128]{1,0:T(8,128)(2,1)S(1)}, u32[]{:S(2)}, u32[]{:S(2)}) collective-permute-start(s16[520,128]{1,0:T(8,128)(2,1)S(1)} %get-tuple-element.32), channel_id=1, source_target_pairs={{0,4},{2,6},{4,0},{6,2},{8,12},{10,14},{12,8},{14,10},{1,5},{3,7},... | collective-permute-start | bytes 399368 | tf_op jit(solution)/shard_map/ppermute | solution.py:450
  12.6 17.7 %collective-permute-start.5 = (s16[520,128]{1,0:T(8,128)(2,1)S(1)}, s16[520,128]{1,0:T(8,128)(2,1)S(1)}, u32[]{:S(2)}, u32[]{:S(2)}) collective-permute-start(s16[520,128]{1,0:T(8,128)(2,1)S(1)} %get-tuple-element.43), channel_id=1, source_target_pairs={{0,6},{2,4},{4,2},{6,0},{8,14},{10,12},{12,10},{14,8},{1,7},{3,5},... | collective-permute-start | bytes 399368 | tf_op jit(solution)/shard_map/ppermute | solution.py:450
  22.1 8.1 %collective-permute-start.6 = (s16[520,128]{1,0:T(8,128)(2,1)S(1)}, s16[520,128]{1,0:T(8,128)(2,1)S(1)}, u32[]{:S(2)}, u32[]{:S(2)}) collective-permute-start(s16[520,128]{1,0:T(8,128)(2,1)S(1)} %get-tuple-element.44), channel_id=1, source_target_pairs={{0,14},{2,12},{4,10},{6,8},{8,6},{10,4},{12,2},{14,0},{1,15},{3,13... | collective-permute-start | bytes 399368 | tf_op jit(solution)/shard_map/ppermute | solution.py:450
  27.3 3.6 %copy-start = (bf16[4,8,256,128]{3,2,1,0:T(8,128)(2,1)S(1)}, bf16[4,8,256,128]{3,2,1,0:T(8,128)(2,1)}, u32[]{:S(2)}) copy-start(bf16[4,8,256,128]{3,2,1,0:T(8,128)(2,1)} %weights_ref.3) | copy-start | bytes 6291460
  30.8 1.8 %collective-permute-start.7 = (bf16[2,512,128]{2,1,0:T(8,128)(2,1)S(1)}, bf16[2,512,128]{2,1,0:T(8,128)(2,1)S(1)}, u32[]{:S(2)}, u32[]{:S(2)}) collective-permute-start(bf16[2,512,128]{2,1,0:T(8,128)(2,1)S(1)} %get-tuple-element.46), channel_id=1, source_target_pairs={{0,1},{1,0},{2,3},{3,2},{4,5},{5,4},{6,7},{7,6},{8,9},{9,8},{10,11... | collective-permute-start | bytes 786440 | tf_op jit(solution)/shard_map/ppermute | solution.py:503
  34.2 8.2 %collective-permute-start.8 = (s16[520,128]{1,0:T(8,128)(2,1)S(1)}, s16[520,128]{1,0:T(8,128)(2,1)S(1)}, u32[]{:S(2)}, u32[]{:S(2)}) collective-permute-start(s16[520,128]{1,0:T(8,128)(2,1)S(1)} %get-tuple-element.48), channel_id=1, source_target_pairs={{0,12},{2,14},{4,8},{6,10},{8,4},{10,6},{12,0},{14,2},{1,13},{3,15... | collective-permute-start | bytes 399368 | tf_op jit(solution)/shard_map/ppermute | solution.py:450
  36.2 10.4 %collective-permute-start.9 = (s16[520,128]{1,0:T(8,128)(2,1)S(1)}, s16[520,128]{1,0:T(8,128)(2,1)S(1)}, u32[]{:S(2)}, u32[]{:S(2)}) collective-permute-start(s16[520,128]{1,0:T(8,128)(2,1)S(1)} %get-tuple-element.49), channel_id=1, source_target_pairs={{0,4},{2,6},{4,0},{6,2},{8,12},{10,14},{12,8},{14,10},{1,5},{3,7},... | collective-permute-start | bytes 399368 | tf_op jit(solution)/shard_map/ppermute | solution.py:450
  37.8 14.5 %collective-permute-start.10 = (s16[520,128]{1,0:T(8,128)(2,1)S(1)}, s16[520,128]{1,0:T(8,128)(2,1)S(1)}, u32[]{:S(2)}, u32[]{:S(2)}) collective-permute-start(s16[520,128]{1,0:T(8,128)(2,1)S(1)} %get-tuple-element.51), channel_id=1, source_target_pairs={{0,8},{2,10},{4,12},{6,14},{8,0},{10,2},{12,4},{14,6},{1,9},{3,11}... | collective-permute-start | bytes 399368 | tf_op jit(solution)/shard_map/ppermute | solution.py:450
  39.8 15.6 %collective-permute-start.11 = (s16[520,128]{1,0:T(8,128)(2,1)S(1)}, s16[520,128]{1,0:T(8,128)(2,1)S(1)}, u32[]{:S(2)}, u32[]{:S(2)}) collective-permute-start(s16[520,128]{1,0:T(8,128)(2,1)S(1)} %get-tuple-element.52), channel_id=1, source_target_pairs={{0,10},{2,8},{4,14},{6,12},{8,2},{10,0},{12,6},{14,4},{1,11},{3,9}... | collective-permute-start | bytes 399368 | tf_op jit(solution)/shard_map/ppermute | solution.py:450
  41.2 14.1 %collective-permute-start.12 = (s16[520,128]{1,0:T(8,128)(2,1)S(1)}, s16[520,128]{1,0:T(8,128)(2,1)S(1)}, u32[]{:S(2)}, u32[]{:S(2)}) collective-permute-start(s16[520,128]{1,0:T(8,128)(2,1)S(1)} %get-tuple-element.53), channel_id=1, source_target_pairs={{0,2},{2,0},{4,6},{6,4},{8,10},{10,8},{12,14},{14,12},{1,3},{3,1},... | collective-permute-start | bytes 399368 | tf_op jit(solution)/shard_map/ppermute | solution.py:450
  42.4 14.0 %collective-permute-start.13 = (s16[520,128]{1,0:T(8,128)(2,1)S(1)}, s16[520,128]{1,0:T(8,128)(2,1)S(1)}, u32[]{:S(2)}, u32[]{:S(2)}) collective-permute-start(s16[520,128]{1,0:T(8,128)(2,1)S(1)} %get-tuple-element.55), channel_id=1, source_target_pairs={{0,6},{2,4},{4,2},{6,0},{8,14},{10,12},{12,10},{14,8},{1,7},{3,5},... | collective-permute-start | bytes 399368 | tf_op jit(solution)/shard_map/ppermute | solution.py:450
  46.6 11.3 %collective-permute-start.14 = (s16[520,128]{1,0:T(8,128)(2,1)S(1)}, s16[520,128]{1,0:T(8,128)(2,1)S(1)}, u32[]{:S(2)}, u32[]{:S(2)}) collective-permute-start(s16[520,128]{1,0:T(8,128)(2,1)S(1)} %get-tuple-element.56), channel_id=1, source_target_pairs={{0,14},{2,12},{4,10},{6,8},{8,6},{10,4},{12,2},{14,0},{1,15},{3,13... | collective-permute-start | bytes 399368 | tf_op jit(solution)/shard_map/ppermute | solution.py:450

commit v9 on v8

--- a/solution.py
+++ b/solution.py
@@ -128,7 +128,7 @@
 TILES = 8
 LINES = 2 * LINES_DEV
 SIDE = LINES_DEV // 2
-EARLY = (6, 2, 4, 5, 1, 0)
+EARLY = (6, 2, 5, 4, 1, 0)
 LATE = (3, 7)
 EARLY_ROWS = 192
 LEAD = (2,)
@@ -184,7 +184,7 @@
     for _, value in pieces:
         top = jnp.max(jnp.abs(value), axis=0, keepdims=True)
         peak = top if peak is None else jnp.maximum(peak, top)
-    code = jnp.ceil(jnp.log2(jnp.maximum(peak, 1e-30) * (1.0 / FULL)) * CODE_STEPS + 0.01)
+    code = jnp.ceil(jnp.log2(jnp.maximum(peak, 1e-33) * (1.0 / FULL)) * CODE_STEPS + 0.01)
     inverse = jnp.exp2(code * (-1.0 / CODE_STEPS))
     for row, value in pieces:
         coded = jnp.round(value * inverse).astype(jnp.int32).astype(jnp.int16)

time: 59.5 us -> 59.6 us (level)
  waiting for transfers between devices: 13.7 us -> 17.6 us
  starting transfers between devices: 33.3 us -> 29.7 us
    ppermute x14, waiting for transfers between devices: 13.7 us -> 17.6 us  [exchange(): lax.ppermute(messages[i], 'az', [(d, d ^ i) for d in range(NDEV)])]
    ppermute x14, starting transfers between devices: 33.2 us -> 29.6 us  [exchange(): lax.ppermute(messages[i], 'az', [(d, d ^ i) for d in range(NDEV)])]
  transfers between devices with their start and end apart: 15 -> 15, of which waited for: 8 -> 7; matrix products, arithmetic and copies ran while one was open for 0% -> 0% of each run, Pallas kernels for 11% -> 11%
where the time goes in v9:
time: 59.6 us; the launch traced here: 59.4 us
  starting transfers between devices  29.7 us (50%)
  waiting for transfers between devices  17.6 us (30%)
  Pallas kernels  10.7 us (18%)
  local copies, waits for them, and re-layouts  1.25 us (2%)
    ppermute x14, starting transfers between devices, exchange(): lax.ppermute(messages[i], 'az', [(d, d ^ i) for d in range(NDEV)])  29.6 us
    ppermute x14, waiting for transfers between devices, exchange(): lax.ppermute(messages[i], 'az', [(d, d ^ i) for d in range(NDEV)])  17.6 us
    pallas_call x2, Pallas kernels, fast_body(): vmem_call(functools.partial(spread_kernel, which), name, [message] * len(...  1.75 us
    pallas_call x1, Pallas kernels, fast_body(): vmem_call(inner_kernel, 'inner', jax.ShapeDtypeStruct((2, 2, TILES, LINES...  1.67 us
    pallas_call x1, Pallas kernels, fast_body(): vmem_call(outer_kernel, 'outer', [message, message, jax.ShapeDtypeStruct(...  1.62 us
    unnamed x8, local copies, waits for them, and re-layouts  1.25 us
    pallas_call x1, Pallas kernels, fast_body(): vmem_call(image_kernel, 'image', jax.ShapeDtypeStruct((LINES, bins), BF16...  1.24 us
  transfers between devices with their start and end apart: 15, of which 7 were waited for; matrix products, arithmetic and copies ran while one was open for 0% of the time, Pallas kernels for 11%

profile of v9, /device:TPU:0, one launch (start us, length us, event | category | flops | bytes accessed | tf_op | source)
XLA Modules:
  0.0 59.4 jit_solution(15799616298286437806)
XLA Ops:
  0.0 0.0 copy-start.3
  0.0 0.0 copy-start.1
  0.0 1.2 %copy-done.1 = bf16[2,32,8,1024]{3,2,1,0:T(8,128)(2,1)S(1)} copy-done((bf16[2,32,8,1024]{3,2,1,0:T(8,128)(2,1)S(1)}, bf16[2,32,8,1024]{3,2,1,0:T(8,128)(2,1)}, u32[]{:S(2)}) %copy-start.1) | copy-done | bytes 1048600
  1.2 0.0 copy-start.2
  1.2 0.6 spread.1
  1.8 5.1 %collective-permute-start = (s16[520,128]{1,0:T(8,128)(2,1)S(1)}, s16[520,128]{1,0:T(8,128)(2,1)S(1)}, u32[]{:S(2)}, u32[]{:S(2)}) collective-permute-start(s16[520,128]{1,0:T(8,128)(2,1)S(1)} %spread.1), channel_id=1, source_target_pairs={{0,12},{2,14},{4,8},{6,10},{8,4},{10,6},{12,0},{14,2},{1,13},{3,15... | collective-permute-start | bytes 399368 | tf_op jit(solution)/shard_map/ppermute | solution.py:450
  6.9 1.2 %spread_rest.1 = (s16[520,128]{1,0:T(8,128)(2,1)S(1)}, s16[520,128]{1,0:T(8,128)(2,1)S(1)}, s16[520,128]{1,0:T(8,128)(2,1)S(1)}, s16[520,128]{1,0:T(8,128)(2,1)S...) custom-call(s32[1]{0:T(128)} %bitcast.me_ref, ...), custom_call_target="tpu_custom_call" | custom-call | tf_op jit(solution)/shard_map/spread_rest/pallas_call | solution.py:468
  8.1 0.4 collective-permute-start.2
  8.6 3.5 %collective-permute-start.3 = (s16[520,128]{1,0:T(8,128)(2,1)S(1)}, s16[520,128]{1,0:T(8,128)(2,1)S(1)}, u32[]{:S(2)}, u32[]{:S(2)}) collective-permute-start(s16[520,128]{1,0:T(8,128)(2,1)S(1)} %get-tuple-element.40), channel_id=1, source_target_pairs={{0,8},{2,10},{4,12},{6,14},{8,0},{10,2},{12,4},{14,6},{1,9},{3,11}... | collective-permute-start | bytes 399368 | tf_op jit(solution)/shard_map/ppermute | solution.py:450
  12.1 0.5 collective-permute-start.4
  12.6 0.0 collective-permute-start.1
  12.6 0.0 collective-permute-done.refs_0_
  12.6 8.1 %collective-permute-start.5 = (s16[520,128]{1,0:T(8,128)(2,1)S(1)}, s16[520,128]{1,0:T(8,128)(2,1)S(1)}, u32[]{:S(2)}, u32[]{:S(2)}) collective-permute-start(s16[520,128]{1,0:T(8,128)(2,1)S(1)} %get-tuple-element.43), channel_id=1, source_target_pairs={{0,6},{2,4},{4,2},{6,0},{8,14},{10,12},{12,10},{14,8},{1,7},{3,5},... | collective-permute-start | bytes 399368 | tf_op jit(solution)/shard_map/ppermute | solution.py:450
  20.6 2.4 %collective-permute-done.2.refs_2_ = s16[520,128]{1,0:T(8,128)(2,1)S(1)} collective-permute-done((s16[520,128]{1,0:T(8,128)(2,1)S(1)}, s16[520,128]{1,0:T(8,128)(2,1)S(1)}, u32[]{:S(2)}, u32[]{:S(2)}) %collective-permute-start.2) | collective-permute-done | bytes 133152 | tf_op jit(solution)/shard_map/ppermute | solution.py:450
  23.0 2.2 %collective-permute-start.6 = (s16[520,128]{1,0:T(8,128)(2,1)S(1)}, s16[520,128]{1,0:T(8,128)(2,1)S(1)}, u32[]{:S(2)}, u32[]{:S(2)}) collective-permute-start(s16[520,128]{1,0:T(8,128)(2,1)S(1)} %get-tuple-element.44), channel_id=1, source_target_pairs={{0,14},{2,12},{4,10},{6,8},{8,6},{10,4},{12,2},{14,0},{1,15},{3,13... | collective-permute-start | bytes 399368 | tf_op jit(solution)/shard_map/ppermute | solution.py:450
  25.3 0.0 copy-done.3
  25.3 0.0 copy-done.2
  25.3 0.7 %tables.1 = (bf16[2,2,256,192]{3,2,1,0:T(8,128)(2,1)S(1)}, bf16[2,256,192]{2,1,0:T(8,128)(2,1)S(1)}, bf16[2,2,256,256]{3,2,1,0:T(8,128)(2,1)S(1)}, bf16[2,256,19...) custom-call(s32[1]{0:T(128)} %bitcast.me_ref, s32[4,16]{1,0:T(4,128)S(1)} %copy-done.3, ...), custom_call_target="tpu_custom_call" | custom-call | tf_op jit(solution)/shard_map/tables/pallas_call | solution.py:474
  26.0 0.0 collective-permute-done.3.refs_3_
  26.0 0.0 collective-permute-done.4.refs_4_
  26.0 0.0 collective-permute-done.1.refs_1_
  26.0 1.1 %forward_early.1.sum_ref = f32[2,256,1024]{2,1,0:T(8,128)S(1)} custom-call(s32[1]{0:T(128)} %bitcast.me_ref, bf16[2,2,256,192]{3,2,1,0:T(8,128)(2,1)S(1)} %get-tuple-element.38.table_ref, s16[520,128]{1,0:T(8,128)(2,1)S(1)} %collective-permute-done.refs_0_, s16[520,128]{1,0:T(8,128)(2,1)S(1)} %collective-permute-done.1.refs_1_, ...), custom_call_target="tpu_custom_call" | custom-call | tf_op jit(solution)/shard_map/forward_early/pallas_call | solution.py:489
  27.1 0.0 copy-start
  27.1 1.7 %collective-permute-done.5.refs_0_ = s16[520,128]{1,0:T(8,128)(2,1)S(1)} collective-permute-done((s16[520,128]{1,0:T(8,128)(2,1)S(1)}, s16[520,128]{1,0:T(8,128)(2,1)S(1)}, u32[]{:S(2)}, u32[]{:S(2)}) %collective-permute-start.5) | collective-permute-done | bytes 133152 | tf_op jit(solution)/shard_map/ppermute | solution.py:450
  28.8 1.9 %collective-permute-done.6.refs_1_ = s16[520,128]{1,0:T(8,128)(2,1)S(1)} collective-permute-done((s16[520,128]{1,0:T(8,128)(2,1)S(1)}, s16[520,128]{1,0:T(8,128)(2,1)S(1)}, u32[]{:S(2)}, u32[]{:S(2)}) %collective-permute-start.6) | collective-permute-done | bytes 133152 | tf_op jit(solution)/shard_map/ppermute | solution.py:450
  30.7 0.5 forward.1
  31.2 0.1 collective-permute-start.7
  31.3 0.0 copy-done
  31.3 1.7 %inner.1.focus_ref = bf16[2,2,8,256,128]{4,3,2,1,0:T(8,128)(2,1)S(1)} custom-call(s32[1]{0:T(128)} %bitcast.2.rg_ref, s32[4,16]{1,0:T(4,128)S(1)} %get-tuple-element.36.starts_ref, bf16[8,2,512,128]{3,2,1,0:T(8,128)(2,1)S(1)} %get-tuple-element.45.spectrum_ref, bf16[4,8,256,128]{3,2,1,0:T(8,128)(2,1)S(1)} %copy-done), custom_call_target="tpu_custom_call" | custom-call | tf_op jit(solution)/shard_map/inner/pallas_call | solution.py:504
  33.0 0.0 collective-permute-done.7.halo_ref
  33.0 1.6 %outer.1 = (s16[520,128]{1,0:T(8,128)(2,1)S(1)}, s16[520,128]{1,0:T(8,128)(2,1)S(1)}, bf16[2,2,256,128]{3,2,1,0:T(8,128)(2,1)S(1)}) custom-call(s32[1]{0:T(128)} %bitcast.me_ref, s32[1]{0:T(128)} %bitcast.2.rg_ref, s32[4,16]{1,0:T(4,128)S(1)} %get-tuple-element.36.starts_ref, bf16[8,2,512,128]{3,2,1,0:T(8,128)(2,1)S(1)} %get-tuple-element.45.spectrum_ref, ...), custom_call_target="tpu_custom_call" | custom-call | tf_op jit(solution)/shard_map/outer/pallas_call | solution.py:512
  34.7 2.4 %collective-permute-start.8 = (s16[520,128]{1,0:T(8,128)(2,1)S(1)}, s16[520,128]{1,0:T(8,128)(2,1)S(1)}, u32[]{:S(2)}, u32[]{:S(2)}) collective-permute-start(s16[520,128]{1,0:T(8,128)(2,1)S(1)} %get-tuple-element.48), channel_id=1, source_target_pairs={{0,12},{2,14},{4,8},{6,10},{8,4},{10,6},{12,0},{14,2},{1,13},{3,15... | collective-permute-start | bytes 399368 | tf_op jit(solution)/shard_map/ppermute | solution.py:450
  37.0 0.0 collective-permute-start.9
  37.0 1.1 %rest.1 = (s16[520,128]{1,0:T(8,128)(2,1)S(1)}, s16[520,128]{1,0:T(8,128)(2,1)S(1)}, s16[520,128]{1,0:T(8,128)(2,1)S(1)}, s16[520,128]{1,0:T(8,128)(2,1)S(1)}, s...) custom-call(s32[1]{0:T(128)} %bitcast.me_ref, s32[1]{0:T(128)} %bitcast.2.rg_ref, ...), custom_call_target="tpu_custom_call" | custom-call | tf_op jit(solution)/shard_map/rest/pallas_call | solution.py:520
  38.2 2.1 %collective-permute-start.10 = (s16[520,128]{1,0:T(8,128)(2,1)S(1)}, s16[520,128]{1,0:T(8,128)(2,1)S(1)}, u32[]{:S(2)}, u32[]{:S(2)}) collective-permute-start(s16[520,128]{1,0:T(8,128)(2,1)S(1)} %get-tuple-element.51), channel_id=1, source_target_pairs={{0,10},{2,8},{4,14},{6,12},{8,2},{10,0},{12,6},{14,4},{1,11},{3,9}... | collective-permute-start | bytes 399368 | tf_op jit(solution)/shard_map/ppermute | solution.py:450
  40.2 0.9 %collective-permute-start.11 = (s16[520,128]{1,0:T(8,128)(2,1)S(1)}, s16[520,128]{1,0:T(8,128)(2,1)S(1)}, u32[]{:S(2)}, u32[]{:S(2)}) collective-permute-start(s16[520,128]{1,0:T(8,128)(2,1)S(1)} %get-tuple-element.52), channel_id=1, source_target_pairs={{0,8},{2,10},{4,12},{6,14},{8,0},{10,2},{12,4},{14,6},{1,9},{3,11}... | collective-permute-start | bytes 399368 | tf_op jit(solution)/shard_map/ppermute | solution.py:450
  41.1 1.5 %collective-permute-start.12 = (s16[520,128]{1,0:T(8,128)(2,1)S(1)}, s16[520,128]{1,0:T(8,128)(2,1)S(1)}, u32[]{:S(2)}, u32[]{:S(2)}) collective-permute-start(s16[520,128]{1,0:T(8,128)(2,1)S(1)} %get-tuple-element.53), channel_id=1, source_target_pairs={{0,2},{2,0},{4,6},{6,4},{8,10},{10,8},{12,14},{14,12},{1,3},{3,1},... | collective-permute-start | bytes 399368 | tf_op jit(solution)/shard_map/ppermute | solution.py:450
  42.6 0.3 collective-permute-done.8.refs_0_
  42.9 1.7 %collective-permute-start.13 = (s16[520,128]{1,0:T(8,128)(2,1)S(1)}, s16[520,128]{1,0:T(8,128)(2,1)S(1)}, u32[]{:S(2)}, u32[]{:S(2)}) collective-permute-start(s16[520,128]{1,0:T(8,128)(2,1)S(1)} %get-tuple-element.55), channel_id=1, source_target_pairs={{0,6},{2,4},{4,2},{6,0},{8,14},{10,12},{12,10},{14,8},{1,7},{3,5},... | collective-permute-start | bytes 399368 | tf_op jit(solution)/shard_map/ppermute | solution.py:450
  44.6 3.6 %collective-permute-done.9.refs_1_ = s16[520,128]{1,0:T(8,128)(2,1)S(1)} collective-permute-done((s16[520,128]{1,0:T(8,128)(2,1)S(1)}, s16[520,128]{1,0:T(8,128)(2,1)S(1)}, u32[]{:S(2)}, u32[]{:S(2)}) %collective-permute-start.9) | collective-permute-done | bytes 133152 | tf_op jit(solution)/shard_map/ppermute | solution.py:450
  48.3 1.2 %collective-permute-start.14 = (s16[520,128]{1,0:T(8,128)(2,1)S(1)}, s16[520,128]{1,0:T(8,128)(2,1)S(1)}, u32[]{:S(2)}, u32[]{:S(2)}) collective-permute-start(s16[520,128]{1,0:T(8,128)(2,1)S(1)} %get-tuple-element.56), channel_id=1, source_target_pairs={{0,14},{2,12},{4,10},{6,8},{8,6},{10,4},{12,2},{14,0},{1,15},{3,13... | collective-permute-start | bytes 399368 | tf_op jit(solution)/shard_map/ppermute | solution.py:450
  49.4 2.8 %collective-permute-done.10.refs_2_ = s16[520,128]{1,0:T(8,128)(2,1)S(1)} collective-permute-done((s16[520,128]{1,0:T(8,128)(2,1)S(1)}, s16[520,128]{1,0:T(8,128)(2,1)S(1)}, u32[]{:S(2)}, u32[]{:S(2)}) %collective-permute-start.10) | collective-permute-done | bytes 133152 | tf_op jit(solution)/shard_map/ppermute | solution.py:450
  52.2 4.8 %collective-permute-done.11.refs_3_ = s16[520,128]{1,0:T(8,128)(2,1)S(1)} collective-permute-done((s16[520,128]{1,0:T(8,128)(2,1)S(1)}, s16[520,128]{1,0:T(8,128)(2,1)S(1)}, u32[]{:S(2)}, u32[]{:S(2)}) %collective-permute-start.11) | collective-permute-done | bytes 133152 | tf_op jit(solution)/shard_map/ppermute | solution.py:450
  57.0 0.0 collective-permute-done.12.refs_4_
  57.0 1.0 %image_early.1.sum_ref = f32[2,256,1024]{2,1,0:T(8,128)S(1)} custom-call(bf16[2,256,192]{2,1,0:T(8,128)(2,1)S(1)} %get-tuple-element.35.table_ref, s16[520,128]{1,0:T(8,128)(2,1)S(1)} %collective-permute-done.8.refs_0_, s16[520,128]{1,0:T(8,128)(2,1)S(1)} %collective-permute-done.9.refs_1_, s16[520,128]{1,0:T(8,128)(2,1)S(1)} %collective-permute-done.10.refs_2_, ...), custom_call_target="tpu_custom_call" | custom-call | tf_op jit(solution)/shard_map/image_early/pallas_call | solution.py:524
  58.1 0.0 collective-permute-done.13.refs_0_
  58.1 0.0 collective-permute-done.14.refs_1_
  58.1 1.2 %image.1 = bf16[512,1024]{1,0:T(8,128)(2,1)} custom-call(bf16[256,192]{1,0:T(8,128)(2,1)S(1)} %get-tuple-element.34.table_ref, f32[2,256,1024]{2,1,0:T(8,128)S(1)} %image_early.1.sum_ref, s16[520,128]{1,0:T(8,128)(2,1)S(1)} %collective-permute-done.13.refs_0_, s16[520,128]{1,0:T(8,128)(2,1)S(1)} %collective-permute-done.14.refs_1_), custom_call_target="tpu_custom_call" | custom-call | tf_op jit(solution)/shard_map/image/pallas_call | solution.py:527
Async XLA Ops:
  0.0 25.3 %copy-start.3 = (s32[4,16]{1,0:T(4,128)S(1)}, s32[4,16]{1,0:T(4,128)}, u32[]{:S(2)}) copy-start(s32[4,16]{1,0:T(4,128)} %band_ref.1) | copy-start | bytes 772
  0.0 1.2 %copy-start.1 = (bf16[2,32,8,1024]{3,2,1,0:T(8,128)(2,1)S(1)}, bf16[2,32,8,1024]{3,2,1,0:T(8,128)(2,1)}, u32[]{:S(2)}) copy-start(bf16[2,32,8,1024]{3,2,1,0:T(8,128)(2,1)} %param.4) | copy-start | bytes 3145732
  1.2 24.0 %copy-start.2 = (f32[2,128,256]{2,1,0:T(8,128)S(1)}, f32[2,128,256]{2,1,0:T(8,128)}, u32[]{:S(2)}) copy-start(f32[2,128,256]{2,1,0:T(8,128)} %constant.10.clone.base_ref) | copy-start | bytes 786436
  1.8 10.8 %collective-permute-start = (s16[520,128]{1,0:T(8,128)(2,1)S(1)}, s16[520,128]{1,0:T(8,128)(2,1)S(1)}, u32[]{:S(2)}, u32[]{:S(2)}) collective-permute-start(s16[520,128]{1,0:T(8,128)(2,1)S(1)} %spread.1), channel_id=1, source_target_pairs={{0,12},{2,14},{4,8},{6,10},{8,4},{10,6},{12,0},{14,2},{1,13},{3,15... | collective-permute-start | bytes 399368 | tf_op jit(solution)/shard_map/ppermute | solution.py:450
  8.1 14.9 %collective-permute-start.2 = (s16[520,128]{1,0:T(8,128)(2,1)S(1)}, s16[520,128]{1,0:T(8,128)(2,1)S(1)}, u32[]{:S(2)}, u32[]{:S(2)}) collective-permute-start(s16[520,128]{1,0:T(8,128)(2,1)S(1)} %get-tuple-element.39), channel_id=1, source_target_pairs={{0,10},{2,8},{4,14},{6,12},{8,2},{10,0},{12,6},{14,4},{1,11},{3,9}... | collective-permute-start | bytes 399368 | tf_op jit(solution)/shard_map/ppermute | solution.py:450
  8.6 17.4 %collective-permute-start.3 = (s16[520,128]{1,0:T(8,128)(2,1)S(1)}, s16[520,128]{1,0:T(8,128)(2,1)S(1)}, u32[]{:S(2)}, u32[]{:S(2)}) collective-permute-start(s16[520,128]{1,0:T(8,128)(2,1)S(1)} %get-tuple-element.40), channel_id=1, source_target_pairs={{0,8},{2,10},{4,12},{6,14},{8,0},{10,2},{12,4},{14,6},{1,9},{3,11}... | collective-permute-start | bytes 399368 | tf_op jit(solution)/shard_map/ppermute | solution.py:450
  12.1 14.0 %collective-permute-start.4 = (s16[520,128]{1,0:T(8,128)(2,1)S(1)}, s16[520,128]{1,0:T(8,128)(2,1)S(1)}, u32[]{:S(2)}, u32[]{:S(2)}) collective-permute-start(s16[520,128]{1,0:T(8,128)(2,1)S(1)} %get-tuple-element.41), channel_id=1, source_target_pairs={{0,2},{2,0},{4,6},{6,4},{8,10},{10,8},{12,14},{14,12},{1,3},{3,1},... | collective-permute-start | bytes 399368 | tf_op jit(solution)/shard_map/ppermute | solution.py:450
  12.6 13.4 %collective-permute-start.1 = (s16[520,128]{1,0:T(8,128)(2,1)S(1)}, s16[520,128]{1,0:T(8,128)(2,1)S(1)}, u32[]{:S(2)}, u32[]{:S(2)}) collective-permute-start(s16[520,128]{1,0:T(8,128)(2,1)S(1)} %get-tuple-element.32), channel_id=1, source_target_pairs={{0,4},{2,6},{4,0},{6,2},{8,12},{10,14},{12,8},{14,10},{1,5},{3,7},... | collective-permute-start | bytes 399368 | tf_op jit(solution)/shard_map/ppermute | solution.py:450
  12.6 16.2 %collective-permute-start.5 = (s16[520,128]{1,0:T(8,128)(2,1)S(1)}, s16[520,128]{1,0:T(8,128)(2,1)S(1)}, u32[]{:S(2)}, u32[]{:S(2)}) collective-permute-start(s16[520,128]{1,0:T(8,128)(2,1)S(1)} %get-tuple-element.43), channel_id=1, source_target_pairs={{0,6},{2,4},{4,2},{6,0},{8,14},{10,12},{12,10},{14,8},{1,7},{3,5},... | collective-permute-start | bytes 399368 | tf_op jit(solution)/shard_map/ppermute | solution.py:450
  23.0 7.7 %collective-permute-start.6 = (s16[520,128]{1,0:T(8,128)(2,1)S(1)}, s16[520,128]{1,0:T(8,128)(2,1)S(1)}, u32[]{:S(2)}, u32[]{:S(2)}) collective-permute-start(s16[520,128]{1,0:T(8,128)(2,1)S(1)} %get-tuple-element.44), channel_id=1, source_target_pairs={{0,14},{2,12},{4,10},{6,8},{8,6},{10,4},{12,2},{14,0},{1,15},{3,13... | collective-permute-start | bytes 399368 | tf_op jit(solution)/shard_map/ppermute | solution.py:450
  27.1 4.2 %copy-start = (bf16[4,8,256,128]{3,2,1,0:T(8,128)(2,1)S(1)}, bf16[4,8,256,128]{3,2,1,0:T(8,128)(2,1)}, u32[]{:S(2)}) copy-start(bf16[4,8,256,128]{3,2,1,0:T(8,128)(2,1)} %weights_ref.3) | copy-start | bytes 6291460
  31.2 1.8 %collective-permute-start.7 = (bf16[2,512,128]{2,1,0:T(8,128)(2,1)S(1)}, bf16[2,512,128]{2,1,0:T(8,128)(2,1)S(1)}, u32[]{:S(2)}, u32[]{:S(2)}) collective-permute-start(bf16[2,512,128]{2,1,0:T(8,128)(2,1)S(1)} %get-tuple-element.46), channel_id=1, source_target_pairs={{0,1},{1,0},{2,3},{3,2},{4,5},{5,4},{6,7},{7,6},{8,9},{9,8},{10,11... | collective-permute-start | bytes 786440 | tf_op jit(solution)/shard_map/ppermute | solution.py:503
  34.7 8.3 %collective-permute-start.8 = (s16[520,128]{1,0:T(8,128)(2,1)S(1)}, s16[520,128]{1,0:T(8,128)(2,1)S(1)}, u32[]{:S(2)}, u32[]{:S(2)}) collective-permute-start(s16[520,128]{1,0:T(8,128)(2,1)S(1)} %get-tuple-element.48), channel_id=1, source_target_pairs={{0,12},{2,14},{4,8},{6,10},{8,4},{10,6},{12,0},{14,2},{1,13},{3,15... | collective-permute-start | bytes 399368 | tf_op jit(solution)/shard_map/ppermute | solution.py:450
  37.0 11.2 %collective-permute-start.9 = (s16[520,128]{1,0:T(8,128)(2,1)S(1)}, s16[520,128]{1,0:T(8,128)(2,1)S(1)}, u32[]{:S(2)}, u32[]{:S(2)}) collective-permute-start(s16[520,128]{1,0:T(8,128)(2,1)S(1)} %get-tuple-element.49), channel_id=1, source_target_pairs={{0,4},{2,6},{4,0},{6,2},{8,12},{10,14},{12,8},{14,10},{1,5},{3,7},... | collective-permute-start | bytes 399368 | tf_op jit(solution)/shard_map/ppermute | solution.py:450
  38.2 14.0 %collective-permute-start.10 = (s16[520,128]{1,0:T(8,128)(2,1)S(1)}, s16[520,128]{1,0:T(8,128)(2,1)S(1)}, u32[]{:S(2)}, u32[]{:S(2)}) collective-permute-start(s16[520,128]{1,0:T(8,128)(2,1)S(1)} %get-tuple-element.51), channel_id=1, source_target_pairs={{0,10},{2,8},{4,14},{6,12},{8,2},{10,0},{12,6},{14,4},{1,11},{3,9}... | collective-permute-start | bytes 399368 | tf_op jit(solution)/shard_map/ppermute | solution.py:450
  40.2 16.8 %collective-permute-start.11 = (s16[520,128]{1,0:T(8,128)(2,1)S(1)}, s16[520,128]{1,0:T(8,128)(2,1)S(1)}, u32[]{:S(2)}, u32[]{:S(2)}) collective-permute-start(s16[520,128]{1,0:T(8,128)(2,1)S(1)} %get-tuple-element.52), channel_id=1, source_target_pairs={{0,8},{2,10},{4,12},{6,14},{8,0},{10,2},{12,4},{14,6},{1,9},{3,11}... | collective-permute-start | bytes 399368 | tf_op jit(solution)/shard_map/ppermute | solution.py:450
  41.1 15.9 %collective-permute-start.12 = (s16[520,128]{1,0:T(8,128)(2,1)S(1)}, s16[520,128]{1,0:T(8,128)(2,1)S(1)}, u32[]{:S(2)}, u32[]{:S(2)}) collective-permute-start(s16[520,128]{1,0:T(8,128)(2,1)S(1)} %get-tuple-element.53), channel_id=1, source_target_pairs={{0,2},{2,0},{4,6},{6,4},{8,10},{10,8},{12,14},{14,12},{1,3},{3,1},... | collective-permute-start | bytes 399368 | tf_op jit(solution)/shard_map/ppermute | solution.py:450
  42.9 15.2 %collective-permute-start.13 = (s16[520,128]{1,0:T(8,128)(2,1)S(1)}, s16[520,128]{1,0:T(8,128)(2,1)S(1)}, u32[]{:S(2)}, u32[]{:S(2)}) collective-permute-start(s16[520,128]{1,0:T(8,128)(2,1)S(1)} %get-tuple-element.55), channel_id=1, source_target_pairs={{0,6},{2,4},{4,2},{6,0},{8,14},{10,12},{12,10},{14,8},{1,7},{3,5},... | collective-permute-start | bytes 399368 | tf_op jit(solution)/shard_map/ppermute | solution.py:450
  48.3 9.8 %collective-permute-start.14 = (s16[520,128]{1,0:T(8,128)(2,1)S(1)}, s16[520,128]{1,0:T(8,128)(2,1)S(1)}, u32[]{:S(2)}, u32[]{:S(2)}) collective-permute-start(s16[520,128]{1,0:T(8,128)(2,1)S(1)} %get-tuple-element.56), channel_id=1, source_target_pairs={{0,14},{2,12},{4,10},{6,8},{8,6},{10,4},{12,2},{14,0},{1,15},{3,13... | collective-permute-start | bytes 399368 | tf_op jit(solution)/shard_map/ppermute | solution.py:450

commit v10 on v9

--- a/solution.py
+++ b/solution.py
@@ -133,7 +133,7 @@
 EARLY_ROWS = 192
 LEAD = (2,)
 SPREAD_LEAD = (6, )
-SPREAD_REST = (2, 4, 5, 1, 3, 7, 0, )
+SPREAD_REST = (2, 5, 4, 1, 3, 7, 0)
 REST = (0, 1, 3)
 VMEM_LIMIT = 20 * 1024 * 1024
 

time: 59.6 us -> 59.6 us (level)
  no operation moved by 1% of the time
where the time goes in v10:
time: 59.6 us; the launch traced here: 59.4 us
  starting transfers between devices  29.7 us (50%)
  waiting for transfers between devices  17.6 us (30%)
  Pallas kernels  10.7 us (18%)
  local copies, waits for them, and re-layouts  1.25 us (2%)
    ppermute x14, starting transfers between devices, exchange(): lax.ppermute(messages[i], 'az', [(d, d ^ i) for d in range(NDEV)])  29.6 us
    ppermute x14, waiting for transfers between devices, exchange(): lax.ppermute(messages[i], 'az', [(d, d ^ i) for d in range(NDEV)])  17.6 us
    pallas_call x2, Pallas kernels, fast_body(): vmem_call(functools.partial(spread_kernel, which), name, [message] * len(...  1.75 us
    pallas_call x1, Pallas kernels, fast_body(): vmem_call(inner_kernel, 'inner', jax.ShapeDtypeStruct((2, 2, TILES, LINES...  1.67 us
    pallas_call x1, Pallas kernels, fast_body(): vmem_call(outer_kernel, 'outer', [message, message, jax.ShapeDtypeStruct(...  1.62 us
    unnamed x8, local copies, waits for them, and re-layouts  1.25 us
    pallas_call x1, Pallas kernels, fast_body(): vmem_call(image_kernel, 'image', jax.ShapeDtypeStruct((LINES, bins), BF16...  1.24 us
  transfers between devices with their start and end apart: 15, of which 7 were waited for; matrix products, arithmetic and copies ran while one was open for 0% of the time, Pallas kernels for 11%

profile of v10, /device:TPU:0, one launch (start us, length us, event | category | flops | bytes accessed | tf_op | source)
XLA Modules:
  0.0 59.4 jit_solution(1781401002947200538)
XLA Ops:
  0.0 0.0 copy-start.3
  0.0 0.0 copy-start.1
  0.0 1.2 %copy-done.1 = bf16[2,32,8,1024]{3,2,1,0:T(8,128)(2,1)S(1)} copy-done((bf16[2,32,8,1024]{3,2,1,0:T(8,128)(2,1)S(1)}, bf16[2,32,8,1024]{3,2,1,0:T(8,128)(2,1)}, u32[]{:S(2)}) %copy-start.1) | copy-done | bytes 1048600
  1.2 0.0 copy-start.2
  1.2 0.6 spread.1
  1.8 5.1 %collective-permute-start = (s16[520,128]{1,0:T(8,128)(2,1)S(1)}, s16[520,128]{1,0:T(8,128)(2,1)S(1)}, u32[]{:S(2)}, u32[]{:S(2)}) collective-permute-start(s16[520,128]{1,0:T(8,128)(2,1)S(1)} %spread.1), channel_id=1, source_target_pairs={{0,12},{2,14},{4,8},{6,10},{8,4},{10,6},{12,0},{14,2},{1,13},{3,15... | collective-permute-start | bytes 399368 | tf_op jit(solution)/shard_map/ppermute | solution.py:450
  6.9 1.2 %spread_rest.1 = (s16[520,128]{1,0:T(8,128)(2,1)S(1)}, s16[520,128]{1,0:T(8,128)(2,1)S(1)}, s16[520,128]{1,0:T(8,128)(2,1)S(1)}, s16[520,128]{1,0:T(8,128)(2,1)S...) custom-call(s32[1]{0:T(128)} %bitcast.me_ref, ...), custom_call_target="tpu_custom_call" | custom-call | tf_op jit(solution)/shard_map/spread_rest/pallas_call | solution.py:468
  8.1 0.4 collective-permute-start.2
  8.6 3.5 %collective-permute-start.3 = (s16[520,128]{1,0:T(8,128)(2,1)S(1)}, s16[520,128]{1,0:T(8,128)(2,1)S(1)}, u32[]{:S(2)}, u32[]{:S(2)}) collective-permute-start(s16[520,128]{1,0:T(8,128)(2,1)S(1)} %get-tuple-element.40), channel_id=1, source_target_pairs={{0,8},{2,10},{4,12},{6,14},{8,0},{10,2},{12,4},{14,6},{1,9},{3,11}... | collective-permute-start | bytes 399368 | tf_op jit(solution)/shard_map/ppermute | solution.py:450
  12.1 0.5 collective-permute-start.4
  12.6 0.0 collective-permute-start.1
  12.6 0.0 collective-permute-done.refs_0_
  12.6 8.1 %collective-permute-start.5 = (s16[520,128]{1,0:T(8,128)(2,1)S(1)}, s16[520,128]{1,0:T(8,128)(2,1)S(1)}, u32[]{:S(2)}, u32[]{:S(2)}) collective-permute-start(s16[520,128]{1,0:T(8,128)(2,1)S(1)} %get-tuple-element.43), channel_id=1, source_target_pairs={{0,6},{2,4},{4,2},{6,0},{8,14},{10,12},{12,10},{14,8},{1,7},{3,5},... | collective-permute-start | bytes 399368 | tf_op jit(solution)/shard_map/ppermute | solution.py:450
  20.6 2.4 %collective-permute-done.2.refs_2_ = s16[520,128]{1,0:T(8,128)(2,1)S(1)} collective-permute-done((s16[520,128]{1,0:T(8,128)(2,1)S(1)}, s16[520,128]{1,0:T(8,128)(2,1)S(1)}, u32[]{:S(2)}, u32[]{:S(2)}) %collective-permute-start.2) | collective-permute-done | bytes 133152 | tf_op jit(solution)/shard_map/ppermute | solution.py:450
  23.0 2.2 %collective-permute-start.6 = (s16[520,128]{1,0:T(8,128)(2,1)S(1)}, s16[520,128]{1,0:T(8,128)(2,1)S(1)}, u32[]{:S(2)}, u32[]{:S(2)}) collective-permute-start(s16[520,128]{1,0:T(8,128)(2,1)S(1)} %get-tuple-element.44), channel_id=1, source_target_pairs={{0,14},{2,12},{4,10},{6,8},{8,6},{10,4},{12,2},{14,0},{1,15},{3,13... | collective-permute-start | bytes 399368 | tf_op jit(solution)/shard_map/ppermute | solution.py:450
  25.3 0.0 copy-done.3
  25.3 0.0 copy-done.2
  25.3 0.7 %tables.1 = (bf16[2,2,256,192]{3,2,1,0:T(8,128)(2,1)S(1)}, bf16[2,256,192]{2,1,0:T(8,128)(2,1)S(1)}, bf16[2,2,256,256]{3,2,1,0:T(8,128)(2,1)S(1)}, bf16[2,256,19...) custom-call(s32[1]{0:T(128)} %bitcast.me_ref, s32[4,16]{1,0:T(4,128)S(1)} %copy-done.3, ...), custom_call_target="tpu_custom_call" | custom-call | tf_op jit(solution)/shard_map/tables/pallas_call | solution.py:474
  26.0 0.0 collective-permute-done.3.refs_3_
  26.0 0.0 collective-permute-done.4.refs_4_
  26.0 0.0 collective-permute-done.1.refs_1_
  26.0 1.1 %forward_early.1.sum_ref = f32[2,256,1024]{2,1,0:T(8,128)S(1)} custom-call(s32[1]{0:T(128)} %bitcast.me_ref, bf16[2,2,256,192]{3,2,1,0:T(8,128)(2,1)S(1)} %get-tuple-element.38.table_ref, s16[520,128]{1,0:T(8,128)(2,1)S(1)} %collective-permute-done.refs_0_, s16[520,128]{1,0:T(8,128)(2,1)S(1)} %collective-permute-done.1.refs_1_, ...), custom_call_target="tpu_custom_call" | custom-call | tf_op jit(solution)/shard_map/forward_early/pallas_call | solution.py:489
  27.1 0.0 copy-start
  27.1 1.7 %collective-permute-done.5.refs_0_ = s16[520,128]{1,0:T(8,128)(2,1)S(1)} collective-permute-done((s16[520,128]{1,0:T(8,128)(2,1)S(1)}, s16[520,128]{1,0:T(8,128)(2,1)S(1)}, u32[]{:S(2)}, u32[]{:S(2)}) %collective-permute-start.5) | collective-permute-done | bytes 133152 | tf_op jit(solution)/shard_map/ppermute | solution.py:450
  28.8 1.9 %collective-permute-done.6.refs_1_ = s16[520,128]{1,0:T(8,128)(2,1)S(1)} collective-permute-done((s16[520,128]{1,0:T(8,128)(2,1)S(1)}, s16[520,128]{1,0:T(8,128)(2,1)S(1)}, u32[]{:S(2)}, u32[]{:S(2)}) %collective-permute-start.6) | collective-permute-done | bytes 133152 | tf_op jit(solution)/shard_map/ppermute | solution.py:450
  30.7 0.5 forward.1
  31.2 0.1 collective-permute-start.7
  31.3 0.0 copy-done
  31.3 1.7 %inner.1.focus_ref = bf16[2,2,8,256,128]{4,3,2,1,0:T(8,128)(2,1)S(1)} custom-call(s32[1]{0:T(128)} %bitcast.2.rg_ref, s32[4,16]{1,0:T(4,128)S(1)} %get-tuple-element.36.starts_ref, bf16[8,2,512,128]{3,2,1,0:T(8,128)(2,1)S(1)} %get-tuple-element.45.spectrum_ref, bf16[4,8,256,128]{3,2,1,0:T(8,128)(2,1)S(1)} %copy-done), custom_call_target="tpu_custom_call" | custom-call | tf_op jit(solution)/shard_map/inner/pallas_call | solution.py:504
  33.0 0.0 collective-permute-done.7.halo_ref
  33.0 1.6 %outer.1 = (s16[520,128]{1,0:T(8,128)(2,1)S(1)}, s16[520,128]{1,0:T(8,128)(2,1)S(1)}, bf16[2,2,256,128]{3,2,1,0:T(8,128)(2,1)S(1)}) custom-call(s32[1]{0:T(128)} %bitcast.me_ref, s32[1]{0:T(128)} %bitcast.2.rg_ref, s32[4,16]{1,0:T(4,128)S(1)} %get-tuple-element.36.starts_ref, bf16[8,2,512,128]{3,2,1,0:T(8,128)(2,1)S(1)} %get-tuple-element.45.spectrum_ref, ...), custom_call_target="tpu_custom_call" | custom-call | tf_op jit(solution)/shard_map/outer/pallas_call | solution.py:512
  34.7 2.4 %collective-permute-start.8 = (s16[520,128]{1,0:T(8,128)(2,1)S(1)}, s16[520,128]{1,0:T(8,128)(2,1)S(1)}, u32[]{:S(2)}, u32[]{:S(2)}) collective-permute-start(s16[520,128]{1,0:T(8,128)(2,1)S(1)} %get-tuple-element.48), channel_id=1, source_target_pairs={{0,12},{2,14},{4,8},{6,10},{8,4},{10,6},{12,0},{14,2},{1,13},{3,15... | collective-permute-start | bytes 399368 | tf_op jit(solution)/shard_map/ppermute | solution.py:450
  37.0 0.0 collective-permute-start.9
  37.0 1.1 %rest.1 = (s16[520,128]{1,0:T(8,128)(2,1)S(1)}, s16[520,128]{1,0:T(8,128)(2,1)S(1)}, s16[520,128]{1,0:T(8,128)(2,1)S(1)}, s16[520,128]{1,0:T(8,128)(2,1)S(1)}, s...) custom-call(s32[1]{0:T(128)} %bitcast.me_ref, s32[1]{0:T(128)} %bitcast.2.rg_ref, ...), custom_call_target="tpu_custom_call" | custom-call | tf_op jit(solution)/shard_map/rest/pallas_call | solution.py:520
  38.2 2.1 %collective-permute-start.10 = (s16[520,128]{1,0:T(8,128)(2,1)S(1)}, s16[520,128]{1,0:T(8,128)(2,1)S(1)}, u32[]{:S(2)}, u32[]{:S(2)}) collective-permute-start(s16[520,128]{1,0:T(8,128)(2,1)S(1)} %get-tuple-element.51), channel_id=1, source_target_pairs={{0,10},{2,8},{4,14},{6,12},{8,2},{10,0},{12,6},{14,4},{1,11},{3,9}... | collective-permute-start | bytes 399368 | tf_op jit(solution)/shard_map/ppermute | solution.py:450
  40.2 0.9 %collective-permute-start.11 = (s16[520,128]{1,0:T(8,128)(2,1)S(1)}, s16[520,128]{1,0:T(8,128)(2,1)S(1)}, u32[]{:S(2)}, u32[]{:S(2)}) collective-permute-start(s16[520,128]{1,0:T(8,128)(2,1)S(1)} %get-tuple-element.52), channel_id=1, source_target_pairs={{0,8},{2,10},{4,12},{6,14},{8,0},{10,2},{12,4},{14,6},{1,9},{3,11}... | collective-permute-start | bytes 399368 | tf_op jit(solution)/shard_map/ppermute | solution.py:450
  41.1 1.5 %collective-permute-start.12 = (s16[520,128]{1,0:T(8,128)(2,1)S(1)}, s16[520,128]{1,0:T(8,128)(2,1)S(1)}, u32[]{:S(2)}, u32[]{:S(2)}) collective-permute-start(s16[520,128]{1,0:T(8,128)(2,1)S(1)} %get-tuple-element.53), channel_id=1, source_target_pairs={{0,2},{2,0},{4,6},{6,4},{8,10},{10,8},{12,14},{14,12},{1,3},{3,1},... | collective-permute-start | bytes 399368 | tf_op jit(solution)/shard_map/ppermute | solution.py:450
  42.6 0.3 collective-permute-done.8.refs_0_
  42.9 1.7 %collective-permute-start.13 = (s16[520,128]{1,0:T(8,128)(2,1)S(1)}, s16[520,128]{1,0:T(8,128)(2,1)S(1)}, u32[]{:S(2)}, u32[]{:S(2)}) collective-permute-start(s16[520,128]{1,0:T(8,128)(2,1)S(1)} %get-tuple-element.55), channel_id=1, source_target_pairs={{0,6},{2,4},{4,2},{6,0},{8,14},{10,12},{12,10},{14,8},{1,7},{3,5},... | collective-permute-start | bytes 399368 | tf_op jit(solution)/shard_map/ppermute | solution.py:450
  44.6 3.6 %collective-permute-done.9.refs_1_ = s16[520,128]{1,0:T(8,128)(2,1)S(1)} collective-permute-done((s16[520,128]{1,0:T(8,128)(2,1)S(1)}, s16[520,128]{1,0:T(8,128)(2,1)S(1)}, u32[]{:S(2)}, u32[]{:S(2)}) %collective-permute-start.9) | collective-permute-done | bytes 133152 | tf_op jit(solution)/shard_map/ppermute | solution.py:450
  48.3 1.2 %collective-permute-start.14 = (s16[520,128]{1,0:T(8,128)(2,1)S(1)}, s16[520,128]{1,0:T(8,128)(2,1)S(1)}, u32[]{:S(2)}, u32[]{:S(2)}) collective-permute-start(s16[520,128]{1,0:T(8,128)(2,1)S(1)} %get-tuple-element.56), channel_id=1, source_target_pairs={{0,14},{2,12},{4,10},{6,8},{8,6},{10,4},{12,2},{14,0},{1,15},{3,13... | collective-permute-start | bytes 399368 | tf_op jit(solution)/shard_map/ppermute | solution.py:450
  49.4 2.8 %collective-permute-done.10.refs_2_ = s16[520,128]{1,0:T(8,128)(2,1)S(1)} collective-permute-done((s16[520,128]{1,0:T(8,128)(2,1)S(1)}, s16[520,128]{1,0:T(8,128)(2,1)S(1)}, u32[]{:S(2)}, u32[]{:S(2)}) %collective-permute-start.10) | collective-permute-done | bytes 133152 | tf_op jit(solution)/shard_map/ppermute | solution.py:450
  52.2 4.8 %collective-permute-done.11.refs_3_ = s16[520,128]{1,0:T(8,128)(2,1)S(1)} collective-permute-done((s16[520,128]{1,0:T(8,128)(2,1)S(1)}, s16[520,128]{1,0:T(8,128)(2,1)S(1)}, u32[]{:S(2)}, u32[]{:S(2)}) %collective-permute-start.11) | collective-permute-done | bytes 133152 | tf_op jit(solution)/shard_map/ppermute | solution.py:450
  57.0 0.0 collective-permute-done.12.refs_4_
  57.0 1.0 %image_early.1.sum_ref = f32[2,256,1024]{2,1,0:T(8,128)S(1)} custom-call(bf16[2,256,192]{2,1,0:T(8,128)(2,1)S(1)} %get-tuple-element.35.table_ref, s16[520,128]{1,0:T(8,128)(2,1)S(1)} %collective-permute-done.8.refs_0_, s16[520,128]{1,0:T(8,128)(2,1)S(1)} %collective-permute-done.9.refs_1_, s16[520,128]{1,0:T(8,128)(2,1)S(1)} %collective-permute-done.10.refs_2_, ...), custom_call_target="tpu_custom_call" | custom-call | tf_op jit(solution)/shard_map/image_early/pallas_call | solution.py:524
  58.1 0.0 collective-permute-done.13.refs_0_
  58.1 0.0 collective-permute-done.14.refs_1_
  58.1 1.2 %image.1 = bf16[512,1024]{1,0:T(8,128)(2,1)} custom-call(bf16[256,192]{1,0:T(8,128)(2,1)S(1)} %get-tuple-element.34.table_ref, f32[2,256,1024]{2,1,0:T(8,128)S(1)} %image_early.1.sum_ref, s16[520,128]{1,0:T(8,128)(2,1)S(1)} %collective-permute-done.13.refs_0_, s16[520,128]{1,0:T(8,128)(2,1)S(1)} %collective-permute-done.14.refs_1_), custom_call_target="tpu_custom_call" | custom-call | tf_op jit(solution)/shard_map/image/pallas_call | solution.py:527
Async XLA Ops:
  0.0 25.3 %copy-start.3 = (s32[4,16]{1,0:T(4,128)S(1)}, s32[4,16]{1,0:T(4,128)}, u32[]{:S(2)}) copy-start(s32[4,16]{1,0:T(4,128)} %band_ref.1) | copy-start | bytes 772
  0.0 1.2 %copy-start.1 = (bf16[2,32,8,1024]{3,2,1,0:T(8,128)(2,1)S(1)}, bf16[2,32,8,1024]{3,2,1,0:T(8,128)(2,1)}, u32[]{:S(2)}) copy-start(bf16[2,32,8,1024]{3,2,1,0:T(8,128)(2,1)} %param.4) | copy-start | bytes 3145732
  1.2 24.0 %copy-start.2 = (f32[2,128,256]{2,1,0:T(8,128)S(1)}, f32[2,128,256]{2,1,0:T(8,128)}, u32[]{:S(2)}) copy-start(f32[2,128,256]{2,1,0:T(8,128)} %constant.10.clone.base_ref) | copy-start | bytes 786436
  1.8 10.8 %collective-permute-start = (s16[520,128]{1,0:T(8,128)(2,1)S(1)}, s16[520,128]{1,0:T(8,128)(2,1)S(1)}, u32[]{:S(2)}, u32[]{:S(2)}) collective-permute-start(s16[520,128]{1,0:T(8,128)(2,1)S(1)} %spread.1), channel_id=1, source_target_pairs={{0,12},{2,14},{4,8},{6,10},{8,4},{10,6},{12,0},{14,2},{1,13},{3,15... | collective-permute-start | bytes 399368 | tf_op jit(solution)/shard_map/ppermute | solution.py:450
  8.1 14.9 %collective-permute-start.2 = (s16[520,128]{1,0:T(8,128)(2,1)S(1)}, s16[520,128]{1,0:T(8,128)(2,1)S(1)}, u32[]{:S(2)}, u32[]{:S(2)}) collective-permute-start(s16[520,128]{1,0:T(8,128)(2,1)S(1)} %get-tuple-element.39), channel_id=1, source_target_pairs={{0,10},{2,8},{4,14},{6,12},{8,2},{10,0},{12,6},{14,4},{1,11},{3,9}... | collective-permute-start | bytes 399368 | tf_op jit(solution)/shard_map/ppermute | solution.py:450
  8.6 17.4 %collective-permute-start.3 = (s16[520,128]{1,0:T(8,128)(2,1)S(1)}, s16[520,128]{1,0:T(8,128)(2,1)S(1)}, u32[]{:S(2)}, u32[]{:S(2)}) collective-permute-start(s16[520,128]{1,0:T(8,128)(2,1)S(1)} %get-tuple-element.40), channel_id=1, source_target_pairs={{0,8},{2,10},{4,12},{6,14},{8,0},{10,2},{12,4},{14,6},{1,9},{3,11}... | collective-permute-start | bytes 399368 | tf_op jit(solution)/shard_map/ppermute | solution.py:450
  12.1 14.0 %collective-permute-start.4 = (s16[520,128]{1,0:T(8,128)(2,1)S(1)}, s16[520,128]{1,0:T(8,128)(2,1)S(1)}, u32[]{:S(2)}, u32[]{:S(2)}) collective-permute-start(s16[520,128]{1,0:T(8,128)(2,1)S(1)} %get-tuple-element.41), channel_id=1, source_target_pairs={{0,2},{2,0},{4,6},{6,4},{8,10},{10,8},{12,14},{14,12},{1,3},{3,1},... | collective-permute-start | bytes 399368 | tf_op jit(solution)/shard_map/ppermute | solution.py:450
  12.6 13.4 %collective-permute-start.1 = (s16[520,128]{1,0:T(8,128)(2,1)S(1)}, s16[520,128]{1,0:T(8,128)(2,1)S(1)}, u32[]{:S(2)}, u32[]{:S(2)}) collective-permute-start(s16[520,128]{1,0:T(8,128)(2,1)S(1)} %get-tuple-element.32), channel_id=1, source_target_pairs={{0,4},{2,6},{4,0},{6,2},{8,12},{10,14},{12,8},{14,10},{1,5},{3,7},... | collective-permute-start | bytes 399368 | tf_op jit(solution)/shard_map/ppermute | solution.py:450
  12.6 16.2 %collective-permute-start.5 = (s16[520,128]{1,0:T(8,128)(2,1)S(1)}, s16[520,128]{1,0:T(8,128)(2,1)S(1)}, u32[]{:S(2)}, u32[]{:S(2)}) collective-permute-start(s16[520,128]{1,0:T(8,128)(2,1)S(1)} %get-tuple-element.43), channel_id=1, source_target_pairs={{0,6},{2,4},{4,2},{6,0},{8,14},{10,12},{12,10},{14,8},{1,7},{3,5},... | collective-permute-start | bytes 399368 | tf_op jit(solution)/shard_map/ppermute | solution.py:450
  23.0 7.7 %collective-permute-start.6 = (s16[520,128]{1,0:T(8,128)(2,1)S(1)}, s16[520,128]{1,0:T(8,128)(2,1)S(1)}, u32[]{:S(2)}, u32[]{:S(2)}) collective-permute-start(s16[520,128]{1,0:T(8,128)(2,1)S(1)} %get-tuple-element.44), channel_id=1, source_target_pairs={{0,14},{2,12},{4,10},{6,8},{8,6},{10,4},{12,2},{14,0},{1,15},{3,13... | collective-permute-start | bytes 399368 | tf_op jit(solution)/shard_map/ppermute | solution.py:450
  27.1 4.2 %copy-start = (bf16[4,8,256,128]{3,2,1,0:T(8,128)(2,1)S(1)}, bf16[4,8,256,128]{3,2,1,0:T(8,128)(2,1)}, u32[]{:S(2)}) copy-start(bf16[4,8,256,128]{3,2,1,0:T(8,128)(2,1)} %weights_ref.3) | copy-start | bytes 6291460
  31.2 1.8 %collective-permute-start.7 = (bf16[2,512,128]{2,1,0:T(8,128)(2,1)S(1)}, bf16[2,512,128]{2,1,0:T(8,128)(2,1)S(1)}, u32[]{:S(2)}, u32[]{:S(2)}) collective-permute-start(bf16[2,512,128]{2,1,0:T(8,128)(2,1)S(1)} %get-tuple-element.46), channel_id=1, source_target_pairs={{0,1},{1,0},{2,3},{3,2},{4,5},{5,4},{6,7},{7,6},{8,9},{9,8},{10,11... | collective-permute-start | bytes 786440 | tf_op jit(solution)/shard_map/ppermute | solution.py:503
  34.7 8.3 %collective-permute-start.8 = (s16[520,128]{1,0:T(8,128)(2,1)S(1)}, s16[520,128]{1,0:T(8,128)(2,1)S(1)}, u32[]{:S(2)}, u32[]{:S(2)}) collective-permute-start(s16[520,128]{1,0:T(8,128)(2,1)S(1)} %get-tuple-element.48), channel_id=1, source_target_pairs={{0,12},{2,14},{4,8},{6,10},{8,4},{10,6},{12,0},{14,2},{1,13},{3,15... | collective-permute-start | bytes 399368 | tf_op jit(solution)/shard_map/ppermute | solution.py:450
  37.0 11.2 %collective-permute-start.9 = (s16[520,128]{1,0:T(8,128)(2,1)S(1)}, s16[520,128]{1,0:T(8,128)(2,1)S(1)}, u32[]{:S(2)}, u32[]{:S(2)}) collective-permute-start(s16[520,128]{1,0:T(8,128)(2,1)S(1)} %get-tuple-element.49), channel_id=1, source_target_pairs={{0,4},{2,6},{4,0},{6,2},{8,12},{10,14},{12,8},{14,10},{1,5},{3,7},... | collective-permute-start | bytes 399368 | tf_op jit(solution)/shard_map/ppermute | solution.py:450
  38.2 14.0 %collective-permute-start.10 = (s16[520,128]{1,0:T(8,128)(2,1)S(1)}, s16[520,128]{1,0:T(8,128)(2,1)S(1)}, u32[]{:S(2)}, u32[]{:S(2)}) collective-permute-start(s16[520,128]{1,0:T(8,128)(2,1)S(1)} %get-tuple-element.51), channel_id=1, source_target_pairs={{0,10},{2,8},{4,14},{6,12},{8,2},{10,0},{12,6},{14,4},{1,11},{3,9}... | collective-permute-start | bytes 399368 | tf_op jit(solution)/shard_map/ppermute | solution.py:450
  40.2 16.8 %collective-permute-start.11 = (s16[520,128]{1,0:T(8,128)(2,1)S(1)}, s16[520,128]{1,0:T(8,128)(2,1)S(1)}, u32[]{:S(2)}, u32[]{:S(2)}) collective-permute-start(s16[520,128]{1,0:T(8,128)(2,1)S(1)} %get-tuple-element.52), channel_id=1, source_target_pairs={{0,8},{2,10},{4,12},{6,14},{8,0},{10,2},{12,4},{14,6},{1,9},{3,11}... | collective-permute-start | bytes 399368 | tf_op jit(solution)/shard_map/ppermute | solution.py:450
  41.1 15.9 %collective-permute-start.12 = (s16[520,128]{1,0:T(8,128)(2,1)S(1)}, s16[520,128]{1,0:T(8,128)(2,1)S(1)}, u32[]{:S(2)}, u32[]{:S(2)}) collective-permute-start(s16[520,128]{1,0:T(8,128)(2,1)S(1)} %get-tuple-element.53), channel_id=1, source_target_pairs={{0,2},{2,0},{4,6},{6,4},{8,10},{10,8},{12,14},{14,12},{1,3},{3,1},... | collective-permute-start | bytes 399368 | tf_op jit(solution)/shard_map/ppermute | solution.py:450
  42.9 15.2 %collective-permute-start.13 = (s16[520,128]{1,0:T(8,128)(2,1)S(1)}, s16[520,128]{1,0:T(8,128)(2,1)S(1)}, u32[]{:S(2)}, u32[]{:S(2)}) collective-permute-start(s16[520,128]{1,0:T(8,128)(2,1)S(1)} %get-tuple-element.55), channel_id=1, source_target_pairs={{0,6},{2,4},{4,2},{6,0},{8,14},{10,12},{12,10},{14,8},{1,7},{3,5},... | collective-permute-start | bytes 399368 | tf_op jit(solution)/shard_map/ppermute | solution.py:450
  48.3 9.8 %collective-permute-start.14 = (s16[520,128]{1,0:T(8,128)(2,1)S(1)}, s16[520,128]{1,0:T(8,128)(2,1)S(1)}, u32[]{:S(2)}, u32[]{:S(2)}) collective-permute-start(s16[520,128]{1,0:T(8,128)(2,1)S(1)} %get-tuple-element.56), channel_id=1, source_target_pairs={{0,14},{2,12},{4,10},{6,8},{8,6},{10,4},{12,2},{14,0},{1,15},{3,13... | collective-permute-start | bytes 399368 | tf_op jit(solution)/shard_map/ppermute | solution.py:450
